TPU v7x, 32 devices: a whole 2x2x4 slice. The times are simulated.
32 devices in a mesh: dp: 16 (over z, y, core), seq: 2 (over x).
Axes of the slice: x: 2, y: 2, z: 4, core: 2. Of those that a mesh axis runs over, the one named last changes fastest.
Arguments:
- token_ids: int32 [16, 1024], P('dp'), may hold values from 0 to 31999
- segment_ids: int32 [16, 1024], P('dp'), may hold values from 0 to 7, never falling along the last dimension, each value on 1 to 512 neighbouring positions
- time_steps: int32 [16], P('dp'), may hold values from 0 to 999
- row_seeds: int32 [16], P('dp'), may hold values from 0 to 65520
- loss_weights: float32 [16, 1024], P('dp', 'seq'), may hold values from -6 to 6
- embed_table: bfloat16 [32000, 256], P(('dp', 'seq')), may hold values from -6 to 6
- input_proj: bfloat16 [256, 1024], P(('dp', 'seq')), may hold values from -0.375 to 0.375
- attn_gain: bfloat16 [1024], P(('dp', 'seq')), may hold values from 0.5 to 1.5
- attn_bias: bfloat16 [1024], P(('dp', 'seq')), may hold values from -1.796875 to 1.796875
- qkv_proj: bfloat16 [1024, 3072], P(('dp', 'seq')), may hold values from -0.1875 to 0.1875
- attn_proj: bfloat16 [1024, 1024], P(('dp', 'seq')), may hold values from -0.75 to 0.75
- mlp_gain: bfloat16 [1024], P(('dp', 'seq')), may hold values from 0.5 to 1.5
- mlp_bias: bfloat16 [1024], P(('dp', 'seq')), may hold values from -1.796875 to 1.796875
- up_proj: bfloat16 [1024, 4096], P(('dp', 'seq')), may hold values from -0.1875 to 0.1875
- up_bias: bfloat16 [4096], P(('dp', 'seq')), may hold values from -1.796875 to 1.796875
- down_proj: bfloat16 [4096, 1024], P(('dp', 'seq')), may hold values from -0.09375 to 0.09375
- output_proj: bfloat16 [1024, 256], P(('dp', 'seq')), may hold values from -0.1875 to 0.1875
Outputs:
- token_loss: float32 [16, 1024], P('dp', 'seq')
- table_grad: float32 [32000, 256], P(('dp', 'seq'))
- input_proj_grad: float32 [256, 1024], P(('dp', 'seq'))
- attn_gain_grad: float32 [1024], P(('dp', 'seq'))
- attn_bias_grad: float32 [1024], P(('dp', 'seq'))
- qkv_proj_grad: float32 [1024, 3072], P(('dp', 'seq'))
- attn_proj_grad: float32 [1024, 1024], P(('dp', 'seq'))
- mlp_gain_grad: float32 [1024], P(('dp', 'seq'))
- mlp_bias_grad: float32 [1024], P(('dp', 'seq'))
- up_proj_grad: float32 [1024, 4096], P(('dp', 'seq'))
- up_bias_grad: float32 [4096], P(('dp', 'seq'))
- down_proj_grad: float32 [4096, 1024], P(('dp', 'seq'))
- output_proj_grad: float32 [1024, 256], P(('dp', 'seq'))
Inputs may be any that keep to these rules, and one draw needn't show every extreme that they name: `token_ids`: token ids over the vocabulary; a few of them are very common. `segment_ids`: within a row the ids never fall, so each document is one run of positions of at most 512; the longest run in a draw has exactly 512 positions.
All inputs are finite; a program needn't handle non-finite values.
Results may differ from a plain program's by a relative error of at most 0.015.
Values may be sent and summed in bfloat16 or wider, within the bound.
No kernel may reach another device: no remote copies, remote signals or barrier semaphores. Data moves between devices by JAX's collectives and lax.ppermute only.
A program may use at most 256 MiB of HBM per device.

v0:
```python
import math

import jax
import jax.numpy as jnp
from jax import lax
from jax.experimental import pallas as pl
from jax.experimental.pallas import tpu as pltpu
from jax.sharding import Mesh
from jax.sharding import PartitionSpec as P

D = 1024
HEAD_DIM = 64
TSTEPS = 1000
SWAP = ((0, 1), (1, 0))
BF = jnp.bfloat16
F32 = jnp.float32
NEG = -1e30
LIMIT = 70.0
MIB = 1 << 20


def dot_nn(left, right):
    return lax.dot_general(left, right, (((1,), (0,)), ((), ())), preferred_element_type=F32)


def dot_nt(left, right):
    return lax.dot_general(left, right, (((1,), (1,)), ((), ())), preferred_element_type=F32)


def dot_tn(left, right):
    return lax.dot_general(left, right, (((0,), (0,)), ((), ())), preferred_element_type=F32)


def swap(value, axis):
    return lax.ppermute(value, axis, SWAP)


def ring_down(value, axis):
    n = lax.axis_size(axis)
    return lax.ppermute(value, axis, [(i, (i - 1) % n) for i in range(n)])


def ring_up(value, axis):
    n = lax.axis_size(axis)
    return lax.ppermute(value, axis, [(i, (i + 1) % n) for i in range(n)])


def ordered(own, other, place, axis):
    return jnp.where(
        place == 0, jnp.stack([own, other], axis), jnp.stack([other, own], axis)
    )


def pick(value, index, axis):
    return lax.dynamic_index_in_dim(value, index, axis, keepdims=False)


def after(value, *others):
    return lax.optimization_barrier((value,) + others)[0]


def ring_blocks(value, axis):
    parts = [value]
    for _ in range(lax.axis_size(axis) - 1):
        parts.append(ring_down(parts[-1], axis))
    return parts


def joined_swap(held, axis):
    return jnp.concatenate([held, swap(held, axis)], 0)


def apart(value, axis, distance):
    n = lax.axis_size(axis)
    return lax.ppermute(value, axis, [(i, i ^ distance) for i in range(n)])


def joined_apart(value, axis):
    held, distance = value[None], 1
    while distance < lax.axis_size(axis):
        held = jnp.concatenate([held, apart(held, axis, distance)], 0)
        distance *= 2
    return held


def halve(value, axis, at):
    here = lax.axis_index(axis)
    return pick(value, here, at), swap(pick(value, 1 - here, at), axis)


def added(kept, moved):
    return (kept.astype(F32) + moved.astype(F32)).astype(BF)


def ring_start(value, axis):
    n, here = lax.axis_size(axis), lax.axis_index(axis)
    return ring_up(pick(value, (here - 1) % n, 0), axis)


def ring_next(value, moved, step, axis):
    n, here = lax.axis_size(axis), lax.axis_index(axis)
    return pick(value, (here - 1 - step) % n, 0).astype(F32) + moved.astype(F32)


def place_blocks(places, halves, outs):
    flat = halves[0] + halves[1]
    count = sum(piece.shape[0] for piece in flat) * len(outs)

    def body(places_ref, *refs):
        ins, results, sems = refs[: len(flat)], refs[len(flat) : -1], refs[-1]
        copies, block = [], 0
        for number, piece in enumerate(ins):
            for k in range(piece.shape[0]):
                p, h = places_ref[block], number // len(halves[0])
                block += 1
                for (low, high, _, index), result in zip(outs, results):
                    copies.append(
                        pltpu.make_async_copy(
                            piece.at[k, :, low:high],
                            result.at[index(p, h)],
                            sems.at[len(copies)],
                        )
                    )
        for copy in copies:
            copy.start()
        for copy in copies:
            copy.wait()

    return pl.pallas_call(
        body,
        out_shape=tuple(jax.ShapeDtypeStruct(shape, BF) for _, _, shape, _ in outs),
        grid=(1,),
        in_specs=[pl.BlockSpec(memory_space=pltpu.SMEM)]
        + [pl.BlockSpec(memory_space=pl.ANY)] * len(flat),
        out_specs=tuple(
            pl.BlockSpec(shape, lambda i, n=len(shape): (0,) * n) for _, _, shape, _ in outs
        ),
        scratch_shapes=[pltpu.SemaphoreType.DMA((count,))],
        compiler_params=pltpu.CompilerParams(vmem_limit_bytes=24 * MIB),
        name="place_blocks",
    )(places, *flat)


def for_each_window(lo, hi, blocks, run):
    for count in range(1, blocks + 1):

        @pl.when(hi - lo == count)
        def _():
            run(lo, count)


def attend_body(
    lo_ref, hi_ref, q_ref, k_ref, v_ref, seg_col_ref, seg_row_ref, o_ref, lse_ref, v_ones
):
    length = q_ref.shape[0]
    blk = min(256, length)
    lane = lax.broadcasted_iota(jnp.int32, (1, 128), 1)
    masks = (lane < HEAD_DIM, lane >= HEAD_DIM)
    v = v_ref[...]
    for h in range(2):
        v_ones[h] = jnp.where(masks[h], v, jnp.ones_like(v))

    def largest(ref):
        rows = ref[...].astype(F32)
        return jnp.max(jnp.sum(rows * rows, axis=1, keepdims=True))

    small = largest(q_ref) * largest(k_ref) <= LIMIT * LIMIT

    def finish(rows, accs):
        totals = [pltpu.roll(acc, HEAD_DIM, axis=1) for acc in accs]
        o_ref[rows, :] = (
            jnp.where(masks[0], accs[0], accs[1]) / jnp.where(masks[0], totals[0], totals[1])
        ).astype(BF)
        return [accs[0].T[HEAD_DIM : HEAD_DIM + 1], accs[1].T[0:1]]

    def each(qi, _):
        rows = pl.ds(pl.multiple_of(qi * blk, blk), blk)
        q = q_ref[rows, :]
        q_heads = [jnp.where(m, q, jnp.zeros_like(q)) for m in masks]

        def run(first, count):
            at = pl.ds(pl.multiple_of(first * blk, blk), count * blk)
            k = k_ref[at, :]
            same = seg_col_ref[at, :] == seg_row_ref[:, rows]
            accs = []
            for h in range(2):
                e = jnp.exp(jnp.where(same, dot_nt(k, q_heads[h]), NEG)).astype(BF)
                accs.append(dot_tn(e, v_ones[h, at, :]))
            for h, total in enumerate(finish(rows, accs)):
                lse_ref[0, h : h + 1, rows] = jnp.log(total)

        @pl.when(small)
        def _():
            for_each_window(lo_ref[qi], hi_ref[qi], length // blk, run)

        @pl.when(jnp.logical_not(small))
        def _():
            def scores(kb, h):
                at = pl.ds(pl.multiple_of(kb * blk, blk), blk)
                same = seg_col_ref[at, :] == seg_row_ref[:, rows]
                return jnp.where(same, dot_nt(k_ref[at, :], q_heads[h]), NEG)

            def highest(kb, tops):
                return tuple(
                    jnp.maximum(tops[h], jnp.max(scores(kb, h), axis=0, keepdims=True))
                    for h in range(2)
                )

            tops = lax.fori_loop(
                lo_ref[qi], hi_ref[qi], highest, (jnp.full((1, blk), NEG, F32),) * 2
            )

            def gather(kb, accs):
                at = pl.ds(pl.multiple_of(kb * blk, blk), blk)
                return tuple(
                    accs[h]
                    + dot_tn(jnp.exp(scores(kb, h) - tops[h]).astype(BF), v_ones[h, at, :])
                    for h in range(2)
                )

            accs = lax.fori_loop(
                lo_ref[qi], hi_ref[qi], gather, (jnp.zeros((blk, 128), F32),) * 2
            )
            for h, total in enumerate(finish(rows, accs)):
                lse_ref[0, h : h + 1, rows] = tops[h] + jnp.log(total)

        return 0

    lax.fori_loop(0, length // blk, each, 0)


def attend(q, k, v, seg_col, seg_row, lo, hi):
    length, width = q.shape
    pairs = width // 128
    spec = pl.BlockSpec((length, 128), lambda i, *_: (0, i))
    return pl.pallas_call(
        attend_body,
        out_shape=(
            jax.ShapeDtypeStruct((length, width), BF),
            jax.ShapeDtypeStruct((pairs, 2, length), F32),
        ),
        grid_spec=pltpu.PrefetchScalarGridSpec(
            num_scalar_prefetch=2,
            grid=(pairs,),
            in_specs=[
                spec,
                spec,
                spec,
                pl.BlockSpec((length, 1), lambda i, *_: (0, 0)),
                pl.BlockSpec((1, length), lambda i, *_: (0, 0)),
            ],
            out_specs=(spec, pl.BlockSpec((1, 2, length), lambda i, *_: (i, 0, 0))),
            scratch_shapes=[pltpu.VMEM((2, length, 128), BF)],
        ),
        compiler_params=pltpu.CompilerParams(vmem_limit_bytes=32 * MIB),
        cost_estimate=pl.CostEstimate(
            flops=16 * length * length * width,
            bytes_accessed=8 * length * width,
            transcendentals=length * length * width // HEAD_DIM,
        ),
        name="attend",
    )(lo, hi, q, k, v, seg_col, seg_row)


def attend_back_body(
    lo_ref,
    hi_ref,
    q_ref,
    k_ref,
    v_ref,
    o_ref,
    g_ref,
    lse_ref,
    seg_col_ref,
    seg_row_ref,
    dq_ref,
    dk_ref,
    dv_ref,
    dk_sum,
    dv_sum,
):
    length = q_ref.shape[0]
    blk = min(256, length)
    lane = lax.broadcasted_iota(jnp.int32, (1, 128), 1)
    masks = (lane < HEAD_DIM, lane >= HEAD_DIM)
    dk_sum[...] = jnp.zeros_like(dk_sum)
    dv_sum[...] = jnp.zeros_like(dv_sum)
    def each(qi, _):
        rows = pl.ds(pl.multiple_of(qi * blk, blk), blk)

        def run(first, count):
            q, g = q_ref[rows, :], g_ref[rows, :]
            mixed = (g.astype(F32) * o_ref[rows, :].astype(F32)).T
            at = pl.ds(pl.multiple_of(first * blk, blk), count * blk)
            k, v = k_ref[at, :], v_ref[at, :]
            same = seg_col_ref[at, :] == seg_row_ref[:, rows]
            dq = jnp.zeros((blk, 128), F32)
            dk, dv = dk_sum[at, :], dv_sum[at, :]
            for h in range(2):
                q_head = jnp.where(masks[h], q, jnp.zeros_like(q))
                g_head = jnp.where(masks[h], g, jnp.zeros_like(g))
                k_head = jnp.where(masks[h], k, jnp.zeros_like(k))
                delta = jnp.sum(mixed[h * HEAD_DIM : (h + 1) * HEAD_DIM], axis=0, keepdims=True)
                s = dot_nt(k, q_head)
                p = jnp.exp(jnp.where(same, s - lse_ref[0, h : h + 1, rows], NEG))
                dp = dot_nt(v, g_head)
                ds = (p * (dp - delta)).astype(BF)
                dv = dv + dot_nn(p.astype(BF), g_head)
                dk = dk + dot_nn(ds, q_head)
                dq = dq + dot_tn(ds, k_head)
            dk_sum[at, :] = dk
            dv_sum[at, :] = dv
            dq_ref[rows, :] = dq.astype(BF)

        for_each_window(lo_ref[qi], hi_ref[qi], length // blk, run)
        return 0

    lax.fori_loop(0, length // blk, each, 0)
    dk_ref[...] = dk_sum[...].astype(BF)
    dv_ref[...] = dv_sum[...].astype(BF)


def attend_back(q, k, v, o, g, lse, seg_col, seg_row, lo, hi):
    length, width = q.shape
    pairs = width // 128
    spec = pl.BlockSpec((length, 128), lambda i, *_: (0, i))
    shape = jax.ShapeDtypeStruct((length, width), BF)
    return pl.pallas_call(
        attend_back_body,
        out_shape=(shape, shape, shape),
        grid_spec=pltpu.PrefetchScalarGridSpec(
            num_scalar_prefetch=2,
            grid=(pairs,),
            in_specs=[
                spec,
                spec,
                spec,
                spec,
                spec,
                pl.BlockSpec((1, 2, length), lambda i, *_: (i, 0, 0)),
                pl.BlockSpec((length, 1), lambda i, *_: (0, 0)),
                pl.BlockSpec((1, length), lambda i, *_: (0, 0)),
            ],
            out_specs=(spec, spec, spec),
            scratch_shapes=[pltpu.VMEM((length, 128), F32), pltpu.VMEM((length, 128), F32)],
        ),
        compiler_params=pltpu.CompilerParams(vmem_limit_bytes=32 * MIB),
        cost_estimate=pl.CostEstimate(
            flops=32 * length * length * width,
            bytes_accessed=16 * length * width,
            transcendentals=length * length * width // HEAD_DIM,
        ),
        name="attend_back",
    )(lo, hi, q, k, v, o, g, lse, seg_col, seg_row)


def score_body(
    norm_ref, out_ref, table_ref, slot_ref, raised_ref, tops_ref, acc_ref, total_ref, top, fast
):
    j = pl.program_id(0)
    tokens, width = out_ref.shape
    count = table_ref.shape[1]
    rows = table_ref[0].astype(F32)
    unit = rows * lax.rsqrt(jnp.mean(rows * rows, axis=1, keepdims=True) + 1e-06)
    low = unit * width ** (-0.5)
    scaled, scaled_t = low.astype(BF), low.T.astype(BF)
    row = lax.broadcasted_iota(jnp.int32, (count, 1), 0) + j * count

    @pl.when(j == 0)
    def _():
        acc_ref[...] = jnp.zeros_like(acc_ref)
        total_ref[...] = jnp.zeros_like(total_ref)
        some = scaled[: min(count, 128)]
        first = jnp.max(dot_nt(some, out_ref[...]), axis=0, keepdims=True)
        floor = norm_ref[...] - LIMIT
        kept = jnp.max(floor - first) <= LIMIT
        top[...] = jnp.where(kept, jnp.maximum(first, floor), NEG)
        fast[0] = kept.astype(jnp.int32)

    @pl.when(fast[0] == 1)
    def _():
        e = jnp.exp(dot_nt(scaled, out_ref[...]) - top[...])
        total_ref[...] += jnp.sum(e, axis=0, keepdims=True)
        raised_ref[0] = jnp.where(row == slot_ref[...], 0.0, e).astype(BF)
        acc_ref[...] += dot_nn(scaled_t, raised_ref[0])
        tops_ref[0] = top[...]

    @pl.when(fast[0] == 0)
    def _():
        part = math.gcd(tokens, 512)

        def each(n, _):
            at = pl.ds(pl.multiple_of(n * part, part), part)
            logits = dot_nt(scaled, out_ref[at, :])
            new_top = jnp.maximum(top[:, at], jnp.max(logits, axis=0, keepdims=True))
            keep = jnp.exp(top[:, at] - new_top)
            e = jnp.exp(logits - new_top)
            total_ref[:, at] = total_ref[:, at] * keep + jnp.sum(e, axis=0, keepdims=True)
            raised_ref[0, :, at] = jnp.where(row == slot_ref[:, at], 0.0, e).astype(BF)
            acc_ref[:, at] = acc_ref[:, at] * keep + dot_nn(scaled_t, raised_ref[0, :, at])
            tops_ref[0, :, at] = new_top
            top[:, at] = new_top
            return 0

        lax.fori_loop(0, tokens // part, each, 0)


def score(outputs, table, slots):
    tokens, width = outputs.shape
    blocks, rows, _ = table.shape
    squares = jnp.square(outputs.astype(F32))
    norms = 1.01 * jnp.sqrt(dot_nt(jnp.ones((8, width), BF), squares.astype(BF))[:1])
    return pl.pallas_call(
        score_body,
        out_shape=(
            jax.ShapeDtypeStruct((blocks, rows, tokens), BF),
            jax.ShapeDtypeStruct((blocks, 1, tokens), F32),
            jax.ShapeDtypeStruct((width, tokens), F32),
            jax.ShapeDtypeStruct((1, tokens), F32),
        ),
        grid=(blocks,),
        in_specs=[
            pl.BlockSpec((1, tokens), lambda j: (0, 0)),
            pl.BlockSpec((tokens, width), lambda j: (0, 0)),
            pl.BlockSpec((1, rows, width), lambda j: (j, 0, 0)),
            pl.BlockSpec((1, tokens), lambda j: (0, 0)),
        ],
        out_specs=(
            pl.BlockSpec((1, rows, tokens), lambda j: (j, 0, 0)),
            pl.BlockSpec((1, 1, tokens), lambda j: (j, 0, 0)),
            pl.BlockSpec((width, tokens), lambda j: (0, 0)),
            pl.BlockSpec((1, tokens), lambda j: (0, 0)),
        ),
        scratch_shapes=[pltpu.VMEM((1, tokens), F32), pltpu.SMEM((1,), jnp.int32)],
        compiler_params=pltpu.CompilerParams(vmem_limit_bytes=48 * MIB),
        cost_estimate=pl.CostEstimate(
            flops=4 * blocks * rows * tokens * width,
            bytes_accessed=2 * blocks * rows * tokens,
            transcendentals=blocks * rows * tokens,
        ),
        name="score",
    )(norms, outputs, table, slots)


def table_product_body(raised_ref, out_ref, coef_ref, sum_ref):
    j = pl.program_id(0)
    lane = lax.broadcasted_iota(jnp.int32, coef_ref.shape, 1)
    coef = jnp.sum(jnp.where(lane == j, coef_ref[...], 0.0), axis=1, keepdims=True)
    weighted = (out_ref[...].astype(F32) * coef).astype(BF)
    sum_ref[0] = dot_nn(raised_ref[0], weighted)


def table_product(raised, outputs, coef):
    blocks, rows, tokens = raised.shape
    width = outputs.shape[1]
    return pl.pallas_call(
        table_product_body,
        out_shape=jax.ShapeDtypeStruct((blocks, rows, width), F32),
        grid=(blocks,),
        in_specs=[
            pl.BlockSpec((1, rows, tokens), lambda j: (j, 0, 0)),
            pl.BlockSpec((tokens, width), lambda j: (0, 0)),
            pl.BlockSpec((tokens, blocks), lambda j: (0, 0)),
        ],
        out_specs=pl.BlockSpec((1, rows, width), lambda j: (j, 0, 0)),
        compiler_params=pltpu.CompilerParams(vmem_limit_bytes=48 * MIB),
        cost_estimate=pl.CostEstimate(
            flops=2 * blocks * rows * tokens * width,
            bytes_accessed=2 * blocks * rows * tokens,
            transcendentals=0,
        ),
        name="table_product",
    )(raised, outputs, coef)


def table_add_body(sum_ref, slot_ref, grad_ref, out_ref):
    j = pl.program_id(0)
    rows = sum_ref.shape[1]
    row = lax.broadcasted_iota(jnp.int32, (rows, 1), 0) + j * rows
    chosen = (row == slot_ref[...]).astype(F32).astype(BF)
    out_ref[0] = (sum_ref[0] + dot_nn(chosen, grad_ref[...])).astype(BF)


def table_add(sums, slots, grads):
    blocks, rows, width = sums.shape
    tokens = grads.shape[0]
    return pl.pallas_call(
        table_add_body,
        out_shape=jax.ShapeDtypeStruct(sums.shape, BF),
        grid=(blocks,),
        in_specs=[
            pl.BlockSpec((1, rows, width), lambda j: (j, 0, 0)),
            pl.BlockSpec((1, tokens), lambda j: (0, 0)),
            pl.BlockSpec((tokens, width), lambda j: (0, 0)),
        ],
        out_specs=pl.BlockSpec((1, rows, width), lambda j: (j, 0, 0)),
        compiler_params=pltpu.CompilerParams(vmem_limit_bytes=48 * MIB),
        cost_estimate=pl.CostEstimate(
            flops=2 * blocks * rows * tokens * width,
            bytes_accessed=6 * blocks * rows * width,
            transcendentals=0,
        ),
        name="table_add",
    )(sums, slots, grads)


def norm_parts(hidden):
    centre = hidden - jnp.mean(hidden, axis=-1, keepdims=True)
    spread = jnp.mean(centre * centre, axis=-1, keepdims=True)
    inverse = lax.rsqrt(spread + 1e-05)
    return centre * inverse, inverse


def norm_back(grad, gain, normed, inverse):
    grad_normed = grad * gain
    first = jnp.mean(grad_normed, axis=-1, keepdims=True)
    second = jnp.mean(grad_normed * normed, axis=-1, keepdims=True)
    return inverse * (grad_normed - first - normed * second)


def noise_field(row_seed, length, channel_count):
    position = lax.iota(jnp.int32, length)[:, None]
    channel = lax.iota(jnp.int32, channel_count)[None, :]
    mixed_once = (row_seed + 7919 * position + 104729 * channel) % 65521
    mixed_twice = (mixed_once * (mixed_once % 32719) + 31 * channel) % 65521
    return (mixed_twice.astype(F32) / 32760.5 - 1.0) * 1.7320508


def paired(
    token_ids,
    segment_ids,
    time_steps,
    row_seeds,
    loss_weights,
    embed_table,
    input_proj,
    attn_gain,
    attn_bias,
    qkv_proj,
    attn_proj,
    mlp_gain,
    mlp_bias,
    up_proj,
    up_bias,
    down_proj,
    output_proj,
):
    z, y, c, x = (lax.axis_index(a) for a in ("z", "y", "c", "x"))
    groups = lax.axis_size("z") * lax.axis_size("y")
    length = token_ids.shape[1]
    half = length // 2
    block_len, width = embed_table.shape
    ff = up_proj.shape[1]
    rows_here = qkv_proj.shape[0]
    heads = D // HEAD_DIM
    ff_block = down_proj.shape[0] * 2

    meta = jnp.concatenate([token_ids[0], segment_ids[0], time_steps, row_seeds])
    meta_two = ordered(meta, swap(meta, "c"), c, 0)
    weight_c = ordered(loss_weights[0], swap(loss_weights[0], "c"), c, 0)
    weight_two = ordered(weight_c, swap(weight_c, "x"), x, 1).reshape(2, length)
    ids_two = meta_two[:, :length]
    own_meta = pick(meta_two, x, 0)
    segments = own_meta[length : 2 * length]
    weight_row = pick(weight_two, x, 0)
    fraction = own_meta[2 * length].astype(F32) / (TSTEPS - 1)
    noise_level = 0.3 * jnp.exp(fraction * math.log(30.0))
    input_scale = lax.rsqrt(1.0 + noise_level * noise_level)
    residual_scale = 0.5 + fraction
    noise = noise_field(own_meta[2 * length + 1], length, width)

    small_width = 2 * width + 128
    vector = jnp.concatenate([attn_gain, attn_bias, mlp_gain, mlp_bias, up_bias])
    small = jnp.concatenate(
        [
            input_proj.reshape(rows_here, width),
            output_proj,
            jnp.pad(vector.reshape(-1, 128), ((0, rows_here - vector.size // 128), (0, 0))),
        ],
        axis=1,
    )
    qkv_split = qkv_proj.reshape(rows_here, 3 * heads // 2, 2, HEAD_DIM)
    up_split = up_proj.reshape(rows_here, groups, 2, ff_block)

    def packed(core):
        return jnp.concatenate(
            [
                pick(qkv_split, core, 2).reshape(rows_here, -1),
                small,
                pick(up_split, core, 2).reshape(rows_here, -1),
            ],
            axis=1,
        )

    pair = ordered(packed(c), swap(packed(1 - c), "c"), c, 0).reshape(2 * rows_here, -1)
    qkv_cols, small_cols = 3 * D // 2, 3 * D // 2 + small_width
    first_cols = small_cols + D // 2
    first_shard = jnp.concatenate(
        [
            pair[:, :small_cols],
            jnp.concatenate([attn_proj[:, : D // 2], attn_proj[:, D // 2 :]], axis=0),
        ],
        axis=1,
    )
    up_shard = pair[:, small_cols:]

    def places(order, ring):
        block, found = jnp.arange(2 * groups, dtype=jnp.int32), {}
        for axis in order:
            n, here = lax.axis_size(axis), lax.axis_index(axis)
            found[axis] = (block + here) % n if ring else (block % n) ^ here
            block = block // n
        return (found["z"] * 2 + found["y"]) * 2 + found["x"]

    def both_places(ring):
        return jnp.concatenate([places(("z", "y", "x"), ring), places(("z", "x", "y"), ring)])

    def over_one(blocks):
        rows = blocks.shape[1] // 2
        return joined_swap(blocks[:, :rows], "y"), joined_swap(blocks[:, rows:], "x")

    def over_one_start(blocks):
        rows = blocks.shape[1] // 2
        first, second = blocks[:, :rows], blocks[:, rows:]
        return (first, swap(first, "y")), (second, swap(second, "x"))

    def over_other(held):
        return [[held[0], swap(held[0], "x")], [held[1], swap(held[1], "y")]]

    cut = block_len // 32 * 16
    with jax.named_scope("gather_table"):
        table_a = ring_blocks(embed_table[None, :cut], "z")
        table_b = ring_blocks(joined_swap(embed_table[None, cut:], "y"), "z")
        table_z = table_b[-1]
        table_a = joined_swap(jnp.concatenate(table_a, 0), "y")
        table_b = jnp.stack(table_b, 1).reshape(groups, block_len - cut, width)
    with jax.named_scope("gather_first"):
        first_z = ring_blocks(first_shard[None], "z")
        first_held = over_one(jnp.concatenate(first_z, 0))
        first_pieces = over_other(first_held)
    with jax.named_scope("gather_up"):
        up_first = after(up_shard[None], table_z, first_z[-1])
        up_moved = apart(up_first, "z", 1)
        up_two = jnp.concatenate([up_first, up_moved], 0)
        up_z = jnp.concatenate([up_two, apart(up_two, "z", 2)], 0)
        up_held = over_one(after(up_z, first_pieces[0][1], first_pieces[1][1]))
        up_pieces = over_other(up_held)
    with jax.named_scope("gather_down"):
        down_z = joined_apart(after(down_proj, up_two), "z")

    flat_ids = ids_two.reshape(-1)
    owner = flat_ids // block_len
    within = flat_ids % block_len
    home = {"z": owner // 8, "y": owner // 4 % 2}
    mine = owner % 4 == c * 2 + x
    table_rows = jnp.concatenate([after(table_a, *first_held), table_b], axis=1)
    zn = lax.axis_size("z")
    relative_y, relative_z = (home["y"] - y) % 2, (home["z"] - z) % zn
    slot = (relative_y * zn + relative_z) * block_len + within
    found = jnp.take(
        table_rows.reshape(groups * block_len, width), jnp.where(mine, slot, 0), axis=0
    )
    found = after(found, up_moved)
    found = jnp.where(mine[:, None], found, jnp.zeros_like(found)).reshape(2, length, width)

    def to_rows(terms, kind):
        split = terms.reshape(2, 2, half, width)
        moved = swap(pick(split, 1 - c, 1).astype(kind), "c")
        both = pick(split, c, 1).astype(F32) + moved.astype(F32)
        moved = swap(pick(both, 1 - x, 0).astype(kind), "x")
        own = (pick(both, x, 0).astype(F32) + moved.astype(F32)).astype(kind)
        return ordered(own, swap(own, "c"), c, 0).reshape(length, width)

    def to_pair(row):
        own = pick(row.reshape(2, half, width), c, 0)
        moved = swap(own, "x")
        other = ordered(moved, swap(moved, "c"), c, 0).reshape(length, width)
        return ordered(row, other, x, 0)

    raw = to_rows(found, BF).astype(F32)
    paired_shape = (groups, 2, 2, rows_here)

    def in_pairs(p, h):
        return (p // 2, h, p % 2)

    def held_back(pieces, *values):
        return [[after(piece, *values) for piece in half_pieces] for half_pieces in pieces]

    qkv_half, small_full, attn_half = place_blocks(
        both_places(True),
        held_back(first_pieces, found),
        [
            (0, qkv_cols, paired_shape + (qkv_cols,), in_pairs),
            (qkv_cols, small_cols, paired_shape + (small_width,), in_pairs),
            (
                small_cols,
                first_cols,
                (2 * groups, rows_here, D),
                lambda p, h: (p, slice(None), slice(h * D // 2, (h + 1) * D // 2)),
            ),
        ],
    )
    qkv_half, small_full = qkv_half.reshape(D, qkv_cols), small_full.reshape(D, small_width)
    attn_half = attn_half.reshape(D // 2, D)
    input_full = small_full[:, :width].reshape(width, D)
    output_full = small_full[:, width : 2 * width]
    vectors = small_full[:, 2 * width :].reshape(groups, 2, 2, rows_here, 128)
    vectors = vectors[..., : vector.size // 128, :].reshape(groups, 2, 2, vector.size)
    gain_one, bias_one, gain_two, bias_two = (
        vectors[..., k * rows_here : (k + 1) * rows_here].reshape(1, D).astype(F32)
        for k in range(4)
    )
    up_bias_half = pick(vectors[..., 4 * rows_here :], c, 1).reshape(1, ff // 2).astype(F32)
    unit = raw * lax.rsqrt(jnp.mean(raw * raw, axis=1, keepdims=True) + 1e-06)
    target = (unit * width ** (-0.5)).astype(BF)
    inputs = (input_scale * (unit + noise_level * noise)).astype(BF)

    hidden_zero = dot_nn(inputs, input_full)
    normed_one, inverse_one = norm_parts(hidden_zero)
    first_in = (normed_one * gain_one + bias_one).astype(BF)
    qkv = dot_nn(first_in, qkv_half)
    split = D // 2
    queries = (qkv[:, :split] * HEAD_DIM ** (-0.5)).astype(BF)
    keys = qkv[:, split : 2 * split].astype(BF)
    values = qkv[:, 2 * split :].astype(BF)
    seg_col, seg_row = segments[:, None], segments[None, :]
    blk = min(256, length)
    edges = segments.reshape(length // blk, blk)
    before = jnp.sum(seg_row < edges[:, :1], axis=1, dtype=jnp.int32)
    through = jnp.sum(seg_row <= edges[:, -1:], axis=1, dtype=jnp.int32)
    low_block, high_block = before // blk, (through + blk - 1) // blk
    with jax.named_scope("gather_down"):
        down_z = after(down_z, inputs)
        down_moved = over_one_start(down_z)
    attended, log_total = attend(
        after(queries, down_z), keys, values, seg_col, seg_row, low_block, high_block
    )
    attended = after(
        attended, up_pieces[0][1], up_pieces[1][1], down_moved[0][1], down_moved[1][1]
    )
    with jax.named_scope("gather_down"):
        down_held = [jnp.concatenate([own, after(got, attended)], 0) for own, got in down_moved]
        down_pieces = over_other(down_held)

    def both_cores(part):
        return part + swap(part.astype(BF), "c").astype(F32)

    hidden_one = hidden_zero + residual_scale * both_cores(dot_nn(attended, attn_half))
    normed_two, inverse_two = norm_parts(hidden_one)
    second_in = (normed_two * gain_two + bias_two).astype(BF)
    (up_half,) = place_blocks(
        both_places(False),
        held_back(up_pieces, queries),
        [(0, ff // 2, paired_shape + (ff // 2,), in_pairs)],
    )
    up_half = up_half.reshape(D, ff // 2)
    pre_act = dot_nn(second_in, up_half) + up_bias_half
    below = 0.5 * (1.0 + lax.erf(pre_act * math.sqrt(0.5)))
    activated = (pre_act * below).astype(BF)
    slope = (
        below + pre_act * (jnp.exp(-0.5 * pre_act * pre_act) * (1.0 / math.sqrt(2.0 * math.pi)))
    ).astype(BF)
    (down_half,) = place_blocks(
        both_places(False),
        held_back(down_pieces, activated),
        [
            (
                0,
                D,
                (2 * groups, 2, down_proj.shape[0] // 2, D),
                lambda p, h: (p, h),
            )
        ],
    )
    down_half = down_half.reshape(ff // 2, D)
    hidden_two = hidden_one + residual_scale * both_cores(dot_nn(activated, down_half))
    final_in = hidden_two.astype(BF)
    outputs = dot_nn(final_in, output_full).astype(BF)

    outputs_two = to_pair(outputs).reshape(2 * length, width)
    slots_here = jnp.where(mine, slot, -1)[None, :]
    raised, tops, reached, total = score(outputs_two, table_rows, slots_here)
    ends = jnp.concatenate([tops[-1], total])

    def joined(first, second):
        top = jnp.maximum(first[0], second[0])
        return jnp.stack(
            [top, first[1] * jnp.exp(first[0] - top) + second[1] * jnp.exp(second[0] - top)]
        )

    all_ends = joined(ends, swap(ends, "c"))
    all_ends = joined(all_ends, swap(all_ends, "x"))
    log_sum = all_ends[0] + jnp.log(all_ends[1])
    share = (reached * jnp.exp(ends[0] - log_sum)[None, :]).astype(BF)
    parts = [share[:, k * half : (k + 1) * half] for k in range(4)]
    kept = jnp.concatenate([jnp.where(c == 0, parts[0], parts[1]), jnp.where(c == 0, parts[2], parts[3])], 1)
    sent = jnp.concatenate([jnp.where(c == 0, parts[1], parts[0]), jnp.where(c == 0, parts[3], parts[2])], 1)
    both = kept.astype(F32) + swap(sent, "c").astype(F32)
    own, other = jnp.where(x == 0, both[:, :half], both[:, half:]), jnp.where(x == 0, both[:, half:], both[:, :half])
    own = (own + swap(other.astype(BF), "x").astype(F32)).astype(BF)
    moved = swap(own, "c")
    expected = jnp.concatenate(
        [jnp.where(c == 0, own, moved), jnp.where(c == 0, moved, own)], 1
    ).astype(F32).T
    log_row = pick(log_sum.reshape(2, length), x, 0)
    chosen = jnp.sum(outputs.astype(F32) * target.astype(F32), axis=1)
    loss_row = log_row - chosen
    loss_two = ordered(loss_row, swap(loss_row, "x"), x, 0)
    token_loss = pick(pick(loss_two, c, 0).reshape(2, half), x, 0)[None]

    own_term = weight_row * (jnp.exp(chosen - log_row) - 1.0)
    out_grad = (
        weight_row[:, None] * expected + own_term[:, None] * target.astype(F32)
    ).astype(BF)
    coef = (
        (weight_two.reshape(-1) * width ** (-0.5))[None, :] * jnp.exp(tops[:, 0] - log_sum[None, :])
    ).T
    table_sums = table_product(raised, outputs_two, coef)

    zy = (zn, lax.axis_size("y"))
    table_cut = block_len * 5 // 128 * 16

    def rows_of(grad):
        rows = grad.shape[0] // (2 * groups)
        return grad.astype(BF).reshape(zy + (2, rows, grad.shape[1]))

    def pairs_of(grad):
        rows = grad.shape[0] // (4 * groups)
        shaped = grad.astype(BF).reshape(zy + (2, 2, rows, grad.shape[1]))
        return shaped[:, :, 0], shaped[:, :, 1]

    output_w_grad = dot_tn(final_in, out_grad)
    hidden_two_grad = dot_nt(out_grad, output_full)
    branch_grad = (residual_scale * hidden_two_grad).astype(BF)
    with jax.named_scope("reduce_down"):
        down_terms = rows_of(dot_tn(activated, branch_grad))
        rows = down_terms.shape[3] // 2
        down_a = halve(down_terms[..., :rows, :], "x", 2)
        down_b = halve(down_terms[..., rows:, :], "y", 1)
    pre_grad = (
        dot_nt(after(branch_grad, down_terms), down_half) * slope.astype(F32)
    ).astype(BF)
    with jax.named_scope("reduce_up"):
        up_terms = dot_tn(second_in, pre_grad).astype(BF)
        up_a, up_b = pairs_of(up_terms)
        up_a, up_b = halve(up_a, "y", 1), halve(up_b, "x", 2)
    up_bias_part = jnp.sum(pre_grad, axis=0, dtype=F32)
    second_grad = both_cores(
        dot_nt(after(pre_grad, up_terms, down_a[1], down_b[1]), up_half)
    )
    gain_two_part = jnp.sum(second_grad * normed_two, axis=0)
    bias_two_part = jnp.sum(second_grad, axis=0)
    hidden_one_grad = hidden_two_grad + norm_back(second_grad, gain_two, normed_two, inverse_two)
    attn_grad = after((residual_scale * hidden_one_grad).astype(BF), up_a[1], up_b[1])
    with jax.named_scope("reduce_attn"):
        attn_terms = halve(rows_of(dot_tn(attended, attn_grad)), "y", 1)
    attended_grad = dot_nt(attn_grad, attn_half).astype(BF)
    with jax.named_scope("reduce_down"):
        down_a = added(down_a[0], after(down_a[1], up_terms))
        down_b = added(down_b[0], after(down_b[1], up_terms))
        down_next_a, down_next_b = halve(down_a, "y", 1), halve(down_b, "x", 1)
    with jax.named_scope("reduce_up"):
        up_a = added(up_a[0], after(up_a[1], attn_grad))
        up_b = added(up_b[0], after(up_b[1], attn_grad))
        up_next_a, up_next_b = halve(up_a, "x", 1), halve(up_b, "y", 1)
    query_grad, key_grad, value_grad = attend_back(
        queries,
        keys,
        values,
        attended,
        after(attended_grad, down_a, down_b, up_a, up_b, attn_terms[0]),
        log_total,
        seg_col,
        seg_row,
        low_block,
        high_block,
    )
    query_grad = after(
        query_grad,
        up_next_a[1],
        up_next_b[1],
        down_next_a[1],
        down_next_b[1],
        attn_terms[1],
    )
    with jax.named_scope("reduce_mlp"):
        mlp_sum = jnp.concatenate(
            [
                jnp.concatenate(
                    [
                        added(up_next_a[0], after(up_next_a[1], query_grad)),
                        added(up_next_b[0], after(up_next_b[1], query_grad)),
                    ],
                    1,
                ),
                added(down_next_a[0], after(down_next_a[1], query_grad)),
                added(down_next_b[0], after(down_next_b[1], query_grad)),
            ],
            2,
        )
        mlp_ring = ring_start(mlp_sum, "z")
    with jax.named_scope("reduce_attn"):
        attn_terms = halve(added(attn_terms[0], after(attn_terms[1], query_grad)), "x", 1)
    qkv_grad = jnp.concatenate(
        [query_grad * jnp.asarray(HEAD_DIM ** (-0.5), BF), key_grad, value_grad], axis=1
    )
    with jax.named_scope("reduce_qkv"):
        qkv_terms = dot_tn(first_in, after(qkv_grad, mlp_sum)).astype(BF)
        qkv_a, qkv_b = pairs_of(qkv_terms)
        qkv_a, qkv_b = halve(qkv_a, "y", 1), halve(qkv_b, "x", 2)
    first_grad = both_cores(dot_nt(after(qkv_grad, qkv_terms), qkv_half))
    gain_one_part = jnp.sum(first_grad * normed_one, axis=0)
    bias_one_part = jnp.sum(first_grad, axis=0)
    hidden_zero_grad = (
        hidden_one_grad + norm_back(first_grad, gain_one, normed_one, inverse_one)
    ).astype(BF)
    embed_grad = input_scale * dot_nt(hidden_zero_grad, input_full)
    token_grad = (
        embed_grad + (own_term * width ** (-0.5))[:, None] * outputs.astype(F32)
    ).astype(BF)
    token_own = pick(token_grad.reshape(2, half, width), c, 0)
    with jax.named_scope("token_pair"):
        token_moved = swap(token_own, "x")
    with jax.named_scope("reduce_mlp"):
        mlp_ring = ring_up(ring_next(mlp_sum, after(mlp_ring, token_own), 1, "z").astype(BF), "z")
    with jax.named_scope("token_pair"):
        token_other = ordered(token_moved, swap(token_moved, "c"), c, 0).reshape(length, width)
        token_grad_two = ordered(token_grad, token_other, x, 0).reshape(2 * length, width)
    with jax.named_scope("reduce_qkv"):
        qkv_a = halve(added(qkv_a[0], after(qkv_a[1], token_moved)), "x", 1)
        qkv_b = halve(added(qkv_b[0], after(qkv_b[1], token_moved)), "y", 1)

    input_w_grad = dot_tn(inputs, hidden_zero_grad)
    input_rows = input_proj.shape[0]
    with jax.named_scope("reduce_small"):
        vector_grad = jnp.concatenate(
            [
                pick(part.reshape(zy + (2, 2, rows_here)), c, 2)
                for part in (gain_one_part, bias_one_part, gain_two_part, bias_two_part)
            ]
            + [up_bias_part.reshape(zy + (2, -1))],
            axis=-1,
        ).reshape(zy + (2, -1, 128))
        small_grad = jnp.concatenate(
            [
                pick(input_w_grad.reshape(zy + (2, 2, input_rows, D)), c, 2).reshape(
                    zy + (2, rows_here, width)
                ),
                pick(output_w_grad.reshape(zy + (2, 2, rows_here, width)), c, 2),
                jnp.pad(
                    vector_grad,
                    ((0, 0),) * 3 + ((0, rows_here - vector_grad.shape[3]), (0, 128)),
                ),
            ],
            axis=-1,
        ).astype(BF)
        small_terms = halve(small_grad, "y", 1)

    with jax.named_scope("reduce_small"):
        small_terms = halve(added(small_terms[0], after(small_terms[1], token_moved)), "x", 1)
    with jax.named_scope("reduce_attn"):
        attn_sum = added(attn_terms[0], after(attn_terms[1], token_moved))
    with jax.named_scope("reduce_mlp"):
        mlp_ring = ring_up(ring_next(mlp_sum, after(mlp_ring, token_moved), 2, "z").astype(BF), "z")
    table_terms = table_add(table_sums, slots_here, token_grad_two)
    table_terms = after(table_terms, qkv_a[1], qkv_b[1], small_terms[1], mlp_ring)
    with jax.named_scope("reduce_table"):
        terms = table_terms.reshape(2, zn, block_len, width)
        terms_a, terms_b = terms[:, :, :table_cut], terms[:, :, table_cut:]
        moved_a = swap(terms_a[1], "y")
        moved_b = ring_up(terms_b[:, zn - 1], "z")
    with jax.named_scope("reduce_rest"):
        rest_sum = jnp.concatenate(
            [
                jnp.concatenate(
                    [
                        added(qkv_a[0], after(qkv_a[1], table_terms)),
                        added(qkv_b[0], after(qkv_b[1], table_terms)),
                    ],
                    1,
                ),
                added(small_terms[0], after(small_terms[1], table_terms))
                .reshape(zn, rows_here, 2, -1)
                .transpose(0, 2, 1, 3)
                .reshape(zn, 2 * rows_here, -1),
                attn_sum.reshape(zn, rows_here, 2, D // 2)
                .transpose(0, 2, 1, 3)
                .reshape(zn, 2 * rows_here, D // 2),
            ],
            2,
        )
        rest_ring = ring_start(rest_sum, "z")
    moved_b, rest_ring = lax.optimization_barrier((moved_b, rest_ring))
    for step in range(1, zn):
        with jax.named_scope("reduce_table"):
            total_b = terms_b[:, zn - 1 - step].astype(F32) + moved_b.astype(F32)
            if step < zn - 1:
                moved_b = ring_up(total_b.astype(BF), "z")
            else:
                moved_b = swap(total_b[1].astype(BF), "y")
        with jax.named_scope("reduce_rest"):
            rest_own = ring_next(rest_sum, rest_ring, step, "z")
            if step < zn - 1:
                rest_ring = ring_up(rest_own.astype(BF), "z")
        with jax.named_scope("reduce_table"):
            if step == 1:
                sum_a = added(terms_a[0], moved_a)
                moving_a = ring_up(sum_a[zn - 1], "z")
            else:
                total_a = sum_a[zn - step].astype(F32) + moving_a.astype(F32)
                moving_a = ring_up(total_a.astype(BF), "z")
        moved_b, rest_ring, moving_a = lax.optimization_barrier((moved_b, rest_ring, moving_a))
    with jax.named_scope("reduce_table"):
        total_b = total_b[0] + moved_b.astype(F32)
        total_a = sum_a[0].astype(F32) + moving_a.astype(F32)
    with jax.named_scope("reduce_mlp"):
        mlp_own = ring_next(mlp_sum, after(mlp_ring, rest_sum), 3, "z")

    up_total = mlp_own[:, : ff // 2].reshape(2, rows_here, ff // 2)
    down_own = jnp.concatenate([mlp_own[:, ff // 2 : ff // 2 + D], mlp_own[:, ff // 2 + D :]], 0)
    qkv_total = rest_own[:, :qkv_cols].reshape(2, rows_here, qkv_cols)
    small_end = rest_own.shape[1] - D // 2
    small_own = rest_own[:, qkv_cols:small_end]
    small_own = jnp.concatenate([small_own[:rows_here], small_own[rows_here:]], 1)
    attn_own = rest_own[:, small_end:]
    attn_own = jnp.concatenate([attn_own[:rows_here], attn_own[rows_here:]], 1)

    unit_grad = jnp.concatenate([total_a, total_b], axis=0)
    own_rows = embed_table.astype(F32)
    inverse = lax.rsqrt(jnp.mean(own_rows * own_rows, axis=1, keepdims=True) + 1e-06)
    along = jnp.mean(own_rows * unit_grad, axis=1, keepdims=True)
    table_grad = inverse * unit_grad - own_rows * (inverse * inverse * inverse * along)

    input_own = small_own[:, :width].reshape(input_rows, D)
    output_own = small_own[:, width : 2 * width]
    vector_own = small_own[: vector.size // 128, 2 * width : 2 * width + 128].reshape(-1)
    gains = [vector_own[k * rows_here : (k + 1) * rows_here] for k in range(4)]

    def columns_back(sums, split_shape, axis):
        mine_rows, other_rows = pick(sums, c, 0), pick(sums, 1 - c, 0)
        other_cols = swap(other_rows, "c")
        return ordered(
            mine_rows.reshape(split_shape), other_cols.reshape(split_shape), c, axis
        ).reshape(rows_here, -1)

    qkv_own = columns_back(qkv_total, (rows_here, 3 * heads // 2, HEAD_DIM), 2)
    up_own = columns_back(up_total, (rows_here, groups, ff_block), 2)
    return (
        token_loss,
        table_grad,
        input_own,
        gains[0],
        gains[1],
        qkv_own,
        attn_own,
        gains[2],
        gains[3],
        up_own,
        vector_own[4 * rows_here :],
        down_own,
        output_own,
    )


def combined_all(shard, axis, combine):
    everything = jax.tree.map(lambda part: lax.all_gather(part, axis), shard)
    first = jax.tree.map(lambda part: part[0], everything)

    def step(k, so_far):
        return combine(so_far, jax.tree.map(lambda part: part[k], everything))

    return lax.fori_loop(1, lax.axis_size(axis), step, first)


def product(left, right):
    return jnp.dot(left, right, preferred_element_type=jnp.float32)


def product_left(left, right):
    return lax.dot_general(
        left, right, (((0,), (0,)), ((), ())), preferred_element_type=jnp.float32
    )


def product_right(left, right):
    return lax.dot_general(
        left, right, (((1,), (1,)), ((), ())), preferred_element_type=jnp.float32
    )


def normalize_rows(matrix):
    return matrix * lax.rsqrt(jnp.mean(matrix * matrix, axis=1, keepdims=True) + 1e-06)


def layer_norm(hidden, norm_gain, norm_bias):
    centre = hidden - jnp.mean(hidden, axis=-1, keepdims=True)
    spread = jnp.mean(centre * centre, axis=-1, keepdims=True)
    return centre * lax.rsqrt(spread + 1e-05) * norm_gain + norm_bias


def exact_gelu(pre_act):
    return jax.nn.gelu(pre_act, approximate=False)


def noise_rows(row_seeds, positions, channel_count):
    channel = lax.iota(jnp.int32, channel_count)
    mixed_once = (
        row_seeds[:, None, None] + 7919 * positions[None, :, None] + 104729 * channel[None, None, :]
    ) % 65521
    mixed_twice = (mixed_once * (mixed_once % 32719) + 31 * channel[None, None, :]) % 65521
    return (mixed_twice.astype(jnp.float32) / 32760.5 - 1.0) * 1.7320508


def time_terms(time_steps):
    fraction = time_steps.astype(jnp.float32) / (TSTEPS - 1)
    noise_level = 0.3 * jnp.exp(fraction * math.log(30.0))
    return (noise_level, lax.rsqrt(1.0 + noise_level * noise_level), 0.5 + fraction)


def masked_scores(query_block, key_rows, segment_block, segment_row):
    scores = jnp.einsum("qhd,khd->hqk", query_block, key_rows, preferred_element_type=jnp.float32)
    same_doc = segment_block[:, None] == segment_row[None, :]
    return jnp.where(same_doc[None], scores, -1e30)


def attend_row(operands):
    queries, key_rows, value_rows, segment_row = operands
    length = queries.shape[0]
    block_rows = math.gcd(length, 512)
    block_count = length // block_rows

    def attend_block(pieces):
        query_block, segment_block = pieces
        scores = masked_scores(query_block, key_rows, segment_block, segment_row)
        row_max = jnp.max(scores, axis=-1, keepdims=True)
        raised = jnp.exp(scores - row_max)
        summed = jnp.sum(raised, axis=-1, keepdims=True)
        probs_low = (raised / summed).astype(jnp.bfloat16)
        attended = jnp.einsum(
            "hqk,khd->qhd", probs_low, value_rows, preferred_element_type=jnp.float32
        )
        return (attended.astype(jnp.bfloat16), (row_max + jnp.log(summed))[..., 0])

    attended, log_total = lax.map(
        attend_block,
        (
            queries.reshape((block_count, block_rows) + queries.shape[1:]),
            segment_row.reshape(block_count, block_rows),
        ),
    )
    return (attended.reshape(queries.shape), log_total)


def attend_back_row(operands):
    queries, key_rows, value_rows, segment_row, grad_rows, log_total = operands
    length = queries.shape[0]
    block_rows = math.gcd(length, 512)
    block_count = length // block_rows

    def back_block(carry, pieces):
        key_sum, value_sum = carry
        query_block, segment_block, grad_block, total_block = pieces
        scores = masked_scores(query_block, key_rows, segment_block, segment_row)
        probs = jnp.exp(scores - total_block[:, :, None])
        prob_grad = jnp.einsum(
            "qhd,khd->hqk", grad_block, value_rows, preferred_element_type=jnp.float32
        )
        score_grad = (
            probs * (prob_grad - jnp.sum(probs * prob_grad, axis=-1, keepdims=True))
        ).astype(jnp.bfloat16)
        query_grad = jnp.einsum(
            "hqk,khd->qhd", score_grad, key_rows, preferred_element_type=jnp.float32
        )
        key_sum = key_sum + jnp.einsum(
            "hqk,qhd->khd", score_grad, query_block, preferred_element_type=jnp.float32
        )
        value_sum = value_sum + jnp.einsum(
            "hqk,qhd->khd",
            probs.astype(jnp.bfloat16),
            grad_block,
            preferred_element_type=jnp.float32,
        )
        return ((key_sum, value_sum), query_grad.astype(jnp.bfloat16))

    block_shape = (block_count, block_rows) + queries.shape[1:]
    start_sums = (jnp.zeros(key_rows.shape, jnp.float32), jnp.zeros(value_rows.shape, jnp.float32))
    (key_sum, value_sum), query_grad = lax.scan(
        back_block,
        start_sums,
        (
            queries.reshape(block_shape),
            segment_row.reshape(block_count, block_rows),
            grad_rows.reshape(block_shape),
            log_total,
        ),
    )
    return (
        query_grad.reshape(queries.shape),
        key_sum.astype(jnp.bfloat16),
        value_sum.astype(jnp.bfloat16),
    )


def join_parts(first, second):
    top = jnp.maximum(first[0], second[0])
    total = first[1] * jnp.exp(first[0] - top) + second[1] * jnp.exp(second[0] - top)
    return (top, total, first[2] + second[2], first[3] + second[3])


def local(
    token_ids,
    segment_ids,
    time_steps,
    row_seeds,
    loss_weights,
    embed_table,
    input_proj,
    attn_gain,
    attn_bias,
    qkv_proj,
    attn_proj,
    mlp_gain,
    mlp_bias,
    up_proj,
    up_bias,
    down_proj,
    output_proj,
):
    seq_count = lax.axis_size("seq")
    seq_place = lax.axis_index("seq")
    dp_count = lax.axis_size("dp")
    row_count, length = token_ids.shape
    local_len = length // seq_count
    tok_count = row_count * local_len
    start_pos = seq_place * local_len
    own_ids = lax.dynamic_slice_in_dim(token_ids, start_pos, local_len, 1)
    positions = start_pos + lax.iota(jnp.int32, local_len)
    gathered = (
        lax.all_gather(embed_table, ("dp", "seq"), axis=0, tiled=True),
        lax.all_gather(input_proj, ("dp", "seq"), axis=0, tiled=True),
        lax.all_gather(attn_gain, ("dp", "seq"), axis=0, tiled=True),
        lax.all_gather(attn_bias, ("dp", "seq"), axis=0, tiled=True),
        lax.all_gather(qkv_proj, ("dp", "seq"), axis=0, tiled=True),
        lax.all_gather(attn_proj, ("dp", "seq"), axis=0, tiled=True),
        lax.all_gather(mlp_gain, ("dp", "seq"), axis=0, tiled=True),
        lax.all_gather(mlp_bias, ("dp", "seq"), axis=0, tiled=True),
        lax.all_gather(up_proj, ("dp", "seq"), axis=0, tiled=True),
        lax.all_gather(up_bias, ("dp", "seq"), axis=0, tiled=True),
        lax.all_gather(down_proj, ("dp", "seq"), axis=0, tiled=True),
        lax.all_gather(output_proj, ("dp", "seq"), axis=0, tiled=True),
    )
    (
        table_full,
        input_full,
        gain_one,
        bias_one,
        qkv_full,
        attn_full,
        gain_two,
        bias_two,
        up_full,
        upbias_full,
        down_full,
        output_full,
    ) = gathered
    vocab_size, embed_width = table_full.shape
    block_len = vocab_size // (dp_count * seq_count)
    unit, unit_back = jax.vjp(normalize_rows, table_full.astype(jnp.float32))
    sub_table = lax.dynamic_slice_in_dim(
        table_full.reshape(dp_count, seq_count, block_len, embed_width), seq_place, 1, 1
    ).reshape(dp_count * block_len, embed_width)
    sub_unit = lax.dynamic_slice_in_dim(
        unit.reshape(dp_count, seq_count, block_len, embed_width), seq_place, 1, 1
    ).reshape(dp_count * block_len, embed_width)
    scaled = (sub_unit * embed_width ** (-0.5)).astype(jnp.bfloat16)
    local_rows = lax.iota(jnp.int32, dp_count * block_len)
    vocab_index = (
        local_rows // block_len * seq_count + seq_place
    ) * block_len + local_rows % block_len
    noise_level, input_scale, residual_scale = time_terms(time_steps)
    noise = noise_rows(row_seeds, positions, embed_width)
    embedded = jnp.take(unit, own_ids, axis=0)
    inputs = (
        (input_scale[:, None, None] * (embedded + noise_level[:, None, None] * noise))
        .astype(jnp.bfloat16)
        .reshape(tok_count, embed_width)
    )
    token_scale = jnp.repeat(residual_scale, local_len)[:, None]
    token_input_scale = jnp.repeat(input_scale, local_len)[:, None]
    hidden_zero = product(inputs, input_full)
    first_norm, first_back = jax.vjp(
        layer_norm, hidden_zero, gain_one.astype(jnp.float32), bias_one.astype(jnp.float32)
    )
    first_in = first_norm.astype(jnp.bfloat16)
    qkv = product(first_in, qkv_full)
    query_tok = (
        (qkv[:, :D] * HEAD_DIM ** (-0.5)).astype(jnp.bfloat16).reshape(row_count, local_len, D)
    )
    key_tok = qkv[:, D : 2 * D].astype(jnp.bfloat16).reshape(row_count, local_len, D)
    value_tok = qkv[:, 2 * D :].astype(jnp.bfloat16).reshape(row_count, local_len, D)
    head_q, head_k, head_v = (
        lax.all_to_all(query_tok, "seq", split_axis=2, concat_axis=1, tiled=True),
        lax.all_to_all(key_tok, "seq", split_axis=2, concat_axis=1, tiled=True),
        lax.all_to_all(value_tok, "seq", split_axis=2, concat_axis=1, tiled=True),
    )
    heads_here = head_q.shape[2] // HEAD_DIM
    head_shape = (row_count, length, heads_here, HEAD_DIM)
    head_q = head_q.reshape(head_shape)
    head_k = head_k.reshape(head_shape)
    head_v = head_v.reshape(head_shape)
    attended, log_total = lax.map(attend_row, (head_q, head_k, head_v, segment_ids))
    attended = attended.reshape(row_count, length, heads_here * HEAD_DIM)
    mixed = lax.all_to_all(attended, "seq", split_axis=1, concat_axis=2, tiled=True).reshape(
        tok_count, D
    )
    hidden_one = hidden_zero + token_scale * product(mixed, attn_full)
    second_norm, second_back = jax.vjp(
        layer_norm, hidden_one, gain_two.astype(jnp.float32), bias_two.astype(jnp.float32)
    )
    second_in = second_norm.astype(jnp.bfloat16)
    pre_act = product(second_in, up_full) + upbias_full.astype(jnp.float32)
    activated, gelu_back = jax.vjp(exact_gelu, pre_act)
    act_low = activated.astype(jnp.bfloat16)
    hidden_two = hidden_one + token_scale * product(act_low, down_full)
    final_in = hidden_two.astype(jnp.bfloat16)
    outputs = product(final_in, output_full).astype(jnp.bfloat16)
    group_tok = seq_count * tok_count
    group_out = lax.all_gather(outputs, "seq", axis=0, tiled=True)
    group_ids = (
        token_ids.reshape(row_count, seq_count, local_len).transpose(1, 0, 2).reshape(group_tok)
    )
    spread = jnp.where(
        lax.iota(jnp.int32, seq_count)[:, None] == seq_place,
        loss_weights.reshape(1, tok_count),
        0.0,
    )
    tile_rows = math.gcd(group_tok, 512)
    tile_count = group_tok // tile_rows
    out_tiles = group_out.reshape(tile_count, tile_rows, embed_width)
    id_tiles = group_ids.reshape(tile_count, tile_rows)

    def part_tile(pieces):
        out_block, target_block = pieces
        logits = product_right(out_block, scaled)
        row_max = jnp.max(logits, axis=1)
        exp_sum = jnp.sum(jnp.exp(logits - row_max[:, None]), axis=1)
        picked = jnp.sum(
            jnp.where(vocab_index[None, :] == target_block[:, None], logits, 0.0), axis=1
        )
        return (row_max, exp_sum, picked)

    part_max, part_sum, part_pick = lax.map(part_tile, (out_tiles, id_tiles))
    top, total, pick, weight_tiles = combined_all(
        (part_max, part_sum, part_pick, spread), "seq", join_parts
    )
    log_tiles = top + jnp.log(total)
    all_loss = log_tiles - pick
    token_loss = lax.dynamic_slice_in_dim(all_loss, seq_place, 1, 0)

    def back_tile(scaled_sum, pieces):
        out_block, target_block, log_block, weight_block = pieces
        logits = product_right(out_block, scaled)
        probs = jnp.exp(logits - log_block[:, None])
        onehot = (vocab_index[None, :] == target_block[:, None]).astype(jnp.float32)
        grad_logits = (weight_block[:, None] * (probs - onehot)).astype(jnp.bfloat16)
        scaled_sum = scaled_sum + product_left(grad_logits, out_block)
        return (scaled_sum, product(grad_logits, scaled))

    scaled_grad, out_terms = lax.scan(
        back_tile,
        jnp.zeros(scaled.shape, jnp.float32),
        (out_tiles, id_tiles, log_tiles, weight_tiles),
    )
    out_terms = out_terms.reshape(tile_count * tile_rows, embed_width)
    out_grad = lax.psum_scatter(out_terms, "seq", scatter_dimension=0, tiled=True).astype(
        jnp.bfloat16
    )
    output_w_grad = product_left(final_in, out_grad)
    hidden_two_grad = product_right(out_grad, output_full)
    branch_grad = (token_scale * hidden_two_grad).astype(jnp.bfloat16)
    down_w_grad = product_left(act_low, branch_grad)
    pre_grad = gelu_back(product_right(branch_grad, down_full))[0].astype(jnp.bfloat16)
    up_w_grad = product_left(second_in, pre_grad)
    upbias_grad = jnp.sum(pre_grad, axis=0, dtype=jnp.float32)
    hidden_one_part, gain_two_grad, bias_two_grad = second_back(product_right(pre_grad, up_full))
    hidden_one_grad = hidden_two_grad + hidden_one_part
    attn_grad = (token_scale * hidden_one_grad).astype(jnp.bfloat16)
    attn_w_grad = product_left(mixed, attn_grad)
    mixed_grad = (
        product_right(attn_grad, attn_full).astype(jnp.bfloat16).reshape(row_count, local_len, D)
    )
    head_grad = lax.all_to_all(mixed_grad, "seq", split_axis=2, concat_axis=1, tiled=True).reshape(
        head_shape
    )
    query_grad, key_grad, value_grad = lax.map(
        attend_back_row, (head_q, head_k, head_v, segment_ids, head_grad, log_total)
    )
    merged_shape = (row_count, length, heads_here * HEAD_DIM)
    query_back, key_back, value_back = (
        lax.all_to_all(
            query_grad.reshape(merged_shape), "seq", split_axis=1, concat_axis=2, tiled=True
        ),
        lax.all_to_all(
            key_grad.reshape(merged_shape), "seq", split_axis=1, concat_axis=2, tiled=True
        ),
        lax.all_to_all(
            value_grad.reshape(merged_shape), "seq", split_axis=1, concat_axis=2, tiled=True
        ),
    )
    qkv_grad = jnp.concatenate(
        [query_back * HEAD_DIM ** (-0.5), key_back, value_back], axis=2
    ).reshape(tok_count, 3 * D)
    qkv_w_grad = product_left(first_in, qkv_grad)
    hidden_zero_part, gain_one_grad, bias_one_grad = first_back(product_right(qkv_grad, qkv_full))
    hidden_zero_grad = (hidden_one_grad + hidden_zero_part).astype(jnp.bfloat16)
    input_w_grad = product_left(inputs, hidden_zero_grad)
    embedded_grad = token_input_scale * product_right(hidden_zero_grad, input_full)
    scaled_part = scaled_grad * embed_width ** (-0.5)
    group_grad = lax.all_gather(
        embedded_grad.astype(jnp.bfloat16), "seq", axis=0, tiled=True
    ).astype(embedded_grad.dtype)
    block_id = group_ids // block_len
    owned = block_id % seq_count == seq_place
    local_slot = jnp.where(
        owned, block_id // seq_count * block_len + group_ids % block_len, scaled.shape[0]
    )
    unit_grad = scaled_part.at[local_slot].add(group_grad, mode="drop")
    table_term = jax.vjp(normalize_rows, sub_table.astype(jnp.float32))[1](unit_grad)[0]
    table_grad = lax.psum_scatter(
        table_term.astype(jnp.bfloat16), "dp", scatter_dimension=0, tiled=True
    ).astype(jnp.float32)
    summed = (
        lax.psum_scatter(input_w_grad, ("dp", "seq"), scatter_dimension=0, tiled=True),
        lax.psum_scatter(gain_one_grad, ("dp", "seq"), scatter_dimension=0, tiled=True),
        lax.psum_scatter(bias_one_grad, ("dp", "seq"), scatter_dimension=0, tiled=True),
        lax.psum_scatter(qkv_w_grad, ("dp", "seq"), scatter_dimension=0, tiled=True),
        lax.psum_scatter(attn_w_grad, ("dp", "seq"), scatter_dimension=0, tiled=True),
        lax.psum_scatter(gain_two_grad, ("dp", "seq"), scatter_dimension=0, tiled=True),
        lax.psum_scatter(bias_two_grad, ("dp", "seq"), scatter_dimension=0, tiled=True),
        lax.psum_scatter(up_w_grad, ("dp", "seq"), scatter_dimension=0, tiled=True),
        lax.psum_scatter(upbias_grad, ("dp", "seq"), scatter_dimension=0, tiled=True),
        lax.psum_scatter(down_w_grad, ("dp", "seq"), scatter_dimension=0, tiled=True),
        lax.psum_scatter(output_w_grad, ("dp", "seq"), scatter_dimension=0, tiled=True),
    )
    return (token_loss.reshape(row_count, local_len), table_grad) + tuple(summed)


def solution(mesh):
    dp, seq = mesh.shape["dp"], mesh.shape["seq"]
    if (dp, seq) == (16, 2):
        inner = Mesh(mesh.devices.reshape(dp // 4, 2, 2, seq), ("z", "y", "c", "x"))
        dp_names, seq_names, body = ("z", "y", "c"), ("x",), paired
    else:
        inner, dp_names, seq_names, body = mesh, ("dp",), ("seq",), local
    every = dp_names + seq_names
    in_specs = (
        P(dp_names, None),
        P(dp_names, None),
        P(dp_names),
        P(dp_names),
        P(dp_names, seq_names),
        P(every, None),
        P(every, None),
        P(every),
        P(every),
        P(every, None),
        P(every, None),
        P(every),
        P(every),
        P(every, None),
        P(every),
        P(every, None),
        P(every, None),
    )
    out_specs = (
        P(dp_names, seq_names),
        P(every, None),
        P(every, None),
        P(every),
        P(every),
        P(every, None),
        P(every, None),
        P(every),
        P(every),
        P(every, None),
        P(every),
        P(every, None),
        P(every, None),
    )
    return jax.shard_map(body, mesh=inner, in_specs=in_specs, out_specs=out_specs, check_vma=False)
```

profile of v0, /device:TPU:0, one launch (start us, length us, event | category | flops | bytes accessed | tf_op | source)
XLA Modules:
  0.0 682.9 jit_solution(3214709683674541375)
XLA Ops:
  24.8 8.1 %collective-permute-done.6 = bf16[1,64,2688]{2,1,0:T(8,128)(2,1)} collective-permute-done((bf16[1,64,2688]{2,1,0:T(8,128)(2,1)S(1)}, bf16[1,64,2688]{2,1,0:T(8,128)(2,1)}, u32[]{:S(2)}, u32[]{:S(2)}) %collective-permute-start.6) | collective-permute-done | bytes 344096 | tf_op jit(solution)/shard_map/gather_first/ppermute | solution.py:40
  35.2 14.1 %collective-permute-done.2 = bf16[1,496,256]{2,1,0:T(8,128)(2,1)S(1)} collective-permute-done((bf16[1,496,256]{2,1,0:T(8,128)(2,1)S(1)}, bf16[1,496,256]{2,1,0:T(8,128)(2,1)S(1)}, u32[]{:S(2)}, u32[]{:S(2)}) %collective-permute-start.2) | collective-permute-done | bytes 253984 | tf_op jit(solution)/shard_map/gather_table/ppermute | solution.py:40
  51.9 4.9 collective-permute-done.7
  62.8 10.5 %collective-permute-done.13 = bf16[2,504,256]{2,1,0:T(8,128)(2,1)} collective-permute-done((bf16[2,504,256]{2,1,0:T(8,128)(2,1)}, bf16[2,504,256]{2,1,0:T(8,128)(2,1)}, u32[]{:S(2)}, u32[]{:S(2)}) %collective-permute-start.13) | collective-permute-done | bytes 516128 | tf_op jit(solution)/shard_map/gather_table/ppermute | solution.py:40
  75.7 4.8 collective-permute-done.8
  92.8 5.8 collective-permute-done.10
  103.2 11.2 %gather_fusion = bf16[2048,256]{1,0:T(8,128)(2,1)} fusion(bf16[8000,256]{1,0:T(8,128)(2,1)} %bitcast.452, s32[2048]{0:T(1024)S(1)} %broadcast_clamp_fusion), kind=kCustom, calls=%fused_computation | custom fusion | bytes 2105344 | tf_op jit(solution)/shard_map/jit(_take)/gather | solution.py:660
  125.4 11.2 %collective-permute-done.21 = bf16[1,128,1024]{2,1,0:T(8,128)(2,1)S(1)} collective-permute-done((bf16[1,128,1024]{2,1,0:T(8,128)(2,1)S(1)}, bf16[1,128,1024]{2,1,0:T(8,128)(2,1)S(1)}, u32[]{:S(2)}, u32[]{:S(2)}) %collective-permute-start.21) | collective-permute-done | bytes 262176 | tf_op jit(solution)/shard_map/gather_down/ppermute | solution.py:75
  146.4 9.8 %collective-permute-done.23 = bf16[2,64,2048]{2,1,0:T(8,128)(2,1)} collective-permute-done((bf16[2,64,2048]{2,1,0:T(8,128)(2,1)}, bf16[2,64,2048]{2,1,0:T(8,128)(2,1)}, u32[]{:S(2)}, u32[]{:S(2)}) %collective-permute-start.23) | collective-permute-done | bytes 524320 | tf_op jit(solution)/shard_map/gather_up/ppermute | solution.py:75
  158.6 8.9 %collective-permute-done.22 = bf16[2,128,1024]{2,1,0:T(8,128)(2,1)} collective-permute-done((bf16[2,128,1024]{2,1,0:T(8,128)(2,1)}, bf16[2,128,1024]{2,1,0:T(8,128)(2,1)}, u32[]{:S(2)}, u32[]{:S(2)}) %collective-permute-start.22) | collective-permute-done | bytes 524320 | tf_op jit(solution)/shard_map/gather_down/ppermute | solution.py:75
  212.1 20.0 %attend.1 = (bf16[1024,512]{1,0:T(8,128)(2,1)S(1)}, f32[4,2,1024]{2,1,0:T(2,128)S(1)}) custom-call(s32[4]{0:T(128)S(1)} %get-tuple-element.303.lo_ref, s32[4]{0:T(128)S(1)} %get-tuple-element.302.hi_ref, bf16[1024,512]{1,0:T(8,128)(2,1)S(1)} %fusion.7.q_ref, bf16[1024,512]{1,0:T(8,128)(2,1)S(1)} %get-tuple-element.200.k_ref, ...), custom_call_target="tpu_custom_call" | custom-call | flops 8589934592 | bytes 4194304 | tf_op jit(solution)/shard_map/attend/pallas_call | solution.py:236
  242.7 7.4 %place_blocks.4 = bf16[8,2,2,32,2048]{4,3,2,1,0:T(8,128)(2,1)S(1)} custom-call(s32[32]{0:T(128)S(1)} %pad_add_fusion.1.places_ref, bf16[8,32,2048]{2,1,0:T(8,128)(2,1)S(1)} %pad_maximum_fusion.10.refs_0_, bf16[8,32,2048]{2,1,0:T(8,128)(2,1)S(1)} %copy-done.11, bf16[8,32,2048]{2,1,0:T(8,128)(2,1)S(1)} %pad_maximum_fusion.11.refs_2_, ...), custom_call_target="tpu_custom_call" | custom-call | tf_op jit(solution)/shard_map/place_blocks/pallas_call | solution.py:129
  255.4 9.3 %multiply_convert_fusion.1 = (bf16[1024,2048]{1,0:T(8,128)(2,1)S(1)}, f32[1024,2048]{1,0:T(8,128)}) fusion(f32[2048]{0:T(1024)S(1)} %convert.85, bf16[1024,2048]{1,0:T(8,128)(2,1)S(1)} %bitcast.431, f32[1024,1024]{0,1:T(8,128)S(1)} %get-tuple-element.190, f32[1024]{0:T(1024)S(1)} %reshape.1329, f32[1024]{0:T(1024)S(1)} %reshape.1328, ...), kind=kOutput, calls=%fused_computation.8 | convolution fusion | flops 4312793088 | bytes 20996096 | tf_op jit(solution)/shard_map/dot_general | solution.py:23
  267.4 7.1 %place_blocks.5 = bf16[16,2,64,1024]{3,2,1,0:T(8,128)(2,1)S(1)} custom-call(s32[32]{0:T(128)S(1)} %pad_add_fusion.1.places_ref, bf16[8,64,1024]{2,1,0:T(8,128)(2,1)S(1)} %pad_maximum_fusion.12.refs_0_, bf16[8,64,1024]{2,1,0:T(8,128)(2,1)S(1)} %collective-permute-done.31.refs_1_, bf16[8,64,1024]{2,1,0:T(8,128)(2,1)S(1)} %pad_maximum_fusion.13.refs_2_, ...), custom_call_target="tpu_custom_call" | custom-call | tf_op jit(solution)/shard_map/place_blocks/pallas_call | solution.py:129
  293.0 4.8 collective-permute-done.34
  304.5 32.8 %score.1 = (bf16[8,1000,2048]{2,1,0:T(8,128)(2,1)}, f32[8,1,2048]{2,1,0:T(1,128)S(1)}, f32[256,2048]{1,0:T(8,128)S(1)}, f32[1,2048]{1,0:T(1,128)S(1)}) custom-call(f32[1,2048]{1,0:T(1,128)S(1)} %fusion.6.norm_ref, bf16[2048,256]{1,0:T(8,128)(2,1)S(1)} %bitcast.429, bf16[8,1000,256]{2,1,0:T(8,128)(2,1)} %pad_maximum_fusion.table_ref, ...), custom_call_target="tpu_custom_call" | custom-call | flops 16777216000 | bytes 32768000 | tf_op jit(solution)/shard_map/score/pallas_call | solution.py:413
  359.2 18.6 %table_product.1.sum_ref = f32[8,1000,256]{2,1,0:T(8,128)} custom-call(bf16[8,1000,2048]{2,1,0:T(8,128)(2,1)} %get-tuple-element.112.raised_ref, bf16[2048,256]{1,0:T(8,128)(2,1)S(1)} %bitcast.430, f32[2048,8]{1,0:T(8,128)S(1)} %fusion.50.coef_ref), custom_call_target="tpu_custom_call" | custom-call | flops 8388608000 | bytes 32768000 | tf_op jit(solution)/shard_map/table_product/pallas_call | solution.py:456
  381.4 7.4 %collective-permute-done.42 = bf16[256,512]{1,0:T(8,128)(2,1)} collective-permute-done((bf16[256,512]{1,0:T(8,128)(2,1)}, bf16[256,512]{1,0:T(8,128)(2,1)}, u32[]{:S(2)}, u32[]{:S(2)}) %collective-permute-start.42) | collective-permute-done | bytes 262176 | tf_op jit(solution)/shard_map/ppermute | solution.py:35
  394.3 5.2 convolution_convert_fusion.2
  403.0 9.6 %fusion.187 = (bf16[2048]{0:T(1024)(128)(2,1)S(1)}, bf16[1024,2048]{1,0:T(8,128)(2,1)S(1)}) fusion(f32[1024,2048]{1,0:T(8,128)} %get-tuple-element.285, f32[2048]{0:T(1024)S(1)} %copy-done.110, bf16[1024,1024]{0,1:T(8,128)(2,1)S(1)} %get-tuple-element.114, bf16[2048,1024]{1,0:T(8,128)(2,1)S(1)} %bitcast.434), kind=kOutput, calls=%fused_computation.578 | convolution fusion | flops 4324325376 | bytes 18886656 | tf_op jit(solution)/shard_map/dot_general | solution.py:27
  412.7 6.7 convolution_convert_fusion.1
  419.4 6.3 collective-permute-done.45
  427.3 8.4 %fusion.185 = (bf16[1024,1024]{0,1:T(8,128)(2,1)}, f32[1024,1024]{0,1:T(8,128)S(1)}) fusion(bf16[1024,2048]{1,0:T(8,128)(2,1)} %copy-done.122, bf16[1024,2048]{1,0:T(8,128)(2,1)S(1)} %bitcast.432), kind=kOutput, calls=%fused_computation.576 | convolution fusion | flops 4296015872 | bytes 14680064 | tf_op jit(solution)/shard_map/dot_general | solution.py:27
  453.3 11.2 %collective-permute-done.48 = bf16[4,2,32,2048]{3,2,0,1:T(8,128)(2,1)S(1)} collective-permute-done((bf16[4,2,32,2048]{3,2,0,1:T(8,128)(2,1)S(1)}, bf16[4,2,32,2048]{3,2,0,1:T(8,128)(2,1)S(1)}, u32[]{:S(2)}, u32[]{:S(2)}) %collective-permute-start.48) | collective-permute-done | bytes 1048608 | tf_op jit(solution)/shard_map/reduce_up/ppermute | solution.py:35
  476.0 17.5 %attend_back.1 = (bf16[1024,512]{1,0:T(8,128)(2,1)S(1)}, bf16[1024,512]{1,0:T(8,128)(2,1)S(1)}, bf16[1024,512]{1,0:T(8,128)(2,1)S(1)}) custom-call(s32[4]{0:T(128)S(1)} %copy-done.30, s32[4]{0:T(128)S(1)} %copy-done.28, bf16[1024,512]{1,0:T(8,128)(2,1)S(1)} %copy-done.9, bf16[1024,512]{1,0:T(8,128)(2,1)S(1)} %copy-done.17, bf16[1024,512]{1,0:T(8,128)(2,1)S(1)} %copy-done.15, ...), custom_call_target="tpu_custom_call" | custom-call | flops 17179869184 | bytes 8388608 | tf_op jit(solution)/shard_map/attend_back/pallas_call | solution.py:328
  566.3 11.3 %table_add.1 = bf16[8,1000,256]{2,1,0:T(8,128)(2,1)S(1)} custom-call(f32[8,1000,256]{2,1,0:T(8,128)} %table_product.1.sum_ref, s32[1,2048]{1,0:T(1,128)S(1)} %compare_select_fusion.13.slot_ref, bf16[2048,256]{1,0:T(8,128)(2,1)S(1)} %bitcast.445), custom_call_target="tpu_custom_call" | custom-call | flops 8388608000 | bytes 12288000 | tf_op jit(solution)/shard_map/table_add/pallas_call | solution.py:487
  594.2 12.2 %collective-permute-done.69 = bf16[64,2432]{1,0:T(8,128)(2,1)S(1)} collective-permute-done((bf16[64,2432]{1,0:T(8,128)(2,1)}, bf16[64,2432]{1,0:T(8,128)(2,1)S(1)}, u32[]{:S(2)}, u32[]{:S(2)}) %collective-permute-start.69) | collective-permute-done | bytes 311328 | tf_op jit(solution)/shard_map/reduce_rest/ppermute | solution.py:45
  608.7 8.6 %collective-permute-done.66 = bf16[4,624,256]{2,1,0:T(8,128)(2,1)} collective-permute-done((bf16[4,624,256]{2,1,0:T(8,128)(2,1)}, bf16[4,624,256]{2,1,0:T(8,128)(2,1)}, u32[]{:S(2)}, u32[]{:S(2)}) %collective-permute-start.66) | collective-permute-done | bytes 1277984 | tf_op jit(solution)/shard_map/reduce_table/ppermute | solution.py:35
  619.8 8.1 %collective-permute-done.70 = bf16[2,376,256]{2,1,0:T(8,128)(2,1)S(1)} collective-permute-done((bf16[2,376,256]{2,1,0:T(8,128)(2,1)S(1)}, bf16[2,376,256]{2,1,0:T(8,128)(2,1)S(1)}, u32[]{:S(2)}, u32[]{:S(2)}) %collective-permute-start.70) | collective-permute-done | bytes 385056 | tf_op jit(solution)/shard_map/reduce_table/ppermute | solution.py:45
  640.0 8.3 %collective-permute-done.74 = bf16[64,2432]{1,0:T(8,128)(2,1)} collective-permute-done((bf16[64,2432]{1,0:T(8,128)(2,1)}, bf16[64,2432]{1,0:T(8,128)(2,1)}, u32[]{:S(2)}, u32[]{:S(2)}) %collective-permute-start.74) | collective-permute-done | bytes 311328 | tf_op jit(solution)/shard_map/reduce_rest/ppermute | solution.py:45
  648.3 6.8 %collective-permute-done.75 = bf16[624,256]{1,0:T(8,128)(2,1)} collective-permute-done((bf16[624,256]{1,0:T(8,128)(2,1)}, bf16[624,256]{1,0:T(8,128)(2,1)}, u32[]{:S(2)}, u32[]{:S(2)}) %collective-permute-start.75) | collective-permute-done | bytes 319520 | tf_op jit(solution)/shard_map/reduce_table/ppermute | solution.py:45
  655.1 4.7 collective-permute-done.73
  (682 shorter events, 355.6 us)
Async XLA Ops:
  22.5 29.1 %collective-permute-start.12 = (bf16[2,504,256]{2,1,0:T(8,128)(2,1)S(1)}, bf16[2,504,256]{2,1,0:T(8,128)(2,1)}, u32[]{:S(2)}, u32[]{:S(2)}) collective-permute-start(bf16[2,504,256]{2,1,0:T(8,128)(2,1)S(1)} %get-tuple-element.236), channel_id=1, source_target_pairs={{0,24},{8,0},{16,8},{24,16},{1,25},{9,1},{17,9},{25,17},{2,26},{10... | collective-permute-start | bytes 1548296 | tf_op jit(solution)/shard_map/gather_table/ppermute | solution.py:40
  23.1 26.3 %collective-permute-start.2 = (bf16[1,496,256]{2,1,0:T(8,128)(2,1)S(1)}, bf16[1,496,256]{2,1,0:T(8,128)(2,1)S(1)}, u32[]{:S(2)}, u32[]{:S(2)}) collective-permute-start(bf16[1,496,256]{2,1,0:T(8,128)(2,1)S(1)} %collective-permute-done.1), channel_id=1, source_target_pairs={{0,24},{8,0},{16,8},{24,16},{1,25},{9,1},{17,9},{25,17},{2,26},{10... | collective-permute-start | bytes 761864 | tf_op jit(solution)/shard_map/gather_table/ppermute | solution.py:40
  32.9 23.9 %collective-permute-start.7 = (bf16[1,64,2688]{2,1,0:T(8,128)(2,1)}, bf16[1,64,2688]{2,1,0:T(8,128)(2,1)}, u32[]{:S(2)}, u32[]{:S(2)}) collective-permute-start(bf16[1,64,2688]{2,1,0:T(8,128)(2,1)} %collective-permute-done.6), channel_id=1, source_target_pairs={{0,24},{8,0},{16,8},{24,16},{1,25},{9,1},{17,9},{25,17},{2,26},{10... | collective-permute-start | bytes 1032200 | tf_op jit(solution)/shard_map/gather_first/ppermute | solution.py:40
  56.8 23.8 %collective-permute-start.8 = (bf16[1,64,2688]{2,1,0:T(8,128)(2,1)}, bf16[1,64,2688]{2,1,0:T(8,128)(2,1)S(1)}, u32[]{:S(2)}, u32[]{:S(2)}) collective-permute-start(bf16[1,64,2688]{2,1,0:T(8,128)(2,1)} %collective-permute-done.7), channel_id=1, source_target_pairs={{0,24},{8,0},{16,8},{24,16},{1,25},{9,1},{17,9},{25,17},{2,26},{10... | collective-permute-start | bytes 1032200 | tf_op jit(solution)/shard_map/gather_first/ppermute | solution.py:40
  62.3 24.4 %collective-permute-start.4 = (bf16[4,496,256]{2,1,0:T(8,128)(2,1)S(1)}, bf16[4,496,256]{2,1,0:T(8,128)(2,1)S(1)}, u32[]{:S(2)}, u32[]{:S(2)}) collective-permute-start(bf16[4,496,256]{2,1,0:T(8,128)(2,1)S(1)} %pad_maximum_fusion.15), channel_id=1, source_target_pairs={{0,4},{4,0},{1,5},{5,1},{2,6},{6,2},{3,7},{7,3},{8,12},{12,8},{9,1... | collective-permute-start | bytes 3047432 | tf_op jit(solution)/shard_map/gather_table/ppermute | solution.py:35
  91.2 24.7 %collective-permute-start.15 = (bf16[1,64,2048]{2,1,0:T(8,128)(2,1)S(1)}, bf16[1,64,2048]{2,1,0:T(8,128)(2,1)S(1)}, u32[]{:S(2)}, u32[]{:S(2)}) collective-permute-start(bf16[1,64,2048]{2,1,0:T(8,128)(2,1)S(1)} %slice_bitcast_fusion.11), channel_id=1, source_target_pairs={{0,8},{8,0},{16,24},{24,16},{1,9},{9,1},{17,25},{25,17},{2,10},{10... | collective-permute-start | bytes 786440 | tf_op jit(solution)/shard_map/gather_up/ppermute | solution.py:75
  118.6 37.6 %collective-permute-start.23 = (bf16[2,64,2048]{2,1,0:T(8,128)(2,1)}, bf16[2,64,2048]{2,1,0:T(8,128)(2,1)}, u32[]{:S(2)}, u32[]{:S(2)}) collective-permute-start(bf16[2,64,2048]{2,1,0:T(8,128)(2,1)} %constant_dynamic-update-slice_fusion.15), channel_id=1, source_target_pairs={{0,16},{8,24},{16,0},{24,8},{1,17},{9,25},{17,1},{25,9},{2,18},{10... | collective-permute-start | bytes 1572872 | tf_op jit(solution)/shard_map/gather_up/ppermute | solution.py:75
  137.5 30.0 %collective-permute-start.22 = (bf16[2,128,1024]{2,1,0:T(8,128)(2,1)}, bf16[2,128,1024]{2,1,0:T(8,128)(2,1)}, u32[]{:S(2)}, u32[]{:S(2)}) collective-permute-start(bf16[2,128,1024]{2,1,0:T(8,128)(2,1)} %pad_maximum_fusion.16), channel_id=1, source_target_pairs={{0,16},{8,24},{16,0},{24,8},{1,17},{9,25},{17,1},{25,9},{2,18},{10... | collective-permute-start | bytes 1572872 | tf_op jit(solution)/shard_map/gather_down/ppermute | solution.py:75
  143.2 41.8 %collective-permute-start.19 = (bf16[8,32,2688]{2,1,0:T(8,128)(2,1)S(1)}, bf16[8,32,2688]{2,1,0:T(8,128)(2,1)}, u32[]{:S(2)}, u32[]{:S(2)}) collective-permute-start(bf16[8,32,2688]{2,1,0:T(8,128)(2,1)S(1)} %pad_maximum_fusion.5.refs_0_), channel_id=1, source_target_pairs={{0,1},{1,0},{2,3},{3,2},{4,5},{5,4},{6,7},{7,6},{8,9},{9,8},{10,11... | collective-permute-start | bytes 4128776 | tf_op jit(solution)/shard_map/gather_first/ppermute | solution.py:35
  144.7 40.3 %collective-permute-start.20 = (bf16[8,32,2688]{2,1,0:T(8,128)(2,1)S(1)}, bf16[8,32,2688]{2,1,0:T(8,128)(2,1)}, u32[]{:S(2)}, u32[]{:S(2)}) collective-permute-start(bf16[8,32,2688]{2,1,0:T(8,128)(2,1)S(1)} %pad_maximum_fusion.6.refs_2_), channel_id=1, source_target_pairs={{0,4},{4,0},{1,5},{5,1},{2,6},{6,2},{3,7},{7,3},{8,12},{12,8},{9,1... | collective-permute-start | bytes 4128776 | tf_op jit(solution)/shard_map/gather_first/ppermute | solution.py:35
  146.4 23.4 %collective-permute-start.18 = (bf16[512,256]{1,0:T(8,128)(2,1)S(1)}, bf16[512,256]{1,0:T(8,128)(2,1)S(1)}, u32[]{:S(2)}, u32[]{:S(2)}) collective-permute-start(bf16[512,256]{1,0:T(8,128)(2,1)S(1)} %fusion.80), channel_id=1, source_target_pairs={{0,2},{2,0},{1,3},{3,1},{4,6},{6,4},{5,7},{7,5},{8,10},{10,8},{9,1... | collective-permute-start | bytes 786440 | tf_op jit(solution)/shard_map/ppermute | solution.py:35
  179.9 52.2 %collective-permute-start.29 = (bf16[4,64,1024]{2,1,0:T(8,128)(2,1)}, bf16[4,64,1024]{2,1,0:T(8,128)(2,1)}, u32[]{:S(2)}, u32[]{:S(2)}) collective-permute-start(bf16[4,64,1024]{2,1,0:T(8,128)(2,1)} %get-tuple-element.223), channel_id=1, source_target_pairs={{0,1},{1,0},{2,3},{3,2},{4,5},{5,4},{6,7},{7,6},{8,9},{9,8},{10,11... | collective-permute-start | bytes 1572872 | tf_op jit(solution)/shard_map/gather_down/ppermute | solution.py:35
  181.3 50.7 %collective-permute-start.28 = (bf16[4,64,1024]{2,1,0:T(8,128)(2,1)}, bf16[4,64,1024]{2,1,0:T(8,128)(2,1)}, u32[]{:S(2)}, u32[]{:S(2)}) collective-permute-start(bf16[4,64,1024]{2,1,0:T(8,128)(2,1)} %get-tuple-element.224), channel_id=1, source_target_pairs={{0,4},{4,0},{1,5},{5,1},{2,6},{6,2},{3,7},{7,3},{8,12},{12,8},{9,1... | collective-permute-start | bytes 1572872 | tf_op jit(solution)/shard_map/gather_down/ppermute | solution.py:35
  207.7 24.4 %collective-permute-start.25 = (bf16[8,32,2048]{2,1,0:T(8,128)(2,1)S(1)}, bf16[8,32,2048]{2,1,0:T(8,128)(2,1)S(1)}, u32[]{:S(2)}, u32[]{:S(2)}) collective-permute-start(bf16[8,32,2048]{2,1,0:T(8,128)(2,1)S(1)} %pad_maximum_fusion.10.refs_0_), channel_id=1, source_target_pairs={{0,1},{1,0},{2,3},{3,2},{4,5},{5,4},{6,7},{7,6},{8,9},{9,8},{10,11... | collective-permute-start | bytes 3145736 | tf_op jit(solution)/shard_map/gather_up/ppermute | solution.py:35
  210.3 23.2 %collective-permute-start.27 = (bf16[8,32,2048]{2,1,0:T(8,128)(2,1)S(1)}, bf16[8,32,2048]{2,1,0:T(8,128)(2,1)S(1)}, u32[]{:S(2)}, u32[]{:S(2)}) collective-permute-start(bf16[8,32,2048]{2,1,0:T(8,128)(2,1)S(1)} %pad_maximum_fusion.11.refs_2_), channel_id=1, source_target_pairs={{0,4},{4,0},{1,5},{5,1},{2,6},{6,2},{3,7},{7,3},{8,12},{12,8},{9,1... | collective-permute-start | bytes 3145736 | tf_op jit(solution)/shard_map/gather_up/ppermute | solution.py:35
  239.1 28.3 %collective-permute-start.31 = (bf16[8,64,1024]{2,1,0:T(8,128)(2,1)S(1)}, bf16[8,64,1024]{2,1,0:T(8,128)(2,1)S(1)}, u32[]{:S(2)}, u32[]{:S(2)}) collective-permute-start(bf16[8,64,1024]{2,1,0:T(8,128)(2,1)S(1)} %pad_maximum_fusion.12.refs_0_), channel_id=1, source_target_pairs={{0,1},{1,0},{2,3},{3,2},{4,5},{5,4},{6,7},{7,6},{8,9},{9,8},{10,11... | collective-permute-start | bytes 3145736 | tf_op jit(solution)/shard_map/gather_down/ppermute | solution.py:35
  242.1 25.4 %collective-permute-start.32 = (bf16[8,64,1024]{2,1,0:T(8,128)(2,1)S(1)}, bf16[8,64,1024]{2,1,0:T(8,128)(2,1)S(1)}, u32[]{:S(2)}, u32[]{:S(2)}) collective-permute-start(bf16[8,64,1024]{2,1,0:T(8,128)(2,1)S(1)} %pad_maximum_fusion.13.refs_2_), channel_id=1, source_target_pairs={{0,4},{4,0},{1,5},{5,1},{2,6},{6,2},{3,7},{7,3},{8,12},{12,8},{9,1... | collective-permute-start | bytes 3145736 | tf_op jit(solution)/shard_map/gather_down/ppermute | solution.py:35
  291.4 47.5 %collective-permute-start.40 = (f32[2,512]{1,0:T(2,128)}, f32[2,512]{1,0:T(2,128)}, u32[]{:S(2)}, u32[]{:S(2)}) collective-permute-start(f32[2,512]{1,0:T(2,128)} %maximum_select_fusion.10), channel_id=1, source_target_pairs={{0,1},{1,0},{2,3},{3,2},{4,5},{5,4},{6,7},{7,6},{8,9},{9,8},{10,11... | collective-permute-start | bytes 12296 | tf_op jit(solution)/shard_map/ppermute | solution.py:35
  400.4 25.3 %collective-permute-start.45 = (bf16[4,2,64,1024]{3,2,0,1:T(8,128)(2,1)S(1)}, bf16[4,2,64,1024]{3,2,0,1:T(8,128)(2,1)S(1)}, u32[]{:S(2)}, u32[]{:S(2)}) collective-permute-start(bf16[4,2,64,1024]{3,2,0,1:T(8,128)(2,1)S(1)} %bitcast.480), channel_id=1, source_target_pairs={{0,4},{4,0},{1,5},{5,1},{2,6},{6,2},{3,7},{7,3},{8,12},{12,8},{9,1... | collective-permute-start | bytes 3145736 | tf_op jit(solution)/shard_map/reduce_down/ppermute | solution.py:35
  402.3 25.0 %collective-permute-start.44 = (bf16[4,2,64,1024]{3,2,0,1:T(8,128)(2,1)S(1)}, bf16[4,2,64,1024]{3,2,0,1:T(8,128)(2,1)S(1)}, u32[]{:S(2)}, u32[]{:S(2)}) collective-permute-start(bf16[4,2,64,1024]{3,2,0,1:T(8,128)(2,1)S(1)} %bitcast.481), channel_id=1, source_target_pairs={{0,1},{1,0},{2,3},{3,2},{4,5},{5,4},{6,7},{7,6},{8,9},{9,8},{10,11... | collective-permute-start | bytes 3145736 | tf_op jit(solution)/shard_map/reduce_down/ppermute | solution.py:35
  438.5 26.0 %collective-permute-start.48 = (bf16[4,2,32,2048]{3,2,0,1:T(8,128)(2,1)S(1)}, bf16[4,2,32,2048]{3,2,0,1:T(8,128)(2,1)S(1)}, u32[]{:S(2)}, u32[]{:S(2)}) collective-permute-start(bf16[4,2,32,2048]{3,2,0,1:T(8,128)(2,1)S(1)} %bitcast.478), channel_id=1, source_target_pairs={{0,1},{1,0},{2,3},{3,2},{4,5},{5,4},{6,7},{7,6},{8,9},{9,8},{10,11... | collective-permute-start | bytes 3145736 | tf_op jit(solution)/shard_map/reduce_up/ppermute | solution.py:35
  439.8 26.1 %collective-permute-start.47 = (bf16[4,2,32,2048]{3,2,0,1:T(8,128)(2,1)S(1)}, bf16[4,2,32,2048]{3,2,0,1:T(8,128)(2,1)S(1)}, u32[]{:S(2)}, u32[]{:S(2)}) collective-permute-start(bf16[4,2,32,2048]{3,2,0,1:T(8,128)(2,1)S(1)} %bitcast.479), channel_id=1, source_target_pairs={{0,4},{4,0},{1,5},{5,1},{2,6},{6,2},{3,7},{7,3},{8,12},{12,8},{9,1... | collective-permute-start | bytes 3145736 | tf_op jit(solution)/shard_map/reduce_up/ppermute | solution.py:35
  443.2 51.5 %collective-permute-start.52 = (bf16[4,64,1024]{2,1,0:T(8,128)(2,1)}, bf16[4,64,1024]{2,1,0:T(8,128)(2,1)}, u32[]{:S(2)}, u32[]{:S(2)}) collective-permute-start(bf16[4,64,1024]{2,1,0:T(8,128)(2,1)} %dynamic-slice_bitcast_fusion.1), channel_id=1, source_target_pairs={{0,1},{1,0},{2,3},{3,2},{4,5},{5,4},{6,7},{7,6},{8,9},{9,8},{10,11... | collective-permute-start | bytes 1572872 | tf_op jit(solution)/shard_map/reduce_down/ppermute | solution.py:35
  445.3 49.4 %collective-permute-start.51 = (bf16[4,64,1024]{2,1,0:T(8,128)(2,1)}, bf16[4,64,1024]{2,1,0:T(8,128)(2,1)}, u32[]{:S(2)}, u32[]{:S(2)}) collective-permute-start(bf16[4,64,1024]{2,1,0:T(8,128)(2,1)} %dynamic-slice_bitcast_fusion.2), channel_id=1, source_target_pairs={{0,4},{4,0},{1,5},{5,1},{2,6},{6,2},{3,7},{7,3},{8,12},{12,8},{9,1... | collective-permute-start | bytes 1572872 | tf_op jit(solution)/shard_map/reduce_down/ppermute | solution.py:35
  474.8 24.2 %collective-permute-start.53 = (bf16[4,2,32,1024]{3,2,0,1:T(8,128)(2,1)}, bf16[4,2,32,1024]{3,2,0,1:T(8,128)(2,1)}, u32[]{:S(2)}, u32[]{:S(2)}) collective-permute-start(bf16[4,2,32,1024]{3,2,0,1:T(8,128)(2,1)} %bitcast.425), channel_id=1, source_target_pairs={{0,4},{4,0},{1,5},{5,1},{2,6},{6,2},{3,7},{7,3},{8,12},{12,8},{9,1... | collective-permute-start | bytes 1572872 | tf_op jit(solution)/shard_map/reduce_attn/ppermute | solution.py:35
  516.5 27.6 %collective-permute-start.68 = (bf16[4,32,1024]{2,1,0:T(8,128)(2,1)}, bf16[4,32,1024]{2,1,0:T(8,128)(2,1)}, u32[]{:S(2)}, u32[]{:S(2)}) collective-permute-start(bf16[4,32,1024]{2,1,0:T(8,128)(2,1)} %dynamic-slice_bitcast_fusion.11), channel_id=1, source_target_pairs={{0,1},{1,0},{2,3},{3,2},{4,5},{5,4},{6,7},{7,6},{8,9},{9,8},{10,11... | collective-permute-start | bytes 786440 | tf_op jit(solution)/shard_map/reduce_attn/ppermute | solution.py:35
  522.0 27.9 %collective-permute-start.59 = (bf16[4,2,32,1536]{3,2,0,1:T(8,128)(2,1)}, bf16[4,2,32,1536]{3,2,0,1:T(8,128)(2,1)}, u32[]{:S(2)}, u32[]{:S(2)}) collective-permute-start(bf16[4,2,32,1536]{3,2,0,1:T(8,128)(2,1)} %bitcast.423), channel_id=1, source_target_pairs={{0,1},{1,0},{2,3},{3,2},{4,5},{5,4},{6,7},{7,6},{8,9},{9,8},{10,11... | collective-permute-start | bytes 2359304 | tf_op jit(solution)/shard_map/reduce_qkv/ppermute | solution.py:35
  524.3 29.4 %collective-permute-start.57 = (bf16[4,2,32,1536]{3,2,0,1:T(8,128)(2,1)}, bf16[4,2,32,1536]{3,2,0,1:T(8,128)(2,1)}, u32[]{:S(2)}, u32[]{:S(2)}) collective-permute-start(bf16[4,2,32,1536]{3,2,0,1:T(8,128)(2,1)} %bitcast.424), channel_id=1, source_target_pairs={{0,4},{4,0},{1,5},{5,1},{2,6},{6,2},{3,7},{7,3},{8,12},{12,8},{9,1... | collective-permute-start | bytes 2359304 | tf_op jit(solution)/shard_map/reduce_qkv/ppermute | solution.py:35
  533.1 24.5 %collective-permute-start.61 = (bf16[4,2,32,768]{3,2,1,0:T(8,128)(2,1)}, bf16[4,2,32,768]{3,2,1,0:T(8,128)(2,1)}, u32[]{:S(2)}, u32[]{:S(2)}) collective-permute-start(bf16[4,2,32,768]{3,2,1,0:T(8,128)(2,1)} %dynamic-slice_bitcast_fusion.6), channel_id=1, source_target_pairs={{0,4},{4,0},{1,5},{5,1},{2,6},{6,2},{3,7},{7,3},{8,12},{12,8},{9,1... | collective-permute-start | bytes 1179656 | tf_op jit(solution)/shard_map/reduce_small/ppermute | solution.py:35
  552.5 25.2 %collective-permute-start.60 = (bf16[4,32,1536]{2,1,0:T(8,128)(2,1)}, bf16[4,32,1536]{2,1,0:T(8,128)(2,1)}, u32[]{:S(2)}, u32[]{:S(2)}) collective-permute-start(bf16[4,32,1536]{2,1,0:T(8,128)(2,1)} %dynamic-slice_bitcast_fusion.7), channel_id=1, source_target_pairs={{0,4},{4,0},{1,5},{5,1},{2,6},{6,2},{3,7},{7,3},{8,12},{12,8},{9,1... | collective-permute-start | bytes 1179656 | tf_op jit(solution)/shard_map/reduce_qkv/ppermute | solution.py:35
  587.5 29.8 %collective-permute-start.66 = (bf16[4,624,256]{2,1,0:T(8,128)(2,1)}, bf16[4,624,256]{2,1,0:T(8,128)(2,1)}, u32[]{:S(2)}, u32[]{:S(2)}) collective-permute-start(bf16[4,624,256]{2,1,0:T(8,128)(2,1)} %slice_bitcast_fusion), channel_id=1, source_target_pairs={{0,4},{4,0},{1,5},{5,1},{2,6},{6,2},{3,7},{7,3},{8,12},{12,8},{9,1... | collective-permute-start | bytes 3833864 | tf_op jit(solution)/shard_map/reduce_table/ppermute | solution.py:35
  635.9 23.9 %collective-permute-start.73 = (bf16[2,376,256]{2,1,0:T(8,128)(2,1)S(1)}, bf16[2,376,256]{2,1,0:T(8,128)(2,1)S(1)}, u32[]{:S(2)}, u32[]{:S(2)}) collective-permute-start(bf16[2,376,256]{2,1,0:T(8,128)(2,1)S(1)} %fusion.73), channel_id=1, source_target_pairs={{0,8},{8,16},{16,24},{24,0},{1,9},{9,17},{17,25},{25,1},{2,10},{10... | collective-permute-start | bytes 1155080 | tf_op jit(solution)/shard_map/reduce_table/ppermute | solution.py:45
  (171 other events, 2164.2 us)
where the time goes:
time: 692 us; the launch traced here: 683 us
  waiting for transfers between devices  207 us (30%)
  Pallas kernels  119 us (17%)
  other arithmetic  112 us (16%)
  local copies, waits for them, and re-layouts  100 us (14%)
  matrix products  70.8 us (10%)
  starting transfers between devices  68.3 us (10%)
    ppermute x55, waiting for transfers between devices, swap(): return lax.ppermute(value, axis, SWAP)  75.7 us
    ppermute x12, waiting for transfers between devices, ring_up(): return lax.ppermute(value, axis, [(i, (i + 1) % n) for i in range(n)])  52.2 us
    ppermute x9, waiting for transfers between devices, ring_down(): return lax.ppermute(value, axis, [(i, (i - 1) % n) for i in range(n)])  49.2 us
    ppermute x55, starting transfers between devices, swap(): return lax.ppermute(value, axis, SWAP)  45.4 us
    pallas_call x1, Pallas kernels, score(): pl.pallas_call(score_body, out_shape=(jax.ShapeDtypeStruct((blocks, rows,...  32.8 us
    ppermute x4, waiting for transfers between devices, apart(): return lax.ppermute(value, axis, [(i, i ^ distance) for i in range(n)])  29.9 us
    dot_general x7, matrix products, dot_nt(): lax.dot_general(left, right, (((1,), (1,)), ((), ())), preferred_element_...  27.2 us
    dot_general x6, matrix products, dot_nn(): lax.dot_general(left, right, (((1,), (0,)), ((), ())), preferred_element_...  24.6 us
  transfers between devices with their start and end apart: 80, of which 38 were waited for; matrix products, arithmetic and copies ran while one was open for 29% of the time, Pallas kernels for 16%

commit v1 on v0

--- a/solution.py
+++ b/solution.py
@@ -181,11 +181,11 @@
         def run(first, count):
             at = pl.ds(pl.multiple_of(first * blk, blk), count * blk)
             k = k_ref[at, :]
-            same = seg_col_ref[at, :] == seg_row_ref[:, rows]
+            same = seg_col_ref[rows, :] == seg_row_ref[:, at]
             accs = []
             for h in range(2):
-                e = jnp.exp(jnp.where(same, dot_nt(k, q_heads[h]), NEG)).astype(BF)
-                accs.append(dot_tn(e, v_ones[h, at, :]))
+                e = jnp.exp(jnp.where(same, dot_nt(q_heads[h], k), NEG)).astype(BF)
+                accs.append(dot_nn(e, v_ones[h, at, :]))
             for h, total in enumerate(finish(rows, accs)):
                 lse_ref[0, h : h + 1, rows] = jnp.log(total)
 
@@ -278,6 +278,7 @@
     dv_ref,
     dk_sum,
     dv_sum,
+    k_t,
 ):
     length = q_ref.shape[0]
     blk = min(256, length)
@@ -285,6 +286,7 @@
     masks = (lane < HEAD_DIM, lane >= HEAD_DIM)
     dk_sum[...] = jnp.zeros_like(dk_sum)
     dv_sum[...] = jnp.zeros_like(dv_sum)
+    k_t[...] = k_ref[...].astype(F32).T.astype(BF)
     def each(qi, _):
         rows = pl.ds(pl.multiple_of(qi * blk, blk), blk)
 
@@ -294,12 +296,11 @@
             at = pl.ds(pl.multiple_of(first * blk, blk), count * blk)
             k, v = k_ref[at, :], v_ref[at, :]
             same = seg_col_ref[at, :] == seg_row_ref[:, rows]
-            dq = jnp.zeros((blk, 128), F32)
+            dq = []
             dk, dv = dk_sum[at, :], dv_sum[at, :]
             for h in range(2):
                 q_head = jnp.where(masks[h], q, jnp.zeros_like(q))
                 g_head = jnp.where(masks[h], g, jnp.zeros_like(g))
-                k_head = jnp.where(masks[h], k, jnp.zeros_like(k))
                 delta = jnp.sum(mixed[h * HEAD_DIM : (h + 1) * HEAD_DIM], axis=0, keepdims=True)
                 s = dot_nt(k, q_head)
                 p = jnp.exp(jnp.where(same, s - lse_ref[0, h : h + 1, rows], NEG))
@@ -307,10 +308,10 @@
                 ds = (p * (dp - delta)).astype(BF)
                 dv = dv + dot_nn(p.astype(BF), g_head)
                 dk = dk + dot_nn(ds, q_head)
-                dq = dq + dot_tn(ds, k_head)
+                dq.append(dot_nn(k_t[h * HEAD_DIM : (h + 1) * HEAD_DIM, at], ds))
             dk_sum[at, :] = dk
             dv_sum[at, :] = dv
-            dq_ref[rows, :] = dq.astype(BF)
+            dq_ref[rows, :] = jnp.concatenate(dq, axis=0).T.astype(BF)
 
         for_each_window(lo_ref[qi], hi_ref[qi], length // blk, run)
         return 0
@@ -342,7 +343,11 @@
                 pl.BlockSpec((1, length), lambda i, *_: (0, 0)),
             ],
             out_specs=(spec, spec, spec),
-            scratch_shapes=[pltpu.VMEM((length, 128), F32), pltpu.VMEM((length, 128), F32)],
+            scratch_shapes=[
+                pltpu.VMEM((length, 128), F32),
+                pltpu.VMEM((length, 128), F32),
+                pltpu.VMEM((128, length), BF),
+            ],
         ),
         compiler_params=pltpu.CompilerParams(vmem_limit_bytes=32 * MIB),
         cost_estimate=pl.CostEstimate(
@@ -642,31 +647,31 @@
         up_first = after(up_shard[None], table_z, first_z[-1])
         up_moved = apart(up_first, "z", 1)
         up_two = jnp.concatenate([up_first, up_moved], 0)
-        up_z = jnp.concatenate([up_two, apart(up_two, "z", 2)], 0)
-        up_held = over_one(after(up_z, first_pieces[0][1], first_pieces[1][1]))
-        up_pieces = over_other(up_held)
+        up_far = apart(up_two, "z", 2)
     with jax.named_scope("gather_down"):
-        down_z = joined_apart(after(down_proj, up_two), "z")
+        down_first = after(down_proj[None], up_far)
+        down_moved = apart(down_first, "z", 1)
+        down_two = jnp.concatenate([down_first, down_moved], 0)
 
     flat_ids = ids_two.reshape(-1)
     owner = flat_ids // block_len
     within = flat_ids % block_len
     home = {"z": owner // 8, "y": owner // 4 % 2}
     mine = owner % 4 == c * 2 + x
-    table_rows = jnp.concatenate([after(table_a, *first_held), table_b], axis=1)
+    table_rows = jnp.concatenate([after(table_a, *first_held, up_moved), table_b], axis=1)
     zn = lax.axis_size("z")
     relative_y, relative_z = (home["y"] - y) % 2, (home["z"] - z) % zn
     slot = (relative_y * zn + relative_z) * block_len + within
     found = jnp.take(
         table_rows.reshape(groups * block_len, width), jnp.where(mine, slot, 0), axis=0
     )
-    found = after(found, up_moved)
     found = jnp.where(mine[:, None], found, jnp.zeros_like(found)).reshape(2, length, width)
 
-    def to_rows(terms, kind):
+    def to_rows(terms, kind, others):
         split = terms.reshape(2, 2, half, width)
         moved = swap(pick(split, 1 - c, 1).astype(kind), "c")
         both = pick(split, c, 1).astype(F32) + moved.astype(F32)
+        both = after(both, *others)
         moved = swap(pick(both, 1 - x, 0).astype(kind), "x")
         own = (pick(both, x, 0).astype(F32) + moved.astype(F32)).astype(kind)
         return ordered(own, swap(own, "c"), c, 0).reshape(length, width)
@@ -677,7 +682,12 @@
         other = ordered(moved, swap(moved, "c"), c, 0).reshape(length, width)
         return ordered(row, other, x, 0)
 
-    raw = to_rows(found, BF).astype(F32)
+    raw = to_rows(found, BF, (first_pieces[0][1], first_pieces[1][1], up_far))
+    raw_low = after(raw, down_moved)
+    raw = raw_low.astype(F32)
+    with jax.named_scope("gather_up"):
+        up_z = after(jnp.concatenate([up_two, up_far], 0), first_pieces[0][1], first_pieces[1][1])
+        up_moved = over_one_start(up_z)
     paired_shape = (groups, 2, 2, rows_here)
 
     def in_pairs(p, h):
@@ -718,6 +728,14 @@
     hidden_zero = dot_nn(inputs, input_full)
     normed_one, inverse_one = norm_parts(hidden_zero)
     first_in = (normed_one * gain_one + bias_one).astype(BF)
+    first_in = after(first_in, up_moved[0][1], up_moved[1][1])
+    with jax.named_scope("gather_up"):
+        up_held = [
+            jnp.concatenate([own, after(got, first_in)], 0) for own, got in up_moved
+        ]
+        up_pieces = over_other(up_held)
+    with jax.named_scope("gather_down"):
+        down_far = apart(after(down_two, raw_low), "z", 2)
     qkv = dot_nn(first_in, qkv_half)
     split = D // 2
     queries = (qkv[:, :split] * HEAD_DIM ** (-0.5)).astype(BF)
@@ -730,10 +748,10 @@
     through = jnp.sum(seg_row <= edges[:, -1:], axis=1, dtype=jnp.int32)
     low_block, high_block = before // blk, (through + blk - 1) // blk
     with jax.named_scope("gather_down"):
-        down_z = after(down_z, inputs)
+        down_z = jnp.concatenate([down_two, down_far], 0)
         down_moved = over_one_start(down_z)
     attended, log_total = attend(
-        after(queries, down_z), keys, values, seg_col, seg_row, low_block, high_block
+        after(queries, down_z, *up_held), keys, values, seg_col, seg_row, low_block, high_block
     )
     attended = after(
         attended, up_pieces[0][1], up_pieces[1][1], down_moved[0][1], down_moved[1][1]
@@ -784,20 +802,35 @@
 
     def joined(first, second):
         top = jnp.maximum(first[0], second[0])
-        return jnp.stack(
-            [top, first[1] * jnp.exp(first[0] - top) + second[1] * jnp.exp(second[0] - top)]
-        )
-
-    all_ends = joined(ends, swap(ends, "c"))
-    all_ends = joined(all_ends, swap(all_ends, "x"))
-    log_sum = all_ends[0] + jnp.log(all_ends[1])
-    share = (reached * jnp.exp(ends[0] - log_sum)[None, :]).astype(BF)
-    parts = [share[:, k * half : (k + 1) * half] for k in range(4)]
-    kept = jnp.concatenate([jnp.where(c == 0, parts[0], parts[1]), jnp.where(c == 0, parts[2], parts[3])], 1)
-    sent = jnp.concatenate([jnp.where(c == 0, parts[1], parts[0]), jnp.where(c == 0, parts[3], parts[2])], 1)
-    both = kept.astype(F32) + swap(sent, "c").astype(F32)
-    own, other = jnp.where(x == 0, both[:, :half], both[:, half:]), jnp.where(x == 0, both[:, half:], both[:, :half])
-    own = (own + swap(other.astype(BF), "x").astype(F32)).astype(BF)
+        scale_first, scale_second = jnp.exp(first[0] - top), jnp.exp(second[0] - top)
+        return jnp.stack([top, first[1] * scale_first + second[1] * scale_second])
+
+    def own_half(value):
+        parts = [value[:, k * half : (k + 1) * half] for k in range(4)]
+        low, high = jnp.concatenate(parts[::2], 1), jnp.concatenate(parts[1::2], 1)
+        return jnp.where(c == 0, low, high), jnp.where(c == 0, high, low)
+
+    def own_row(value):
+        first, second = value[:, :half], value[:, half:]
+        return jnp.where(x == 0, first, second), jnp.where(x == 0, second, first)
+
+    ends_c = swap(ends, "c")
+    kept, sent = own_half(reached)
+    moved = swap(sent.astype(BF), "c").astype(F32)
+    all_ends = joined(ends, ends_c)
+    ends_x = swap(all_ends, "x")
+    kept_top, _ = own_half(all_ends[:1])
+    both = kept * jnp.exp(own_half(ends[:1])[0] - kept_top) + moved * jnp.exp(
+        own_half(ends_c[:1])[0] - kept_top
+    )
+    kept, sent = own_row(both)
+    moved = swap(sent.astype(BF), "x").astype(F32)
+    last_ends = joined(all_ends, ends_x)
+    log_sum = last_ends[0] + jnp.log(last_ends[1])
+    own_log = own_row(own_half(log_sum[None])[0])[0]
+    here_top = own_row(own_half(all_ends[:1])[0])[0]
+    there_top = own_row(own_half(ends_x[:1])[0])[0]
+    own = (kept * jnp.exp(here_top - own_log) + moved * jnp.exp(there_top - own_log)).astype(BF)
     moved = swap(own, "c")
     expected = jnp.concatenate(
         [jnp.where(c == 0, own, moved), jnp.where(c == 0, moved, own)], 1
@@ -815,7 +848,6 @@
     coef = (
         (weight_two.reshape(-1) * width ** (-0.5))[None, :] * jnp.exp(tops[:, 0] - log_sum[None, :])
     ).T
-    table_sums = table_product(raised, outputs_two, coef)
 
     zy = (zn, lax.axis_size("y"))
     table_cut = block_len * 5 // 128 * 16
@@ -845,9 +877,9 @@
         up_a, up_b = pairs_of(up_terms)
         up_a, up_b = halve(up_a, "y", 1), halve(up_b, "x", 2)
     up_bias_part = jnp.sum(pre_grad, axis=0, dtype=F32)
-    second_grad = both_cores(
-        dot_nt(after(pre_grad, up_terms, down_a[1], down_b[1]), up_half)
-    )
+    second_part = dot_nt(after(pre_grad, up_terms, down_a[1], down_b[1]), up_half)
+    table_sums = table_product(raised, after(outputs_two, second_part), coef)
+    second_grad = after(both_cores(second_part), table_sums)
     gain_two_part = jnp.sum(second_grad * normed_two, axis=0)
     bias_two_part = jnp.sum(second_grad, axis=0)
     hidden_one_grad = hidden_two_grad + norm_back(second_grad, gain_two, normed_two, inverse_two)
@@ -962,24 +994,17 @@
         attn_sum = added(attn_terms[0], after(attn_terms[1], token_moved))
     with jax.named_scope("reduce_mlp"):
         mlp_ring = ring_up(ring_next(mlp_sum, after(mlp_ring, token_moved), 2, "z").astype(BF), "z")
-    table_terms = table_add(table_sums, slots_here, token_grad_two)
-    table_terms = after(table_terms, qkv_a[1], qkv_b[1], small_terms[1], mlp_ring)
-    with jax.named_scope("reduce_table"):
-        terms = table_terms.reshape(2, zn, block_len, width)
-        terms_a, terms_b = terms[:, :, :table_cut], terms[:, :, table_cut:]
-        moved_a = swap(terms_a[1], "y")
-        moved_b = ring_up(terms_b[:, zn - 1], "z")
     with jax.named_scope("reduce_rest"):
         rest_sum = jnp.concatenate(
             [
                 jnp.concatenate(
                     [
-                        added(qkv_a[0], after(qkv_a[1], table_terms)),
-                        added(qkv_b[0], after(qkv_b[1], table_terms)),
+                        added(qkv_a[0], after(qkv_a[1], token_grad_two)),
+                        added(qkv_b[0], after(qkv_b[1], token_grad_two)),
                     ],
                     1,
                 ),
-                added(small_terms[0], after(small_terms[1], table_terms))
+                added(small_terms[0], after(small_terms[1], token_grad_two))
                 .reshape(zn, rows_here, 2, -1)
                 .transpose(0, 2, 1, 3)
                 .reshape(zn, 2 * rows_here, -1),
@@ -990,7 +1015,19 @@
             2,
         )
         rest_ring = ring_start(rest_sum, "z")
-    moved_b, rest_ring = lax.optimization_barrier((moved_b, rest_ring))
+    table_terms = table_add(table_sums, slots_here, after(token_grad_two, rest_sum))
+    table_terms = after(table_terms, mlp_ring, rest_ring)
+    with jax.named_scope("reduce_table"):
+        terms = table_terms.reshape(2, zn, block_len, width)
+        terms_a, terms_b = terms[:, :, :table_cut], terms[:, :, table_cut:]
+        early = table_cut // 32 * 16
+        moved_early = swap(terms_a[1, :, :early], "y")
+        moved_late = swap(terms_a[1, :, early:], "y")
+        moved_b = ring_up(terms_b[:, zn - 1], "z")
+    with jax.named_scope("reduce_rest"):
+        rest_own = ring_next(rest_sum, after(rest_ring, table_terms), 1, "z")
+        rest_ring = ring_up(rest_own.astype(BF), "z")
+    moved_b, rest_ring, moved_early = lax.optimization_barrier((moved_b, rest_ring, moved_early))
     for step in range(1, zn):
         with jax.named_scope("reduce_table"):
             total_b = terms_b[:, zn - 1 - step].astype(F32) + moved_b.astype(F32)
@@ -998,19 +1035,27 @@
                 moved_b = ring_up(total_b.astype(BF), "z")
             else:
                 moved_b = swap(total_b[1].astype(BF), "y")
-        with jax.named_scope("reduce_rest"):
-            rest_own = ring_next(rest_sum, rest_ring, step, "z")
-            if step < zn - 1:
-                rest_ring = ring_up(rest_own.astype(BF), "z")
-        with jax.named_scope("reduce_table"):
-            if step == 1:
-                sum_a = added(terms_a[0], moved_a)
+        if step < zn - 1:
+            with jax.named_scope("reduce_rest"):
+                rest_own = ring_next(rest_sum, rest_ring, step + 1, "z")
+                if step < zn - 2:
+                    rest_ring = ring_up(rest_own.astype(BF), "z")
+        if step == zn - 2:
+            with jax.named_scope("reduce_table"):
+                moved_a = jnp.concatenate([moved_early, moved_late], 1)
+                sum_a = added(terms_a[0], after(moved_a, total_b))
                 moving_a = ring_up(sum_a[zn - 1], "z")
-            else:
-                total_a = sum_a[zn - step].astype(F32) + moving_a.astype(F32)
-                moving_a = ring_up(total_a.astype(BF), "z")
-        moved_b, rest_ring, moving_a = lax.optimization_barrier((moved_b, rest_ring, moving_a))
+            moved_b, moving_a = lax.optimization_barrier((moved_b, moving_a))
+        elif step < zn - 2:
+            moved_b, rest_ring, moved_late = lax.optimization_barrier(
+                (moved_b, rest_ring, moved_late)
+            )
     with jax.named_scope("reduce_table"):
+        for step in range(2, zn):
+            total_a = sum_a[zn - step].astype(F32) + moving_a.astype(F32)
+            moving_a = ring_up(total_a.astype(BF), "z")
+            if step == 2:
+                moved_b, moving_a = lax.optimization_barrier((moved_b, moving_a))
         total_b = total_b[0] + moved_b.astype(F32)
         total_a = sum_a[0].astype(F32) + moving_a.astype(F32)
     with jax.named_scope("reduce_mlp"):

time: 692 us -> 656 us (0.948)
  waiting for transfers between devices: 207 us -> 175 us
  other arithmetic: 112 us -> 100 us
    ppermute x4, waiting for transfers between devices: 29.9 us -> 11.3 us  [apart(): return lax.ppermute(value, axis, [(i, i ^ distance) for i in range(n)])]
    ppermute x55 -> x56, waiting for transfers between devices: 75.7 us -> 60.5 us  [swap(): return lax.ppermute(value, axis, SWAP)]
    convert_element_type x7 -> x5, other arithmetic: 12.3 us -> 4.44 us  [the longest x1 2.66 us: both_cores(): return part + swap(part.astype(BF), 'c').astype(F32)]
    unnamed x270 -> x252, local copies, waits for them, and re-layouts: 22.3 us -> 21 us
    ppermute x55 -> x56, starting transfers between devices: 45.4 us -> 44.8 us  [swap(): return lax.ppermute(value, axis, SWAP)]
  transfers between devices with their start and end apart: 80 -> 81, of which waited for: 38 -> 40; matrix products, arithmetic and copies ran while one was open for 29% -> 33% of each run, Pallas kernels for 16% -> 13%
where the time goes in v1:
time: 656 us; the launch traced here: 647 us
  waiting for transfers between devices  175 us (27%)
  Pallas kernels  121 us (18%)
  other arithmetic  100 us (15%)
  local copies, waits for them, and re-layouts  99.8 us (15%)
  matrix products  75.2 us (11%)
  starting transfers between devices  70.1 us (11%)
    ppermute x56, waiting for transfers between devices, swap(): return lax.ppermute(value, axis, SWAP)  60.5 us
    ppermute x12, waiting for transfers between devices, ring_up(): return lax.ppermute(value, axis, [(i, (i + 1) % n) for i in range(n)])  56.3 us
    ppermute x9, waiting for transfers between devices, ring_down(): return lax.ppermute(value, axis, [(i, (i - 1) % n) for i in range(n)])  47 us
    ppermute x56, starting transfers between devices, swap(): return lax.ppermute(value, axis, SWAP)  44.8 us
    pallas_call x1, Pallas kernels, score(): pl.pallas_call(score_body, out_shape=(jax.ShapeDtypeStruct((blocks, rows,...  32.6 us
    dot_general x6, matrix products, dot_nn(): lax.dot_general(left, right, (((1,), (0,)), ((), ())), preferred_element_...  28.9 us
    dot_general x7, matrix products, dot_nt(): lax.dot_general(left, right, (((1,), (1,)), ((), ())), preferred_element_...  26.8 us
    convert_element_type x17, other arithmetic, added(): return (kept.astype(F32) + moved.astype(F32)).astype(BF)  24.1 us
  transfers between devices with their start and end apart: 81, of which 40 were waited for; matrix products, arithmetic and copies ran while one was open for 33% of the time, Pallas kernels for 13%

profile of v1, /device:TPU:0, one launch (start us, length us, event | category | flops | bytes accessed | tf_op | source)
XLA Modules:
  0.0 646.9 jit_solution(16804046780377231242)
XLA Ops:
  4.2 4.7 collective-permute-start.1
  24.9 8.0 %collective-permute-done.6 = bf16[1,64,2688]{2,1,0:T(8,128)(2,1)} collective-permute-done((bf16[1,64,2688]{2,1,0:T(8,128)(2,1)S(1)}, bf16[1,64,2688]{2,1,0:T(8,128)(2,1)}, u32[]{:S(2)}, u32[]{:S(2)}) %collective-permute-start.6) | collective-permute-done | bytes 344096 | tf_op jit(solution)/shard_map/gather_first/ppermute | solution.py:40
  35.2 14.1 %collective-permute-done.2 = bf16[1,496,256]{2,1,0:T(8,128)(2,1)S(1)} collective-permute-done((bf16[1,496,256]{2,1,0:T(8,128)(2,1)S(1)}, bf16[1,496,256]{2,1,0:T(8,128)(2,1)S(1)}, u32[]{:S(2)}, u32[]{:S(2)}) %collective-permute-start.2) | collective-permute-done | bytes 253984 | tf_op jit(solution)/shard_map/gather_table/ppermute | solution.py:40
  62.9 10.5 %collective-permute-done.13 = bf16[2,504,256]{2,1,0:T(8,128)(2,1)} collective-permute-done((bf16[2,504,256]{2,1,0:T(8,128)(2,1)}, bf16[2,504,256]{2,1,0:T(8,128)(2,1)}, u32[]{:S(2)}, u32[]{:S(2)}) %collective-permute-start.13) | collective-permute-done | bytes 516128 | tf_op jit(solution)/shard_map/gather_table/ppermute | solution.py:40
  92.9 7.9 %collective-permute-done.9 = bf16[4,32,2688]{2,1,0:T(8,128)(2,1)S(1)} collective-permute-done((bf16[4,32,2688]{2,1,0:T(8,128)(2,1)S(1)}, bf16[4,32,2688]{2,1,0:T(8,128)(2,1)S(1)}, u32[]{:S(2)}, u32[]{:S(2)}) %collective-permute-start.9) | collective-permute-done | bytes 688160 | tf_op jit(solution)/shard_map/gather_first/ppermute | solution.py:35
  107.0 11.2 %gather_fusion = bf16[2048,256]{1,0:T(8,128)(2,1)} fusion(bf16[8000,256]{1,0:T(8,128)(2,1)} %bitcast.424, s32[2048]{0:T(1024)S(1)} %broadcast_clamp_fusion), kind=kCustom, calls=%fused_computation | custom fusion | bytes 2105344 | tf_op jit(solution)/shard_map/jit(_take)/gather | solution.py:665
  158.1 4.7 collective-permute-done.24
  172.7 4.8 collective-permute-done.25
  181.8 16.4 %attend.1 = (bf16[1024,512]{1,0:T(8,128)(2,1)S(1)}, f32[4,2,1024]{2,1,0:T(2,128)S(1)}) custom-call(s32[4]{0:T(128)S(1)} %get-tuple-element.341.lo_ref, s32[4]{0:T(128)S(1)} %get-tuple-element.340.hi_ref, bf16[1024,512]{1,0:T(8,128)(2,1)S(1)} %fusion.7.q_ref, bf16[1024,512]{1,0:T(8,128)(2,1)S(1)} %get-tuple-element.222.k_ref, ...), custom_call_target="tpu_custom_call" | custom-call | flops 8589934592 | bytes 4194304 | tf_op jit(solution)/shard_map/attend/pallas_call | solution.py:236
  212.0 7.6 %place_blocks.4 = bf16[8,2,2,32,2048]{4,3,2,1,0:T(8,128)(2,1)S(1)} custom-call(s32[32]{0:T(128)S(1)} %pad_add_fusion.1.places_ref, bf16[8,32,2048]{2,1,0:T(8,128)(2,1)S(1)} %pad_maximum_fusion.10.refs_0_, bf16[8,32,2048]{2,1,0:T(8,128)(2,1)S(1)} %copy-done.9, bf16[8,32,2048]{2,1,0:T(8,128)(2,1)S(1)} %pad_maximum_fusion.11.refs_2_, ...), custom_call_target="tpu_custom_call" | custom-call | tf_op jit(solution)/shard_map/place_blocks/pallas_call | solution.py:129
  219.6 4.7 fusion.161
  224.8 9.3 %multiply_convert_fusion.1 = (bf16[1024,2048]{1,0:T(8,128)(2,1)S(1)}, f32[1024,2048]{1,0:T(8,128)}) fusion(f32[2048]{0:T(1024)S(1)} %convert.84, bf16[1024,2048]{1,0:T(8,128)(2,1)S(1)} %bitcast.402, f32[1024,1024]{0,1:T(8,128)S(1)} %get-tuple-element.206, f32[1024]{0:T(1024)S(1)} %reshape.1525, f32[1024]{0:T(1024)S(1)} %reshape.1524, ...), kind=kOutput, calls=%fused_computation.8 | convolution fusion | flops 4312793088 | bytes 20996096 | tf_op jit(solution)/shard_map/dot_general | solution.py:23
  235.8 6.9 %place_blocks.5 = bf16[16,2,64,1024]{3,2,1,0:T(8,128)(2,1)S(1)} custom-call(s32[32]{0:T(128)S(1)} %pad_add_fusion.1.places_ref, bf16[8,64,1024]{2,1,0:T(8,128)(2,1)S(1)} %pad_maximum_fusion.12.refs_0_, bf16[8,64,1024]{2,1,0:T(8,128)(2,1)S(1)} %collective-permute-done.31.refs_1_, bf16[8,64,1024]{2,1,0:T(8,128)(2,1)S(1)} %pad_maximum_fusion.13.refs_2_, ...), custom_call_target="tpu_custom_call" | custom-call | tf_op jit(solution)/shard_map/place_blocks/pallas_call | solution.py:129
  242.7 7.0 %fusion.188 = (bf16[1024,1024]{0,1:T(8,128)(2,1)}, f32[1024,1024]{0,1:T(8,128)}) fusion(bf16[1024,2048]{1,0:T(8,128)(2,1)S(1)} %get-tuple-element.324, bf16[2048,1024]{1,0:T(8,128)(2,1)S(1)} %bitcast.404), kind=kOutput, calls=%fused_computation.599 | convolution fusion | flops 4296015872 | bytes 14680064 | tf_op jit(solution)/shard_map/dot_general | solution.py:23
  256.5 5.4 add_convert_fusion.1
  265.1 7.6 %collective-permute-done.34 = bf16[512,256]{1,0:T(8,128)(2,1)S(1)} collective-permute-done((bf16[512,256]{1,0:T(8,128)(2,1)S(1)}, bf16[512,256]{1,0:T(8,128)(2,1)S(1)}, u32[]{:S(2)}, u32[]{:S(2)}) %collective-permute-start.34) | collective-permute-done | bytes 262176 | tf_op jit(solution)/shard_map/ppermute | solution.py:35
  277.6 32.6 %score.1 = (bf16[8,1000,2048]{2,1,0:T(8,128)(2,1)}, f32[8,1,2048]{2,1,0:T(1,128)S(1)}, f32[256,2048]{1,0:T(8,128)S(1)}, f32[1,2048]{1,0:T(1,128)S(1)}) custom-call(f32[1,2048]{1,0:T(1,128)S(1)} %fusion.6.norm_ref, bf16[2048,256]{1,0:T(8,128)(2,1)S(1)} %bitcast.400, bf16[8,1000,256]{2,1,0:T(8,128)(2,1)} %pad_maximum_fusion.table_ref, ...), custom_call_target="tpu_custom_call" | custom-call | flops 16777216000 | bytes 32768000 | tf_op jit(solution)/shard_map/score/pallas_call | solution.py:418
  324.1 5.5 collective-permute-done.42
  336.7 5.0 convolution_convert_fusion.2
  348.1 7.9 %fusion.190 = (bf16[2048]{0:T(1024)(128)(2,1)S(1)}, bf16[1024,2048]{1,0:T(8,128)(2,1)S(1)}) fusion(f32[1024,2048]{1,0:T(8,128)S(1)} %bitcast.513, f32[2048]{0:T(1024)S(1)} %convert.84, bf16[1024,1024]{0,1:T(8,128)(2,1)S(1)} %get-tuple-element.127, bf16[2048,1024]{1,0:T(8,128)(2,1)S(1)} %bitcast.405), kind=kOutput, calls=%fused_computation.601 | convolution fusion | flops 4324325376 | bytes 18886656 | tf_op jit(solution)/shard_map/dot_general | solution.py:27
  356.0 5.2 convolution_convert_fusion.1
  372.8 6.3 fusion.194
  379.1 5.3 copy.173
  399.0 18.7 %table_product.1.sum_ref = f32[8,1000,256]{2,1,0:T(8,128)} custom-call(bf16[8,1000,2048]{2,1,0:T(8,128)(2,1)} %get-tuple-element.125.raised_ref, bf16[2048,256]{1,0:T(8,128)(2,1)S(1)} %bitcast.401, f32[2048,8]{1,0:T(8,128)S(1)} %fusion.41.coef_ref), custom_call_target="tpu_custom_call" | custom-call | flops 8388608000 | bytes 32768000 | tf_op jit(solution)/shard_map/table_product/pallas_call | solution.py:461
  438.7 22.7 %attend_back.1 = (bf16[1024,512]{1,0:T(8,128)(2,1)S(1)}, bf16[1024,512]{1,0:T(8,128)(2,1)S(1)}, bf16[1024,512]{1,0:T(8,128)(2,1)S(1)}) custom-call(s32[4]{0:T(128)S(1)} %get-tuple-element.341.lo_ref, s32[4]{0:T(128)S(1)} %copy-done.26, bf16[1024,512]{1,0:T(8,128)(2,1)S(1)} %copy-done.7, bf16[1024,512]{1,0:T(8,128)(2,1)S(1)} %copy-done.15, ...), custom_call_target="tpu_custom_call" | custom-call | flops 17179869184 | bytes 8388608 | tf_op jit(solution)/shard_map/attend_back/pallas_call | solution.py:329
  537.9 11.4 %table_add.1 = bf16[8,1000,256]{2,1,0:T(8,128)(2,1)S(1)} custom-call(f32[8,1000,256]{2,1,0:T(8,128)} %table_product.1.sum_ref, s32[1,2048]{1,0:T(1,128)S(1)} %copy-done.24, bf16[2048,256]{1,0:T(8,128)(2,1)S(1)} %bitcast.417), custom_call_target="tpu_custom_call" | custom-call | flops 8388608000 | bytes 12288000 | tf_op jit(solution)/shard_map/table_add/pallas_call | solution.py:492
  549.4 4.7 collective-permute-done.67
  557.5 8.9 %collective-permute-done.69 = bf16[64,2432]{1,0:T(8,128)(2,1)S(1)} collective-permute-done((bf16[64,2432]{1,0:T(8,128)(2,1)S(1)}, bf16[64,2432]{1,0:T(8,128)(2,1)S(1)}, u32[]{:S(2)}, u32[]{:S(2)}) %collective-permute-start.69) | collective-permute-done | bytes 311328 | tf_op jit(solution)/shard_map/reduce_rest/ppermute | solution.py:45
  566.4 6.6 %collective-permute-done.68 = bf16[2,376,256]{2,1,0:T(8,128)(2,1)S(1)} collective-permute-done((bf16[2,376,256]{2,1,0:T(8,128)(2,1)S(1)}, bf16[2,376,256]{2,1,0:T(8,128)(2,1)S(1)}, u32[]{:S(2)}, u32[]{:S(2)}) %collective-permute-start.68) | collective-permute-done | bytes 385056 | tf_op jit(solution)/shard_map/reduce_table/ppermute | solution.py:45
  586.4 5.6 collective-permute-done.71
  601.9 18.6 %collective-permute-done.75 = bf16[624,256]{1,0:T(8,128)(2,1)S(1)} collective-permute-done((bf16[624,256]{1,0:T(8,128)(2,1)S(1)}, bf16[624,256]{1,0:T(8,128)(2,1)S(1)}, u32[]{:S(2)}, u32[]{:S(2)}) %collective-permute-start.75) | collective-permute-done | bytes 319520 | tf_op jit(solution)/shard_map/reduce_table/ppermute | solution.py:45
  638.9 5.1 collective-permute-done.78
  (680 shorter events, 340.3 us)
Async XLA Ops:
  22.5 29.1 %collective-permute-start.12 = (bf16[2,504,256]{2,1,0:T(8,128)(2,1)S(1)}, bf16[2,504,256]{2,1,0:T(8,128)(2,1)}, u32[]{:S(2)}, u32[]{:S(2)}) collective-permute-start(bf16[2,504,256]{2,1,0:T(8,128)(2,1)S(1)} %get-tuple-element.258), channel_id=1, source_target_pairs={{0,24},{8,0},{16,8},{24,16},{1,25},{9,1},{17,9},{25,17},{2,26},{10... | collective-permute-start | bytes 1548296 | tf_op jit(solution)/shard_map/gather_table/ppermute | solution.py:40
  23.2 26.2 %collective-permute-start.2 = (bf16[1,496,256]{2,1,0:T(8,128)(2,1)S(1)}, bf16[1,496,256]{2,1,0:T(8,128)(2,1)S(1)}, u32[]{:S(2)}, u32[]{:S(2)}) collective-permute-start(bf16[1,496,256]{2,1,0:T(8,128)(2,1)S(1)} %collective-permute-done.1), channel_id=1, source_target_pairs={{0,24},{8,0},{16,8},{24,16},{1,25},{9,1},{17,9},{25,17},{2,26},{10... | collective-permute-start | bytes 761864 | tf_op jit(solution)/shard_map/gather_table/ppermute | solution.py:40
  33.0 23.9 %collective-permute-start.7 = (bf16[1,64,2688]{2,1,0:T(8,128)(2,1)}, bf16[1,64,2688]{2,1,0:T(8,128)(2,1)}, u32[]{:S(2)}, u32[]{:S(2)}) collective-permute-start(bf16[1,64,2688]{2,1,0:T(8,128)(2,1)} %collective-permute-done.6), channel_id=1, source_target_pairs={{0,24},{8,0},{16,8},{24,16},{1,25},{9,1},{17,9},{25,17},{2,26},{10... | collective-permute-start | bytes 1032200 | tf_op jit(solution)/shard_map/gather_first/ppermute | solution.py:40
  56.9 23.8 %collective-permute-start.8 = (bf16[1,64,2688]{2,1,0:T(8,128)(2,1)}, bf16[1,64,2688]{2,1,0:T(8,128)(2,1)S(1)}, u32[]{:S(2)}, u32[]{:S(2)}) collective-permute-start(bf16[1,64,2688]{2,1,0:T(8,128)(2,1)} %collective-permute-done.7), channel_id=1, source_target_pairs={{0,24},{8,0},{16,8},{24,16},{1,25},{9,1},{17,9},{25,17},{2,26},{10... | collective-permute-start | bytes 1032200 | tf_op jit(solution)/shard_map/gather_first/ppermute | solution.py:40
  62.3 25.5 %collective-permute-start.4 = (bf16[4,496,256]{2,1,0:T(8,128)(2,1)S(1)}, bf16[4,496,256]{2,1,0:T(8,128)(2,1)S(1)}, u32[]{:S(2)}, u32[]{:S(2)}) collective-permute-start(bf16[4,496,256]{2,1,0:T(8,128)(2,1)S(1)} %pad_maximum_fusion.17), channel_id=1, source_target_pairs={{0,4},{4,0},{1,5},{5,1},{2,6},{6,2},{3,7},{7,3},{8,12},{12,8},{9,1... | collective-permute-start | bytes 3047432 | tf_op jit(solution)/shard_map/gather_table/ppermute | solution.py:35
  100.9 30.6 %collective-permute-start.17 = (bf16[8,32,2688]{2,1,0:T(8,128)(2,1)S(1)}, bf16[8,32,2688]{2,1,0:T(8,128)(2,1)}, u32[]{:S(2)}, u32[]{:S(2)}) collective-permute-start(bf16[8,32,2688]{2,1,0:T(8,128)(2,1)S(1)} %pad_maximum_fusion.5.refs_0_), channel_id=1, source_target_pairs={{0,1},{1,0},{2,3},{3,2},{4,5},{5,4},{6,7},{7,6},{8,9},{9,8},{10,11... | collective-permute-start | bytes 4128776 | tf_op jit(solution)/shard_map/gather_first/ppermute | solution.py:35
  102.6 30.3 %collective-permute-start.18 = (bf16[8,32,2688]{2,1,0:T(8,128)(2,1)S(1)}, bf16[8,32,2688]{2,1,0:T(8,128)(2,1)}, u32[]{:S(2)}, u32[]{:S(2)}) collective-permute-start(bf16[8,32,2688]{2,1,0:T(8,128)(2,1)S(1)} %pad_maximum_fusion.6.refs_2_), channel_id=1, source_target_pairs={{0,4},{4,0},{1,5},{5,1},{2,6},{6,2},{3,7},{7,3},{8,12},{12,8},{9,1... | collective-permute-start | bytes 4128776 | tf_op jit(solution)/shard_map/gather_first/ppermute | solution.py:35
  104.7 23.7 %collective-permute-start.19 = (bf16[2,64,2048]{2,1,0:T(8,128)(2,1)}, bf16[2,64,2048]{2,1,0:T(8,128)(2,1)}, u32[]{:S(2)}, u32[]{:S(2)}) collective-permute-start(bf16[2,64,2048]{2,1,0:T(8,128)(2,1)} %pad_maximum_fusion.18), channel_id=1, source_target_pairs={{0,16},{8,24},{16,0},{24,8},{1,17},{9,25},{17,1},{25,9},{2,18},{10... | collective-permute-start | bytes 1572872 | tf_op jit(solution)/shard_map/gather_up/ppermute | solution.py:75
  151.3 26.2 %collective-permute-start.25 = (bf16[2,128,1024]{2,1,0:T(8,128)(2,1)}, bf16[2,128,1024]{2,1,0:T(8,128)(2,1)S(1)}, u32[]{:S(2)}, u32[]{:S(2)}) collective-permute-start(bf16[2,128,1024]{2,1,0:T(8,128)(2,1)} %pad_maximum_fusion.19), channel_id=1, source_target_pairs={{0,16},{8,24},{16,0},{24,8},{1,17},{9,25},{17,1},{25,9},{2,18},{10... | collective-permute-start | bytes 1572872 | tf_op jit(solution)/shard_map/gather_down/ppermute | solution.py:75
  165.6 37.0 %collective-permute-start.26 = (bf16[8,32,2048]{2,1,0:T(8,128)(2,1)S(1)}, bf16[8,32,2048]{2,1,0:T(8,128)(2,1)S(1)}, u32[]{:S(2)}, u32[]{:S(2)}) collective-permute-start(bf16[8,32,2048]{2,1,0:T(8,128)(2,1)S(1)} %pad_maximum_fusion.10.refs_0_), channel_id=1, source_target_pairs={{0,1},{1,0},{2,3},{3,2},{4,5},{5,4},{6,7},{7,6},{8,9},{9,8},{10,11... | collective-permute-start | bytes 3145736 | tf_op jit(solution)/shard_map/gather_up/ppermute | solution.py:35
  167.2 35.4 %collective-permute-start.27 = (bf16[8,32,2048]{2,1,0:T(8,128)(2,1)S(1)}, bf16[8,32,2048]{2,1,0:T(8,128)(2,1)S(1)}, u32[]{:S(2)}, u32[]{:S(2)}) collective-permute-start(bf16[8,32,2048]{2,1,0:T(8,128)(2,1)S(1)} %pad_maximum_fusion.11.refs_2_), channel_id=1, source_target_pairs={{0,4},{4,0},{1,5},{5,1},{2,6},{6,2},{3,7},{7,3},{8,12},{12,8},{9,1... | collective-permute-start | bytes 3145736 | tf_op jit(solution)/shard_map/gather_up/ppermute | solution.py:35
  208.5 27.3 %collective-permute-start.31 = (bf16[8,64,1024]{2,1,0:T(8,128)(2,1)S(1)}, bf16[8,64,1024]{2,1,0:T(8,128)(2,1)S(1)}, u32[]{:S(2)}, u32[]{:S(2)}) collective-permute-start(bf16[8,64,1024]{2,1,0:T(8,128)(2,1)S(1)} %pad_maximum_fusion.12.refs_0_), channel_id=1, source_target_pairs={{0,1},{1,0},{2,3},{3,2},{4,5},{5,4},{6,7},{7,6},{8,9},{9,8},{10,11... | collective-permute-start | bytes 3145736 | tf_op jit(solution)/shard_map/gather_down/ppermute | solution.py:35
  210.5 25.3 %collective-permute-start.32 = (bf16[8,64,1024]{2,1,0:T(8,128)(2,1)S(1)}, bf16[8,64,1024]{2,1,0:T(8,128)(2,1)S(1)}, u32[]{:S(2)}, u32[]{:S(2)}) collective-permute-start(bf16[8,64,1024]{2,1,0:T(8,128)(2,1)S(1)} %pad_maximum_fusion.13.refs_2_), channel_id=1, source_target_pairs={{0,4},{4,0},{1,5},{5,1},{2,6},{6,2},{3,7},{7,3},{8,12},{12,8},{9,1... | collective-permute-start | bytes 3145736 | tf_op jit(solution)/shard_map/gather_down/ppermute | solution.py:35
  343.8 25.4 %collective-permute-start.45 = (bf16[4,2,64,1024]{3,2,0,1:T(8,128)(2,1)S(1)}, bf16[4,2,64,1024]{3,2,0,1:T(8,128)(2,1)}, u32[]{:S(2)}, u32[]{:S(2)}) collective-permute-start(bf16[4,2,64,1024]{3,2,0,1:T(8,128)(2,1)S(1)} %bitcast.442), channel_id=1, source_target_pairs={{0,4},{4,0},{1,5},{5,1},{2,6},{6,2},{3,7},{7,3},{8,12},{12,8},{9,1... | collective-permute-start | bytes 3145736 | tf_op jit(solution)/shard_map/reduce_down/ppermute | solution.py:35
  346.6 26.2 %collective-permute-start.44 = (bf16[4,2,64,1024]{3,2,0,1:T(8,128)(2,1)S(1)}, bf16[4,2,64,1024]{3,2,0,1:T(8,128)(2,1)}, u32[]{:S(2)}, u32[]{:S(2)}) collective-permute-start(bf16[4,2,64,1024]{3,2,0,1:T(8,128)(2,1)S(1)} %bitcast.443), channel_id=1, source_target_pairs={{0,1},{1,0},{2,3},{3,2},{4,5},{5,4},{6,7},{7,6},{8,9},{9,8},{10,11... | collective-permute-start | bytes 3145736 | tf_op jit(solution)/shard_map/reduce_down/ppermute | solution.py:35
  365.2 60.4 %collective-permute-start.48 = (bf16[4,2,32,2048]{3,2,0,1:T(8,128)(2,1)}, bf16[4,2,32,2048]{3,2,0,1:T(8,128)(2,1)}, u32[]{:S(2)}, u32[]{:S(2)}) collective-permute-start(bf16[4,2,32,2048]{3,2,0,1:T(8,128)(2,1)} %bitcast.390), channel_id=1, source_target_pairs={{0,1},{1,0},{2,3},{3,2},{4,5},{5,4},{6,7},{7,6},{8,9},{9,8},{10,11... | collective-permute-start | bytes 3145736 | tf_op jit(solution)/shard_map/reduce_up/ppermute | solution.py:35
  387.1 30.6 %collective-permute-start.46 = (bf16[1024,1024]{0,1:T(8,128)(2,1)S(1)}, bf16[1024,1024]{0,1:T(8,128)(2,1)S(1)}, u32[]{:S(2)}, u32[]{:S(2)}) collective-permute-start(bf16[1024,1024]{0,1:T(8,128)(2,1)S(1)} %convert_element_type.616), channel_id=1, source_target_pairs={{0,2},{2,0},{1,3},{3,1},{4,6},{6,4},{5,7},{7,5},{8,10},{10,8},{9,1... | collective-permute-start | bytes 6291464 | tf_op jit(solution)/shard_map/ppermute | solution.py:35
  389.4 36.2 %collective-permute-start.47 = (bf16[4,2,32,2048]{3,2,0,1:T(8,128)(2,1)}, bf16[4,2,32,2048]{3,2,0,1:T(8,128)(2,1)}, u32[]{:S(2)}, u32[]{:S(2)}) collective-permute-start(bf16[4,2,32,2048]{3,2,0,1:T(8,128)(2,1)} %bitcast.391), channel_id=1, source_target_pairs={{0,4},{4,0},{1,5},{5,1},{2,6},{6,2},{3,7},{7,3},{8,12},{12,8},{9,1... | collective-permute-start | bytes 3145736 | tf_op jit(solution)/shard_map/reduce_up/ppermute | solution.py:35
  393.5 69.0 %collective-permute-start.52 = (bf16[4,64,1024]{2,1,0:T(8,128)(2,1)}, bf16[4,64,1024]{2,1,0:T(8,128)(2,1)}, u32[]{:S(2)}, u32[]{:S(2)}) collective-permute-start(bf16[4,64,1024]{2,1,0:T(8,128)(2,1)} %dynamic-slice_bitcast_fusion.1), channel_id=1, source_target_pairs={{0,1},{1,0},{2,3},{3,2},{4,5},{5,4},{6,7},{7,6},{8,9},{9,8},{10,11... | collective-permute-start | bytes 1572872 | tf_op jit(solution)/shard_map/reduce_down/ppermute | solution.py:35
  397.5 65.0 %collective-permute-start.51 = (bf16[4,64,1024]{2,1,0:T(8,128)(2,1)}, bf16[4,64,1024]{2,1,0:T(8,128)(2,1)}, u32[]{:S(2)}, u32[]{:S(2)}) collective-permute-start(bf16[4,64,1024]{2,1,0:T(8,128)(2,1)} %dynamic-slice_bitcast_fusion.2), channel_id=1, source_target_pairs={{0,4},{4,0},{1,5},{5,1},{2,6},{6,2},{3,7},{7,3},{8,12},{12,8},{9,1... | collective-permute-start | bytes 1572872 | tf_op jit(solution)/shard_map/reduce_down/ppermute | solution.py:35
  436.0 26.6 %collective-permute-start.50 = (bf16[4,32,2048]{2,1,0:T(8,128)(2,1)}, bf16[4,32,2048]{2,1,0:T(8,128)(2,1)}, u32[]{:S(2)}, u32[]{:S(2)}) collective-permute-start(bf16[4,32,2048]{2,1,0:T(8,128)(2,1)} %dynamic-slice_bitcast_fusion.3), channel_id=1, source_target_pairs={{0,4},{4,0},{1,5},{5,1},{2,6},{6,2},{3,7},{7,3},{8,12},{12,8},{9,1... | collective-permute-start | bytes 1572872 | tf_op jit(solution)/shard_map/reduce_up/ppermute | solution.py:35
  436.6 26.0 %collective-permute-start.49 = (bf16[4,32,2048]{2,1,0:T(8,128)(2,1)}, bf16[4,32,2048]{2,1,0:T(8,128)(2,1)}, u32[]{:S(2)}, u32[]{:S(2)}) collective-permute-start(bf16[4,32,2048]{2,1,0:T(8,128)(2,1)} %dynamic-slice_bitcast_fusion.4), channel_id=1, source_target_pairs={{0,1},{1,0},{2,3},{3,2},{4,5},{5,4},{6,7},{7,6},{8,9},{9,8},{10,11... | collective-permute-start | bytes 1572872 | tf_op jit(solution)/shard_map/reduce_up/ppermute | solution.py:35
  437.2 25.4 %collective-permute-start.53 = (bf16[4,2,32,1024]{3,2,0,1:T(8,128)(2,1)}, bf16[4,2,32,1024]{3,2,0,1:T(8,128)(2,1)}, u32[]{:S(2)}, u32[]{:S(2)}) collective-permute-start(bf16[4,2,32,1024]{3,2,0,1:T(8,128)(2,1)} %bitcast.396), channel_id=1, source_target_pairs={{0,4},{4,0},{1,5},{5,1},{2,6},{6,2},{3,7},{7,3},{8,12},{12,8},{9,1... | collective-permute-start | bytes 1572872 | tf_op jit(solution)/shard_map/reduce_attn/ppermute | solution.py:35
  479.1 29.2 %collective-permute-start.63 = (bf16[4,32,1024]{2,1,0:T(8,128)(2,1)}, bf16[4,32,1024]{2,1,0:T(8,128)(2,1)}, u32[]{:S(2)}, u32[]{:S(2)}) collective-permute-start(bf16[4,32,1024]{2,1,0:T(8,128)(2,1)} %dynamic-slice_bitcast_fusion.11), channel_id=1, source_target_pairs={{0,1},{1,0},{2,3},{3,2},{4,5},{5,4},{6,7},{7,6},{8,9},{9,8},{10,11... | collective-permute-start | bytes 786440 | tf_op jit(solution)/shard_map/reduce_attn/ppermute | solution.py:35
  481.4 24.9 %collective-permute-start.64 = (bf16[64,4096]{1,0:T(8,128)(2,1)}, bf16[64,4096]{1,0:T(8,128)(2,1)}, u32[]{:S(2)}, u32[]{:S(2)}) collective-permute-start(bf16[64,4096]{1,0:T(8,128)(2,1)} %dynamic-slice_bitcast_fusion), channel_id=1, source_target_pairs={{0,8},{8,16},{16,24},{24,0},{1,9},{9,17},{17,25},{25,1},{2,10},{10... | collective-permute-start | bytes 1572872 | tf_op jit(solution)/shard_map/reduce_mlp/ppermute | solution.py:45
  484.0 32.4 %collective-permute-start.57 = (bf16[4,2,32,1536]{3,2,0,1:T(8,128)(2,1)}, bf16[4,2,32,1536]{3,2,0,1:T(8,128)(2,1)}, u32[]{:S(2)}, u32[]{:S(2)}) collective-permute-start(bf16[4,2,32,1536]{3,2,0,1:T(8,128)(2,1)} %bitcast.395), channel_id=1, source_target_pairs={{0,4},{4,0},{1,5},{5,1},{2,6},{6,2},{3,7},{7,3},{8,12},{12,8},{9,1... | collective-permute-start | bytes 2359304 | tf_op jit(solution)/shard_map/reduce_qkv/ppermute | solution.py:35
  487.8 31.3 %collective-permute-start.59 = (bf16[4,2,32,1536]{3,2,0,1:T(8,128)(2,1)}, bf16[4,2,32,1536]{3,2,0,1:T(8,128)(2,1)}, u32[]{:S(2)}, u32[]{:S(2)}) collective-permute-start(bf16[4,2,32,1536]{3,2,0,1:T(8,128)(2,1)} %bitcast.394), channel_id=1, source_target_pairs={{0,1},{1,0},{2,3},{3,2},{4,5},{5,4},{6,7},{7,6},{8,9},{9,8},{10,11... | collective-permute-start | bytes 2359304 | tf_op jit(solution)/shard_map/reduce_qkv/ppermute | solution.py:35
  497.9 25.0 %collective-permute-start.61 = (bf16[4,2,32,768]{3,2,1,0:T(8,128)(2,1)}, bf16[4,2,32,768]{3,2,1,0:T(8,128)(2,1)}, u32[]{:S(2)}, u32[]{:S(2)}) collective-permute-start(bf16[4,2,32,768]{3,2,1,0:T(8,128)(2,1)} %dynamic-slice_bitcast_fusion.6), channel_id=1, source_target_pairs={{0,4},{4,0},{1,5},{5,1},{2,6},{6,2},{3,7},{7,3},{8,12},{12,8},{9,1... | collective-permute-start | bytes 1179656 | tf_op jit(solution)/shard_map/reduce_small/ppermute | solution.py:35
  531.3 22.8 %collective-permute-start.66 = (bf16[64,4096]{1,0:T(8,128)(2,1)}, bf16[64,4096]{1,0:T(8,128)(2,1)S(1)}, u32[]{:S(2)}, u32[]{:S(2)}) collective-permute-start(bf16[64,4096]{1,0:T(8,128)(2,1)} %fusion.34), channel_id=1, source_target_pairs={{0,8},{8,16},{16,24},{24,0},{1,9},{9,17},{17,25},{25,1},{2,10},{10... | collective-permute-start | bytes 1572872 | tf_op jit(solution)/shard_map/reduce_mlp/ppermute | solution.py:45
  557.1 22.1 %collective-permute-start.80 = (f32[32,2048]{1,0:T(8,128)}, f32[32,2048]{1,0:T(8,128)}, u32[]{:S(2)}, u32[]{:S(2)}) collective-permute-start(f32[32,2048]{1,0:T(8,128)} %get-tuple-element.254), channel_id=1, source_target_pairs={{0,2},{2,0},{1,3},{3,1},{4,6},{6,4},{5,7},{7,5},{8,10},{10,8},{9,1... | collective-permute-start | bytes 786440 | tf_op jit(solution)/shard_map/ppermute | solution.py:35
  557.2 26.7 %collective-permute-start.73 = (bf16[4,320,256]{2,1,0:T(8,128)(2,1)S(1)}, bf16[4,320,256]{2,1,0:T(8,128)(2,1)S(1)}, u32[]{:S(2)}, u32[]{:S(2)}) collective-permute-start(bf16[4,320,256]{2,1,0:T(8,128)(2,1)S(1)} %slice_bitcast_fusion.1), channel_id=1, source_target_pairs={{0,4},{4,0},{1,5},{5,1},{2,6},{6,2},{3,7},{7,3},{8,12},{12,8},{9,1... | collective-permute-start | bytes 1966088 | tf_op jit(solution)/shard_map/reduce_table/ppermute | solution.py:35
  599.4 24.8 %collective-permute-start.79 = (f32[32,1536]{1,0:T(8,128)}, f32[32,1536]{1,0:T(8,128)}, u32[]{:S(2)}, u32[]{:S(2)}) collective-permute-start(f32[32,1536]{1,0:T(8,128)} %get-tuple-element.260), channel_id=1, source_target_pairs={{0,2},{2,0},{1,3},{3,1},{4,6},{6,4},{5,7},{7,5},{8,10},{10,8},{9,1... | collective-permute-start | bytes 589832 | tf_op jit(solution)/shard_map/ppermute | solution.py:35
  (163 other events, 1843.5 us)

commit v2 on v1

--- a/solution.py
+++ b/solution.py
@@ -104,39 +104,23 @@
 
 def place_blocks(places, halves, outs):
     flat = halves[0] + halves[1]
-    count = sum(piece.shape[0] for piece in flat) * len(outs)
 
     def body(places_ref, *refs):
-        ins, results, sems = refs[: len(flat)], refs[len(flat) : -1], refs[-1]
-        copies, block = [], 0
+        ins, results, block = refs[: len(flat)], refs[len(flat) :], 0
         for number, piece in enumerate(ins):
             for k in range(piece.shape[0]):
                 p, h = places_ref[block], number // len(halves[0])
                 block += 1
                 for (low, high, _, index), result in zip(outs, results):
-                    copies.append(
-                        pltpu.make_async_copy(
-                            piece.at[k, :, low:high],
-                            result.at[index(p, h)],
-                            sems.at[len(copies)],
-                        )
-                    )
-        for copy in copies:
-            copy.start()
-        for copy in copies:
-            copy.wait()
+                    result[index(p, h)] = piece[k, :, low:high]
 
     return pl.pallas_call(
         body,
         out_shape=tuple(jax.ShapeDtypeStruct(shape, BF) for _, _, shape, _ in outs),
-        grid=(1,),
         in_specs=[pl.BlockSpec(memory_space=pltpu.SMEM)]
-        + [pl.BlockSpec(memory_space=pl.ANY)] * len(flat),
-        out_specs=tuple(
-            pl.BlockSpec(shape, lambda i, n=len(shape): (0,) * n) for _, _, shape, _ in outs
-        ),
-        scratch_shapes=[pltpu.SemaphoreType.DMA((count,))],
-        compiler_params=pltpu.CompilerParams(vmem_limit_bytes=24 * MIB),
+        + [pl.BlockSpec(memory_space=pltpu.VMEM)] * len(flat),
+        out_specs=tuple(pl.BlockSpec(memory_space=pltpu.VMEM) for _ in outs),
+        compiler_params=pltpu.CompilerParams(vmem_limit_bytes=32 * MIB),
         name="place_blocks",
     )(places, *flat)
 
@@ -551,7 +535,8 @@
     output_proj,
 ):
     z, y, c, x = (lax.axis_index(a) for a in ("z", "y", "c", "x"))
-    groups = lax.axis_size("z") * lax.axis_size("y")
+    zn = lax.axis_size("z")
+    groups = zn * lax.axis_size("y")
     length = token_ids.shape[1]
     half = length // 2
     block_len, width = embed_table.shape
@@ -634,13 +619,26 @@
 
     cut = block_len // 32 * 16
     with jax.named_scope("gather_table"):
-        table_a = ring_blocks(embed_table[None, :cut], "z")
-        table_b = ring_blocks(joined_swap(embed_table[None, cut:], "y"), "z")
+        table_a = [embed_table[None, :cut]]
+        table_a.append(ring_down(table_a[-1], "z"))
+        table_b = [joined_swap(embed_table[None, cut:], "y")]
+        table_b.append(ring_down(table_b[-1], "z"))
+    with jax.named_scope("gather_first"):
+        first_z = [first_shard[None]]
+        first_z.append(ring_down(first_z[-1], "z"))
+    with jax.named_scope("gather_table"):
+        for _ in range(2, zn):
+            table_a.append(ring_down(table_a[-1], "z"))
+    for step in range(2, zn):
+        with jax.named_scope("gather_first"):
+            first_z.append(ring_down(after(first_z[-1], table_a[step - 1]), "z"))
+        with jax.named_scope("gather_table"):
+            table_b.append(ring_down(after(table_b[-1], table_a[-1]), "z"))
+    with jax.named_scope("gather_table"):
         table_z = table_b[-1]
         table_a = joined_swap(jnp.concatenate(table_a, 0), "y")
         table_b = jnp.stack(table_b, 1).reshape(groups, block_len - cut, width)
     with jax.named_scope("gather_first"):
-        first_z = ring_blocks(first_shard[None], "z")
         first_held = over_one(jnp.concatenate(first_z, 0))
         first_pieces = over_other(first_held)
     with jax.named_scope("gather_up"):
@@ -659,7 +657,6 @@
     home = {"z": owner // 8, "y": owner // 4 % 2}
     mine = owner % 4 == c * 2 + x
     table_rows = jnp.concatenate([after(table_a, *first_held, up_moved), table_b], axis=1)
-    zn = lax.axis_size("z")
     relative_y, relative_z = (home["y"] - y) % 2, (home["z"] - z) % zn
     slot = (relative_y * zn + relative_z) * block_len + within
     found = jnp.take(
@@ -956,8 +953,12 @@
     with jax.named_scope("reduce_mlp"):
         mlp_ring = ring_up(ring_next(mlp_sum, after(mlp_ring, token_own), 1, "z").astype(BF), "z")
     with jax.named_scope("token_pair"):
-        token_other = ordered(token_moved, swap(token_moved, "c"), c, 0).reshape(length, width)
-        token_grad_two = ordered(token_grad, token_other, x, 0).reshape(2 * length, width)
+        token_grad_two = jnp.concatenate([token_grad, token_moved, swap(token_moved, "c")], 0)
+        slots_two = slots_here.reshape(2, length)
+        other_slots = pick(slots_two, 1 - x, 0).reshape(2, half)
+        token_slots = jnp.concatenate(
+            [pick(slots_two, x, 0), pick(other_slots, c, 0), pick(other_slots, 1 - c, 0)]
+        )[None, :]
     with jax.named_scope("reduce_qkv"):
         qkv_a = halve(added(qkv_a[0], after(qkv_a[1], token_moved)), "x", 1)
         qkv_b = halve(added(qkv_b[0], after(qkv_b[1], token_moved)), "y", 1)
@@ -1015,7 +1016,7 @@
             2,
         )
         rest_ring = ring_start(rest_sum, "z")
-    table_terms = table_add(table_sums, slots_here, after(token_grad_two, rest_sum))
+    table_terms = table_add(table_sums, token_slots, after(token_grad_two, rest_sum))
     table_terms = after(table_terms, mlp_ring, rest_ring)
     with jax.named_scope("reduce_table"):
         terms = table_terms.reshape(2, zn, block_len, width)

time: 656 us -> 650 us (level)
  waiting for transfers between devices: 175 us -> 187 us
  other arithmetic: 100 us -> 91.8 us
    ppermute x56, waiting for transfers between devices: 60.5 us -> 82.8 us  [swap(): return lax.ppermute(value, axis, SWAP)]
    pallas_call x3, Pallas kernels: 18.9 us -> 3.78 us  [place_blocks(): pl.pallas_call(body, out_shape=tuple((jax.ShapeDtypeStruct(shape, BF) for...]
    pallas_call x1, Pallas kernels: 16.4 us -> 26.1 us  [attend(): pl.pallas_call(attend_body, out_shape=(jax.ShapeDtypeStruct((length, widt...]
    unnamed x252 -> x260, local copies, waits for them, and re-layouts: 21 us -> 28.5 us
    dynamic_slice x15 -> x17, local copies, waits for them, and re-layouts: 14.7 us -> 14.6 us  [pick(): return lax.dynamic_index_in_dim(value, index, axis, keepdims=False)]
  transfers between devices with their start and end apart: 81 -> 81, of which waited for: 40 -> 38; matrix products, arithmetic and copies ran while one was open for 33% -> 30% of each run, Pallas kernels for 13% -> 13%
where the time goes in v2:
time: 650 us; the launch traced here: 642 us
  waiting for transfers between devices  187 us (29%)
  Pallas kernels  115 us (18%)
  local copies, waits for them, and re-layouts  102 us (16%)
  other arithmetic  91.8 us (14%)
  matrix products  73.8 us (11%)
  starting transfers between devices  65.8 us (10%)
    ppermute x56, waiting for transfers between devices, swap(): return lax.ppermute(value, axis, SWAP)  82.8 us
    ppermute x12, waiting for transfers between devices, ring_up(): return lax.ppermute(value, axis, [(i, (i + 1) % n) for i in range(n)])  53.7 us
    ppermute x56, starting transfers between devices, swap(): return lax.ppermute(value, axis, SWAP)  42.6 us
    ppermute x9, waiting for transfers between devices, ring_down(): return lax.ppermute(value, axis, [(i, (i - 1) % n) for i in range(n)])  40.7 us
    pallas_call x1, Pallas kernels, score(): pl.pallas_call(score_body, out_shape=(jax.ShapeDtypeStruct((blocks, rows,...  32.4 us
    dot_general x6, matrix products, dot_nn(): lax.dot_general(left, right, (((1,), (0,)), ((), ())), preferred_element_...  28.8 us
    unnamed x260, local copies, waits for them, and re-layouts  28.5 us
    dot_general x7, matrix products, dot_nt(): lax.dot_general(left, right, (((1,), (1,)), ((), ())), preferred_element_...  26.2 us
  transfers between devices with their start and end apart: 81, of which 38 were waited for; matrix products, arithmetic and copies ran while one was open for 30% of the time, Pallas kernels for 13%

profile of v2, /device:TPU:0, one launch (start us, length us, event | category | flops | bytes accessed | tf_op | source)
XLA Modules:
  0.0 642.0 jit_solution(9946532691154225058)
XLA Ops:
  25.8 5.0 collective-permute-done.2
  33.0 5.2 collective-permute-done.6
  41.0 13.7 %collective-permute-done.3 = bf16[1,496,256]{2,1,0:T(8,128)(2,1)S(1)} collective-permute-done((bf16[1,496,256]{2,1,0:T(8,128)(2,1)S(1)}, bf16[1,496,256]{2,1,0:T(8,128)(2,1)S(1)}, u32[]{:S(2)}, u32[]{:S(2)}) %collective-permute-start.3) | collective-permute-done | bytes 253984 | tf_op jit(solution)/shard_map/gather_table/ppermute | solution.py:40
  66.5 6.6 %collective-permute-done.13 = bf16[2,504,256]{2,1,0:T(8,128)(2,1)S(1)} collective-permute-done((bf16[2,504,256]{2,1,0:T(8,128)(2,1)}, bf16[2,504,256]{2,1,0:T(8,128)(2,1)S(1)}, u32[]{:S(2)}, u32[]{:S(2)}) %collective-permute-start.13) | collective-permute-done | bytes 516128 | tf_op jit(solution)/shard_map/gather_table/ppermute | solution.py:40
  75.3 5.1 collective-permute-done.8
  84.1 7.3 %collective-permute-done.4 = bf16[4,496,256]{2,1,0:T(8,128)(2,1)S(1)} collective-permute-done((bf16[4,496,256]{2,1,0:T(8,128)(2,1)S(1)}, bf16[4,496,256]{2,1,0:T(8,128)(2,1)S(1)}, u32[]{:S(2)}, u32[]{:S(2)}) %collective-permute-start.4) | collective-permute-done | bytes 1015840 | tf_op jit(solution)/shard_map/gather_table/ppermute | solution.py:35
  93.0 11.1 %collective-permute-done.9 = bf16[4,32,2688]{2,1,0:T(8,128)(2,1)S(1)} collective-permute-done((bf16[4,32,2688]{2,1,0:T(8,128)(2,1)S(1)}, bf16[4,32,2688]{2,1,0:T(8,128)(2,1)S(1)}, u32[]{:S(2)}, u32[]{:S(2)}) %collective-permute-start.9) | collective-permute-done | bytes 688160 | tf_op jit(solution)/shard_map/gather_first/ppermute | solution.py:35
  110.3 11.4 %gather_fusion = bf16[2048,256]{1,0:T(8,128)(2,1)} fusion(bf16[8000,256]{1,0:T(8,128)(2,1)} %bitcast.423, s32[2048]{0:T(1024)S(1)} %broadcast_clamp_fusion), kind=kCustom, calls=%fused_computation | custom fusion | bytes 2105344 | tf_op jit(solution)/shard_map/jit(_take)/gather | solution.py:662
  158.0 5.5 collective-permute-done.24
  182.4 26.1 %attend.1 = (bf16[1024,512]{1,0:T(8,128)(2,1)S(1)}, f32[4,2,1024]{2,1,0:T(2,128)S(1)}) custom-call(s32[4]{0:T(128)S(1)} %get-tuple-element.354.lo_ref, s32[4]{0:T(128)S(1)} %get-tuple-element.353.hi_ref, bf16[1024,512]{1,0:T(8,128)(2,1)S(1)} %fusion.7.q_ref, bf16[1024,512]{1,0:T(8,128)(2,1)S(1)} %get-tuple-element.231.k_ref, ...), custom_call_target="tpu_custom_call" | custom-call | flops 8589934592 | bytes 4194304 | tf_op jit(solution)/shard_map/attend/pallas_call | solution.py:220
  225.1 9.2 %multiply_convert_fusion.1 = (bf16[1024,2048]{1,0:T(8,128)(2,1)S(1)}, f32[1024,2048]{1,0:T(8,128)}) fusion(f32[2048]{0:T(1024)S(1)} %convert.84, bf16[1024,2048]{1,0:T(8,128)(2,1)S(1)} %bitcast.401, f32[1024,1024]{0,1:T(8,128)S(1)} %get-tuple-element.219, f32[1024]{0:T(1024)S(1)} %reshape.1504, f32[1024]{0:T(1024)S(1)} %reshape.1503, ...), kind=kOutput, calls=%fused_computation.8 | convolution fusion | flops 4312793088 | bytes 20996096 | tf_op jit(solution)/shard_map/dot_general | solution.py:23
  234.3 7.5 %collective-permute-done.32.refs_3_ = bf16[8,64,1024]{2,1,0:T(8,128)(2,1)S(1)} collective-permute-done((bf16[8,64,1024]{2,1,0:T(8,128)(2,1)S(1)}, bf16[8,64,1024]{2,1,0:T(8,128)(2,1)S(1)}, u32[]{:S(2)}, u32[]{:S(2)}) %collective-permute-start.32) | collective-permute-done | bytes 1048608 | tf_op jit(solution)/shard_map/gather_down/ppermute | solution.py:35
  242.7 6.9 %fusion.189 = (bf16[1024,1024]{0,1:T(8,128)(2,1)}, f32[1024,1024]{0,1:T(8,128)}) fusion(bf16[1024,2048]{1,0:T(8,128)(2,1)S(1)} %get-tuple-element.337, bf16[2048,1024]{1,0:T(8,128)(2,1)S(1)} %bitcast.403), kind=kOutput, calls=%fused_computation.604 | convolution fusion | flops 4296015872 | bytes 14680064 | tf_op jit(solution)/shard_map/dot_general | solution.py:23
  258.5 5.4 add_convert_fusion.1
  268.1 5.7 collective-permute-done.34
  277.2 32.4 %score.1 = (bf16[8,1000,2048]{2,1,0:T(8,128)(2,1)}, f32[8,1,2048]{2,1,0:T(1,128)S(1)}, f32[256,2048]{1,0:T(8,128)S(1)}, f32[1,2048]{1,0:T(1,128)S(1)}) custom-call(f32[1,2048]{1,0:T(1,128)S(1)} %fusion.6.norm_ref, bf16[2048,256]{1,0:T(8,128)(2,1)S(1)} %bitcast.399, bf16[8,1000,256]{2,1,0:T(8,128)(2,1)} %pad_maximum_fusion.table_ref, ...), custom_call_target="tpu_custom_call" | custom-call | flops 16777216000 | bytes 32768000 | tf_op jit(solution)/shard_map/score/pallas_call | solution.py:402
  329.4 6.4 collective-permute-done.42
  343.1 5.0 convolution_convert_fusion.2
  354.1 7.9 %fusion.191 = (bf16[2048]{0:T(1024)(128)(2,1)S(1)}, bf16[1024,2048]{1,0:T(8,128)(2,1)S(1)}) fusion(f32[1024,2048]{1,0:T(8,128)S(1)} %bitcast.517, f32[2048]{0:T(1024)S(1)} %convert.84, bf16[1024,1024]{0,1:T(8,128)(2,1)S(1)} %get-tuple-element.135, bf16[2048,1024]{1,0:T(8,128)(2,1)S(1)} %bitcast.404), kind=kOutput, calls=%fused_computation.606 | convolution fusion | flops 4324325376 | bytes 18886656 | tf_op jit(solution)/shard_map/dot_general | solution.py:27
  361.9 5.2 convolution_convert_fusion.1
  378.8 6.3 fusion.195
  385.1 5.3 copy.162
  404.1 18.7 %table_product.1.sum_ref = f32[8,1000,256]{2,1,0:T(8,128)} custom-call(bf16[8,1000,2048]{2,1,0:T(8,128)(2,1)} %get-tuple-element.133.raised_ref, bf16[2048,256]{1,0:T(8,128)(2,1)S(1)} %bitcast.400, f32[2048,8]{1,0:T(8,128)S(1)} %fusion.41.coef_ref), custom_call_target="tpu_custom_call" | custom-call | flops 8388608000 | bytes 32768000 | tf_op jit(solution)/shard_map/table_product/pallas_call | solution.py:445
  444.4 22.7 %attend_back.1 = (bf16[1024,512]{1,0:T(8,128)(2,1)S(1)}, bf16[1024,512]{1,0:T(8,128)(2,1)S(1)}, bf16[1024,512]{1,0:T(8,128)(2,1)S(1)}) custom-call(s32[4]{0:T(128)S(1)} %copy-done.27, s32[4]{0:T(128)S(1)} %copy-done.25, bf16[1024,512]{1,0:T(8,128)(2,1)S(1)} %copy-done.8, bf16[1024,512]{1,0:T(8,128)(2,1)S(1)} %copy-done.16, bf16[1024,512]{1,0:T(8,128)(2,1)S(1)} %copy-done.14, ...), custom_call_target="tpu_custom_call" | custom-call | flops 17179869184 | bytes 8388608 | tf_op jit(solution)/shard_map/attend_back/pallas_call | solution.py:313
  509.4 7.2 %collective-permute-done.55 = bf16[512,256]{1,0:T(8,128)(2,1)S(1)} collective-permute-done((bf16[512,256]{1,0:T(8,128)(2,1)S(1)}, bf16[512,256]{1,0:T(8,128)(2,1)S(1)}, u32[]{:S(2)}, u32[]{:S(2)}) %collective-permute-start.55) | collective-permute-done | bytes 262176 | tf_op jit(solution)/shard_map/token_pair/ppermute | solution.py:35
  527.7 7.2 %collective-permute-done.62 = bf16[4,32,768]{2,1,0:T(8,128)(2,1)S(1)} collective-permute-done((bf16[4,32,768]{2,1,0:T(8,128)(2,1)S(1)}, bf16[4,32,768]{2,1,0:T(8,128)(2,1)S(1)}, u32[]{:S(2)}, u32[]{:S(2)}) %collective-permute-start.62) | collective-permute-done | bytes 196640 | tf_op jit(solution)/shard_map/reduce_small/ppermute | solution.py:35
  535.5 11.6 %table_add.1 = bf16[8,1000,256]{2,1,0:T(8,128)(2,1)S(1)} custom-call(f32[8,1000,256]{2,1,0:T(8,128)} %table_product.1.sum_ref, s32[1,2048]{1,0:T(1,128)S(1)} %bitcast.420, bf16[2048,256]{1,0:T(8,128)(2,1)S(1)} %pad_maximum_fusion.16.grad_ref), custom_call_target="tpu_custom_call" | custom-call | flops 8388608000 | bytes 12288000 | tf_op jit(solution)/shard_map/table_add/pallas_call | solution.py:476
  554.4 8.1 %collective-permute-done.69 = bf16[64,2432]{1,0:T(8,128)(2,1)S(1)} collective-permute-done((bf16[64,2432]{1,0:T(8,128)(2,1)S(1)}, bf16[64,2432]{1,0:T(8,128)(2,1)S(1)}, u32[]{:S(2)}, u32[]{:S(2)}) %collective-permute-start.69) | collective-permute-done | bytes 311328 | tf_op jit(solution)/shard_map/reduce_rest/ppermute | solution.py:45
  562.4 6.6 %collective-permute-done.68 = bf16[2,376,256]{2,1,0:T(8,128)(2,1)S(1)} collective-permute-done((bf16[2,376,256]{2,1,0:T(8,128)(2,1)S(1)}, bf16[2,376,256]{2,1,0:T(8,128)(2,1)S(1)}, u32[]{:S(2)}, u32[]{:S(2)}) %collective-permute-start.68) | collective-permute-done | bytes 385056 | tf_op jit(solution)/shard_map/reduce_table/ppermute | solution.py:45
  582.3 5.6 collective-permute-done.71
  597.0 18.6 %collective-permute-done.75 = bf16[624,256]{1,0:T(8,128)(2,1)S(1)} collective-permute-done((bf16[624,256]{1,0:T(8,128)(2,1)S(1)}, bf16[624,256]{1,0:T(8,128)(2,1)S(1)}, u32[]{:S(2)}, u32[]{:S(2)}) %collective-permute-start.75) | collective-permute-done | bytes 319520 | tf_op jit(solution)/shard_map/reduce_table/ppermute | solution.py:45
  634.0 5.1 collective-permute-done.78
  (684 shorter events, 324.7 us)
Async XLA Ops:
  24.0 30.7 %collective-permute-start.12 = (bf16[2,504,256]{2,1,0:T(8,128)(2,1)S(1)}, bf16[2,504,256]{2,1,0:T(8,128)(2,1)}, u32[]{:S(2)}, u32[]{:S(2)}) collective-permute-start(bf16[2,504,256]{2,1,0:T(8,128)(2,1)S(1)} %get-tuple-element.267), channel_id=1, source_target_pairs={{0,24},{8,0},{16,8},{24,16},{1,25},{9,1},{17,9},{25,17},{2,26},{10... | collective-permute-start | bytes 1548296 | tf_op jit(solution)/shard_map/gather_table/ppermute | solution.py:40
  30.8 23.9 %collective-permute-start.3 = (bf16[1,496,256]{2,1,0:T(8,128)(2,1)S(1)}, bf16[1,496,256]{2,1,0:T(8,128)(2,1)S(1)}, u32[]{:S(2)}, u32[]{:S(2)}) collective-permute-start(bf16[1,496,256]{2,1,0:T(8,128)(2,1)S(1)} %collective-permute-done.2), channel_id=1, source_target_pairs={{0,24},{8,0},{16,8},{24,16},{1,25},{9,1},{17,9},{25,17},{2,26},{10... | collective-permute-start | bytes 761864 | tf_op jit(solution)/shard_map/gather_table/ppermute | solution.py:40
  38.3 23.9 %collective-permute-start.7 = (bf16[1,64,2688]{2,1,0:T(8,128)(2,1)}, bf16[1,64,2688]{2,1,0:T(8,128)(2,1)}, u32[]{:S(2)}, u32[]{:S(2)}) collective-permute-start(bf16[1,64,2688]{2,1,0:T(8,128)(2,1)} %collective-permute-done.6), channel_id=1, source_target_pairs={{0,24},{8,0},{16,8},{24,16},{1,25},{9,1},{17,9},{25,17},{2,26},{10... | collective-permute-start | bytes 1032200 | tf_op jit(solution)/shard_map/gather_first/ppermute | solution.py:40
  65.9 25.5 %collective-permute-start.4 = (bf16[4,496,256]{2,1,0:T(8,128)(2,1)S(1)}, bf16[4,496,256]{2,1,0:T(8,128)(2,1)S(1)}, u32[]{:S(2)}, u32[]{:S(2)}) collective-permute-start(bf16[4,496,256]{2,1,0:T(8,128)(2,1)S(1)} %pad_maximum_fusion.18), channel_id=1, source_target_pairs={{0,4},{4,0},{1,5},{5,1},{2,6},{6,2},{3,7},{7,3},{8,12},{12,8},{9,1... | collective-permute-start | bytes 3047432 | tf_op jit(solution)/shard_map/gather_table/ppermute | solution.py:35
  81.9 22.2 %collective-permute-start.9 = (bf16[4,32,2688]{2,1,0:T(8,128)(2,1)S(1)}, bf16[4,32,2688]{2,1,0:T(8,128)(2,1)S(1)}, u32[]{:S(2)}, u32[]{:S(2)}) collective-permute-start(bf16[4,32,2688]{2,1,0:T(8,128)(2,1)S(1)} %get-tuple-element.249), channel_id=1, source_target_pairs={{0,4},{4,0},{1,5},{5,1},{2,6},{6,2},{3,7},{7,3},{8,12},{12,8},{9,1... | collective-permute-start | bytes 2064392 | tf_op jit(solution)/shard_map/gather_first/ppermute | solution.py:35
  82.5 23.2 %collective-permute-start.10 = (bf16[4,32,2688]{2,1,0:T(8,128)(2,1)S(1)}, bf16[4,32,2688]{2,1,0:T(8,128)(2,1)S(1)}, u32[]{:S(2)}, u32[]{:S(2)}) collective-permute-start(bf16[4,32,2688]{2,1,0:T(8,128)(2,1)S(1)} %get-tuple-element.248), channel_id=1, source_target_pairs={{0,1},{1,0},{2,3},{3,2},{4,5},{5,4},{6,7},{7,6},{8,9},{9,8},{10,11... | collective-permute-start | bytes 2064392 | tf_op jit(solution)/shard_map/gather_first/ppermute | solution.py:35
  104.2 30.3 %collective-permute-start.17 = (bf16[8,32,2688]{2,1,0:T(8,128)(2,1)S(1)}, bf16[8,32,2688]{2,1,0:T(8,128)(2,1)}, u32[]{:S(2)}, u32[]{:S(2)}) collective-permute-start(bf16[8,32,2688]{2,1,0:T(8,128)(2,1)S(1)} %pad_maximum_fusion.5.refs_0_), channel_id=1, source_target_pairs={{0,1},{1,0},{2,3},{3,2},{4,5},{5,4},{6,7},{7,6},{8,9},{9,8},{10,11... | collective-permute-start | bytes 4128776 | tf_op jit(solution)/shard_map/gather_first/ppermute | solution.py:35
  105.9 30.0 %collective-permute-start.18 = (bf16[8,32,2688]{2,1,0:T(8,128)(2,1)S(1)}, bf16[8,32,2688]{2,1,0:T(8,128)(2,1)}, u32[]{:S(2)}, u32[]{:S(2)}) collective-permute-start(bf16[8,32,2688]{2,1,0:T(8,128)(2,1)S(1)} %pad_maximum_fusion.6.refs_2_), channel_id=1, source_target_pairs={{0,4},{4,0},{1,5},{5,1},{2,6},{6,2},{3,7},{7,3},{8,12},{12,8},{9,1... | collective-permute-start | bytes 4128776 | tf_op jit(solution)/shard_map/gather_first/ppermute | solution.py:35
  108.0 23.0 %collective-permute-start.19 = (bf16[2,64,2048]{2,1,0:T(8,128)(2,1)}, bf16[2,64,2048]{2,1,0:T(8,128)(2,1)}, u32[]{:S(2)}, u32[]{:S(2)}) collective-permute-start(bf16[2,64,2048]{2,1,0:T(8,128)(2,1)} %pad_maximum_fusion.19), channel_id=1, source_target_pairs={{0,16},{8,24},{16,0},{24,8},{1,17},{9,25},{17,1},{25,9},{2,18},{10... | collective-permute-start | bytes 1572872 | tf_op jit(solution)/shard_map/gather_up/ppermute | solution.py:75
  151.5 26.2 %collective-permute-start.25 = (bf16[2,128,1024]{2,1,0:T(8,128)(2,1)}, bf16[2,128,1024]{2,1,0:T(8,128)(2,1)S(1)}, u32[]{:S(2)}, u32[]{:S(2)}) collective-permute-start(bf16[2,128,1024]{2,1,0:T(8,128)(2,1)} %pad_maximum_fusion.20), channel_id=1, source_target_pairs={{0,16},{8,24},{16,0},{24,8},{1,17},{9,25},{17,1},{25,9},{2,18},{10... | collective-permute-start | bytes 1572872 | tf_op jit(solution)/shard_map/gather_down/ppermute | solution.py:75
  166.3 42.4 %collective-permute-start.26 = (bf16[8,32,2048]{2,1,0:T(8,128)(2,1)S(1)}, bf16[8,32,2048]{2,1,0:T(8,128)(2,1)S(1)}, u32[]{:S(2)}, u32[]{:S(2)}) collective-permute-start(bf16[8,32,2048]{2,1,0:T(8,128)(2,1)S(1)} %pad_maximum_fusion.10.refs_0_), channel_id=1, source_target_pairs={{0,1},{1,0},{2,3},{3,2},{4,5},{5,4},{6,7},{7,6},{8,9},{9,8},{10,11... | collective-permute-start | bytes 3145736 | tf_op jit(solution)/shard_map/gather_up/ppermute | solution.py:35
  167.8 40.8 %collective-permute-start.27 = (bf16[8,32,2048]{2,1,0:T(8,128)(2,1)S(1)}, bf16[8,32,2048]{2,1,0:T(8,128)(2,1)S(1)}, u32[]{:S(2)}, u32[]{:S(2)}) collective-permute-start(bf16[8,32,2048]{2,1,0:T(8,128)(2,1)S(1)} %pad_maximum_fusion.11.refs_2_), channel_id=1, source_target_pairs={{0,4},{4,0},{1,5},{5,1},{2,6},{6,2},{3,7},{7,3},{8,12},{12,8},{9,1... | collective-permute-start | bytes 3145736 | tf_op jit(solution)/shard_map/gather_up/ppermute | solution.py:35
  179.9 28.7 %collective-permute-start.29 = (bf16[4,64,1024]{2,1,0:T(8,128)(2,1)S(1)}, bf16[4,64,1024]{2,1,0:T(8,128)(2,1)S(1)}, u32[]{:S(2)}, u32[]{:S(2)}) collective-permute-start(bf16[4,64,1024]{2,1,0:T(8,128)(2,1)S(1)} %get-tuple-element.254), channel_id=1, source_target_pairs={{0,1},{1,0},{2,3},{3,2},{4,5},{5,4},{6,7},{7,6},{8,9},{9,8},{10,11... | collective-permute-start | bytes 1572872 | tf_op jit(solution)/shard_map/gather_down/ppermute | solution.py:35
  181.4 27.2 %collective-permute-start.28 = (bf16[4,64,1024]{2,1,0:T(8,128)(2,1)S(1)}, bf16[4,64,1024]{2,1,0:T(8,128)(2,1)S(1)}, u32[]{:S(2)}, u32[]{:S(2)}) collective-permute-start(bf16[4,64,1024]{2,1,0:T(8,128)(2,1)S(1)} %get-tuple-element.255), channel_id=1, source_target_pairs={{0,4},{4,0},{1,5},{5,1},{2,6},{6,2},{3,7},{7,3},{8,12},{12,8},{9,1... | collective-permute-start | bytes 1572872 | tf_op jit(solution)/shard_map/gather_down/ppermute | solution.py:35
  214.6 27.3 %collective-permute-start.31 = (bf16[8,64,1024]{2,1,0:T(8,128)(2,1)S(1)}, bf16[8,64,1024]{2,1,0:T(8,128)(2,1)S(1)}, u32[]{:S(2)}, u32[]{:S(2)}) collective-permute-start(bf16[8,64,1024]{2,1,0:T(8,128)(2,1)S(1)} %pad_maximum_fusion.12.refs_0_), channel_id=1, source_target_pairs={{0,1},{1,0},{2,3},{3,2},{4,5},{5,4},{6,7},{7,6},{8,9},{9,8},{10,11... | collective-permute-start | bytes 3145736 | tf_op jit(solution)/shard_map/gather_down/ppermute | solution.py:35
  216.5 25.3 %collective-permute-start.32 = (bf16[8,64,1024]{2,1,0:T(8,128)(2,1)S(1)}, bf16[8,64,1024]{2,1,0:T(8,128)(2,1)S(1)}, u32[]{:S(2)}, u32[]{:S(2)}) collective-permute-start(bf16[8,64,1024]{2,1,0:T(8,128)(2,1)S(1)} %pad_maximum_fusion.13.refs_2_), channel_id=1, source_target_pairs={{0,4},{4,0},{1,5},{5,1},{2,6},{6,2},{3,7},{7,3},{8,12},{12,8},{9,1... | collective-permute-start | bytes 3145736 | tf_op jit(solution)/shard_map/gather_down/ppermute | solution.py:35
  350.1 25.4 %collective-permute-start.45 = (bf16[4,2,64,1024]{3,2,0,1:T(8,128)(2,1)S(1)}, bf16[4,2,64,1024]{3,2,0,1:T(8,128)(2,1)}, u32[]{:S(2)}, u32[]{:S(2)}) collective-permute-start(bf16[4,2,64,1024]{3,2,0,1:T(8,128)(2,1)S(1)} %bitcast.444), channel_id=1, source_target_pairs={{0,4},{4,0},{1,5},{5,1},{2,6},{6,2},{3,7},{7,3},{8,12},{12,8},{9,1... | collective-permute-start | bytes 3145736 | tf_op jit(solution)/shard_map/reduce_down/ppermute | solution.py:35
  352.6 26.2 %collective-permute-start.44 = (bf16[4,2,64,1024]{3,2,0,1:T(8,128)(2,1)S(1)}, bf16[4,2,64,1024]{3,2,0,1:T(8,128)(2,1)}, u32[]{:S(2)}, u32[]{:S(2)}) collective-permute-start(bf16[4,2,64,1024]{3,2,0,1:T(8,128)(2,1)S(1)} %bitcast.445), channel_id=1, source_target_pairs={{0,1},{1,0},{2,3},{3,2},{4,5},{5,4},{6,7},{7,6},{8,9},{9,8},{10,11... | collective-permute-start | bytes 3145736 | tf_op jit(solution)/shard_map/reduce_down/ppermute | solution.py:35
  371.2 59.7 %collective-permute-start.48 = (bf16[4,2,32,2048]{3,2,0,1:T(8,128)(2,1)}, bf16[4,2,32,2048]{3,2,0,1:T(8,128)(2,1)}, u32[]{:S(2)}, u32[]{:S(2)}) collective-permute-start(bf16[4,2,32,2048]{3,2,0,1:T(8,128)(2,1)} %bitcast.389), channel_id=1, source_target_pairs={{0,1},{1,0},{2,3},{3,2},{4,5},{5,4},{6,7},{7,6},{8,9},{9,8},{10,11... | collective-permute-start | bytes 3145736 | tf_op jit(solution)/shard_map/reduce_up/ppermute | solution.py:35
  393.1 29.8 %collective-permute-start.46 = (bf16[1024,1024]{0,1:T(8,128)(2,1)S(1)}, bf16[1024,1024]{0,1:T(8,128)(2,1)S(1)}, u32[]{:S(2)}, u32[]{:S(2)}) collective-permute-start(bf16[1024,1024]{0,1:T(8,128)(2,1)S(1)} %convert_element_type.616), channel_id=1, source_target_pairs={{0,2},{2,0},{1,3},{3,1},{4,6},{6,4},{5,7},{7,5},{8,10},{10,8},{9,1... | collective-permute-start | bytes 6291464 | tf_op jit(solution)/shard_map/ppermute | solution.py:35
  395.5 35.4 %collective-permute-start.47 = (bf16[4,2,32,2048]{3,2,0,1:T(8,128)(2,1)}, bf16[4,2,32,2048]{3,2,0,1:T(8,128)(2,1)}, u32[]{:S(2)}, u32[]{:S(2)}) collective-permute-start(bf16[4,2,32,2048]{3,2,0,1:T(8,128)(2,1)} %bitcast.390), channel_id=1, source_target_pairs={{0,4},{4,0},{1,5},{5,1},{2,6},{6,2},{3,7},{7,3},{8,12},{12,8},{9,1... | collective-permute-start | bytes 3145736 | tf_op jit(solution)/shard_map/reduce_up/ppermute | solution.py:35
  400.2 68.1 %collective-permute-start.52 = (bf16[4,64,1024]{2,1,0:T(8,128)(2,1)}, bf16[4,64,1024]{2,1,0:T(8,128)(2,1)}, u32[]{:S(2)}, u32[]{:S(2)}) collective-permute-start(bf16[4,64,1024]{2,1,0:T(8,128)(2,1)} %dynamic-slice_bitcast_fusion.1), channel_id=1, source_target_pairs={{0,1},{1,0},{2,3},{3,2},{4,5},{5,4},{6,7},{7,6},{8,9},{9,8},{10,11... | collective-permute-start | bytes 1572872 | tf_op jit(solution)/shard_map/reduce_down/ppermute | solution.py:35
  403.2 65.0 %collective-permute-start.51 = (bf16[4,64,1024]{2,1,0:T(8,128)(2,1)}, bf16[4,64,1024]{2,1,0:T(8,128)(2,1)}, u32[]{:S(2)}, u32[]{:S(2)}) collective-permute-start(bf16[4,64,1024]{2,1,0:T(8,128)(2,1)} %dynamic-slice_bitcast_fusion.2), channel_id=1, source_target_pairs={{0,4},{4,0},{1,5},{5,1},{2,6},{6,2},{3,7},{7,3},{8,12},{12,8},{9,1... | collective-permute-start | bytes 1572872 | tf_op jit(solution)/shard_map/reduce_down/ppermute | solution.py:35
  440.7 27.6 %collective-permute-start.50 = (bf16[4,32,2048]{2,1,0:T(8,128)(2,1)}, bf16[4,32,2048]{2,1,0:T(8,128)(2,1)}, u32[]{:S(2)}, u32[]{:S(2)}) collective-permute-start(bf16[4,32,2048]{2,1,0:T(8,128)(2,1)} %dynamic-slice_bitcast_fusion.3), channel_id=1, source_target_pairs={{0,4},{4,0},{1,5},{5,1},{2,6},{6,2},{3,7},{7,3},{8,12},{12,8},{9,1... | collective-permute-start | bytes 1572872 | tf_op jit(solution)/shard_map/reduce_up/ppermute | solution.py:35
  441.8 26.5 %collective-permute-start.49 = (bf16[4,32,2048]{2,1,0:T(8,128)(2,1)}, bf16[4,32,2048]{2,1,0:T(8,128)(2,1)}, u32[]{:S(2)}, u32[]{:S(2)}) collective-permute-start(bf16[4,32,2048]{2,1,0:T(8,128)(2,1)} %dynamic-slice_bitcast_fusion.4), channel_id=1, source_target_pairs={{0,1},{1,0},{2,3},{3,2},{4,5},{5,4},{6,7},{7,6},{8,9},{9,8},{10,11... | collective-permute-start | bytes 1572872 | tf_op jit(solution)/shard_map/reduce_up/ppermute | solution.py:35
  443.3 25.0 %collective-permute-start.53 = (bf16[4,2,32,1024]{3,2,0,1:T(8,128)(2,1)}, bf16[4,2,32,1024]{3,2,0,1:T(8,128)(2,1)}, u32[]{:S(2)}, u32[]{:S(2)}) collective-permute-start(bf16[4,2,32,1024]{3,2,0,1:T(8,128)(2,1)} %bitcast.395), channel_id=1, source_target_pairs={{0,4},{4,0},{1,5},{5,1},{2,6},{6,2},{3,7},{7,3},{8,12},{12,8},{9,1... | collective-permute-start | bytes 1572872 | tf_op jit(solution)/shard_map/reduce_attn/ppermute | solution.py:35
  485.0 24.4 %collective-permute-start.63 = (bf16[4,32,1024]{2,1,0:T(8,128)(2,1)}, bf16[4,32,1024]{2,1,0:T(8,128)(2,1)}, u32[]{:S(2)}, u32[]{:S(2)}) collective-permute-start(bf16[4,32,1024]{2,1,0:T(8,128)(2,1)} %dynamic-slice_bitcast_fusion.11), channel_id=1, source_target_pairs={{0,1},{1,0},{2,3},{3,2},{4,5},{5,4},{6,7},{7,6},{8,9},{9,8},{10,11... | collective-permute-start | bytes 786440 | tf_op jit(solution)/shard_map/reduce_attn/ppermute | solution.py:35
  488.5 29.9 %collective-permute-start.57 = (bf16[4,2,32,1536]{3,2,0,1:T(8,128)(2,1)}, bf16[4,2,32,1536]{3,2,0,1:T(8,128)(2,1)}, u32[]{:S(2)}, u32[]{:S(2)}) collective-permute-start(bf16[4,2,32,1536]{3,2,0,1:T(8,128)(2,1)} %bitcast.394), channel_id=1, source_target_pairs={{0,4},{4,0},{1,5},{5,1},{2,6},{6,2},{3,7},{7,3},{8,12},{12,8},{9,1... | collective-permute-start | bytes 2359304 | tf_op jit(solution)/shard_map/reduce_qkv/ppermute | solution.py:35
  491.0 30.9 %collective-permute-start.59 = (bf16[4,2,32,1536]{3,2,0,1:T(8,128)(2,1)}, bf16[4,2,32,1536]{3,2,0,1:T(8,128)(2,1)}, u32[]{:S(2)}, u32[]{:S(2)}) collective-permute-start(bf16[4,2,32,1536]{3,2,0,1:T(8,128)(2,1)} %bitcast.393), channel_id=1, source_target_pairs={{0,1},{1,0},{2,3},{3,2},{4,5},{5,4},{6,7},{7,6},{8,9},{9,8},{10,11... | collective-permute-start | bytes 2359304 | tf_op jit(solution)/shard_map/reduce_qkv/ppermute | solution.py:35
  527.3 22.8 %collective-permute-start.66 = (bf16[64,4096]{1,0:T(8,128)(2,1)S(1)}, bf16[64,4096]{1,0:T(8,128)(2,1)S(1)}, u32[]{:S(2)}, u32[]{:S(2)}) collective-permute-start(bf16[64,4096]{1,0:T(8,128)(2,1)S(1)} %fusion.34), channel_id=1, source_target_pairs={{0,8},{8,16},{16,24},{24,0},{1,9},{9,17},{17,25},{25,1},{2,10},{10... | collective-permute-start | bytes 1572872 | tf_op jit(solution)/shard_map/reduce_mlp/ppermute | solution.py:45
  553.2 26.7 %collective-permute-start.73 = (bf16[4,320,256]{2,1,0:T(8,128)(2,1)S(1)}, bf16[4,320,256]{2,1,0:T(8,128)(2,1)S(1)}, u32[]{:S(2)}, u32[]{:S(2)}) collective-permute-start(bf16[4,320,256]{2,1,0:T(8,128)(2,1)S(1)} %slice_bitcast_fusion.1), channel_id=1, source_target_pairs={{0,4},{4,0},{1,5},{5,1},{2,6},{6,2},{3,7},{7,3},{8,12},{12,8},{9,1... | collective-permute-start | bytes 1966088 | tf_op jit(solution)/shard_map/reduce_table/ppermute | solution.py:35
  594.5 24.0 %collective-permute-start.79 = (f32[32,1536]{1,0:T(8,128)}, f32[32,1536]{1,0:T(8,128)}, u32[]{:S(2)}, u32[]{:S(2)}) collective-permute-start(f32[32,1536]{1,0:T(8,128)} %get-tuple-element.269), channel_id=1, source_target_pairs={{0,2},{2,0},{1,3},{3,1},{4,6},{6,4},{5,7},{7,5},{8,10},{10,8},{9,1... | collective-permute-start | bytes 589832 | tf_op jit(solution)/shard_map/ppermute | solution.py:35
  (167 other events, 1904.3 us)

commit v3 on v2

--- a/solution.py
+++ b/solution.py
@@ -847,7 +847,7 @@
     ).T
 
     zy = (zn, lax.axis_size("y"))
-    table_cut = block_len * 5 // 128 * 16
+    table_cut = block_len * 9 // 256 * 16
 
     def rows_of(grad):
         rows = grad.shape[0] // (2 * groups)

time: 650 us -> 646 us (level)
    unnamed x260 -> x258, local copies, waits for them, and re-layouts: 28.5 us -> 24.8 us
where the time goes in v3:
time: 646 us; the launch traced here: 638 us
  waiting for transfers between devices  186 us (29%)
  Pallas kernels  115 us (18%)
  local copies, waits for them, and re-layouts  96.2 us (15%)
  other arithmetic  93.9 us (15%)
  matrix products  73.8 us (11%)
  starting transfers between devices  67.3 us (10%)
    ppermute x56, waiting for transfers between devices, swap(): return lax.ppermute(value, axis, SWAP)  80 us
    ppermute x12, waiting for transfers between devices, ring_up(): return lax.ppermute(value, axis, [(i, (i + 1) % n) for i in range(n)])  55.2 us
    ppermute x56, starting transfers between devices, swap(): return lax.ppermute(value, axis, SWAP)  44.7 us
    ppermute x9, waiting for transfers between devices, ring_down(): return lax.ppermute(value, axis, [(i, (i - 1) % n) for i in range(n)])  40.7 us
    pallas_call x1, Pallas kernels, score(): pl.pallas_call(score_body, out_shape=(jax.ShapeDtypeStruct((blocks, rows,...  32.4 us
    dot_general x6, matrix products, dot_nn(): lax.dot_general(left, right, (((1,), (0,)), ((), ())), preferred_element_...  28.7 us
    pallas_call x1, Pallas kernels, attend(): pl.pallas_call(attend_body, out_shape=(jax.ShapeDtypeStruct((length, widt...  26.1 us
    dot_general x7, matrix products, dot_nt(): lax.dot_general(left, right, (((1,), (1,)), ((), ())), preferred_element_...  26.1 us
  transfers between devices with their start and end apart: 81, of which 38 were waited for; matrix products, arithmetic and copies ran while one was open for 30% of the time, Pallas kernels for 13%

profile of v3, /device:TPU:0, one launch (start us, length us, event | category | flops | bytes accessed | tf_op | source)
XLA Modules:
  0.0 638.2 jit_solution(11766617221458320390)
XLA Ops:
  25.8 5.0 collective-permute-done.2
  33.0 5.2 collective-permute-done.6
  41.0 13.7 %collective-permute-done.3 = bf16[1,496,256]{2,1,0:T(8,128)(2,1)S(1)} collective-permute-done((bf16[1,496,256]{2,1,0:T(8,128)(2,1)S(1)}, bf16[1,496,256]{2,1,0:T(8,128)(2,1)S(1)}, u32[]{:S(2)}, u32[]{:S(2)}) %collective-permute-start.3) | collective-permute-done | bytes 253984 | tf_op jit(solution)/shard_map/gather_table/ppermute | solution.py:40
  66.5 6.6 %collective-permute-done.13 = bf16[2,504,256]{2,1,0:T(8,128)(2,1)S(1)} collective-permute-done((bf16[2,504,256]{2,1,0:T(8,128)(2,1)}, bf16[2,504,256]{2,1,0:T(8,128)(2,1)S(1)}, u32[]{:S(2)}, u32[]{:S(2)}) %collective-permute-start.13) | collective-permute-done | bytes 516128 | tf_op jit(solution)/shard_map/gather_table/ppermute | solution.py:40
  75.3 5.1 collective-permute-done.8
  84.1 7.3 %collective-permute-done.4 = bf16[4,496,256]{2,1,0:T(8,128)(2,1)S(1)} collective-permute-done((bf16[4,496,256]{2,1,0:T(8,128)(2,1)S(1)}, bf16[4,496,256]{2,1,0:T(8,128)(2,1)S(1)}, u32[]{:S(2)}, u32[]{:S(2)}) %collective-permute-start.4) | collective-permute-done | bytes 1015840 | tf_op jit(solution)/shard_map/gather_table/ppermute | solution.py:35
  93.0 11.1 %collective-permute-done.9 = bf16[4,32,2688]{2,1,0:T(8,128)(2,1)S(1)} collective-permute-done((bf16[4,32,2688]{2,1,0:T(8,128)(2,1)S(1)}, bf16[4,32,2688]{2,1,0:T(8,128)(2,1)S(1)}, u32[]{:S(2)}, u32[]{:S(2)}) %collective-permute-start.9) | collective-permute-done | bytes 688160 | tf_op jit(solution)/shard_map/gather_first/ppermute | solution.py:35
  110.3 11.4 %gather_fusion = bf16[2048,256]{1,0:T(8,128)(2,1)} fusion(bf16[8000,256]{1,0:T(8,128)(2,1)} %bitcast.423, s32[2048]{0:T(1024)S(1)} %broadcast_clamp_fusion), kind=kCustom, calls=%fused_computation | custom fusion | bytes 2105344 | tf_op jit(solution)/shard_map/jit(_take)/gather | solution.py:662
  158.0 5.5 collective-permute-done.24
  182.4 26.1 %attend.1 = (bf16[1024,512]{1,0:T(8,128)(2,1)S(1)}, f32[4,2,1024]{2,1,0:T(2,128)S(1)}) custom-call(s32[4]{0:T(128)S(1)} %get-tuple-element.354.lo_ref, s32[4]{0:T(128)S(1)} %get-tuple-element.353.hi_ref, bf16[1024,512]{1,0:T(8,128)(2,1)S(1)} %fusion.7.q_ref, bf16[1024,512]{1,0:T(8,128)(2,1)S(1)} %get-tuple-element.231.k_ref, ...), custom_call_target="tpu_custom_call" | custom-call | flops 8589934592 | bytes 4194304 | tf_op jit(solution)/shard_map/attend/pallas_call | solution.py:220
  223.6 9.2 %multiply_convert_fusion.1 = (bf16[1024,2048]{1,0:T(8,128)(2,1)S(1)}, f32[1024,2048]{1,0:T(8,128)}) fusion(f32[2048]{0:T(1024)S(1)} %convert.84, bf16[1024,2048]{1,0:T(8,128)(2,1)S(1)} %bitcast.401, f32[1024,1024]{0,1:T(8,128)S(1)} %get-tuple-element.219, f32[1024]{0:T(1024)S(1)} %reshape.1504, f32[1024]{0:T(1024)S(1)} %reshape.1503, ...), kind=kOutput, calls=%fused_computation.8 | convolution fusion | flops 4312793088 | bytes 20996096 | tf_op jit(solution)/shard_map/dot_general | solution.py:23
  232.7 8.8 %collective-permute-done.32.refs_3_ = bf16[8,64,1024]{2,1,0:T(8,128)(2,1)S(1)} collective-permute-done((bf16[8,64,1024]{2,1,0:T(8,128)(2,1)S(1)}, bf16[8,64,1024]{2,1,0:T(8,128)(2,1)S(1)}, u32[]{:S(2)}, u32[]{:S(2)}) %collective-permute-start.32) | collective-permute-done | bytes 1048608 | tf_op jit(solution)/shard_map/gather_down/ppermute | solution.py:35
  242.4 6.9 %fusion.189 = (bf16[1024,1024]{0,1:T(8,128)(2,1)}, f32[1024,1024]{0,1:T(8,128)}) fusion(bf16[1024,2048]{1,0:T(8,128)(2,1)S(1)} %get-tuple-element.337, bf16[2048,1024]{1,0:T(8,128)(2,1)S(1)} %bitcast.403), kind=kOutput, calls=%fused_computation.604 | convolution fusion | flops 4296015872 | bytes 14680064 | tf_op jit(solution)/shard_map/dot_general | solution.py:23
  258.3 5.4 add_convert_fusion.1
  268.1 5.5 collective-permute-done.34
  277.0 32.4 %score.1 = (bf16[8,1000,2048]{2,1,0:T(8,128)(2,1)}, f32[8,1,2048]{2,1,0:T(1,128)S(1)}, f32[256,2048]{1,0:T(8,128)S(1)}, f32[1,2048]{1,0:T(1,128)S(1)}) custom-call(f32[1,2048]{1,0:T(1,128)S(1)} %fusion.6.norm_ref, bf16[2048,256]{1,0:T(8,128)(2,1)S(1)} %bitcast.399, bf16[8,1000,256]{2,1,0:T(8,128)(2,1)} %pad_maximum_fusion.table_ref, ...), custom_call_target="tpu_custom_call" | custom-call | flops 16777216000 | bytes 32768000 | tf_op jit(solution)/shard_map/score/pallas_call | solution.py:402
  329.2 6.6 %collective-permute-done.42 = bf16[256,512]{0,1:T(8,128)(2,1)S(1)} collective-permute-done((bf16[256,512]{0,1:T(8,128)(2,1)S(1)}, bf16[256,512]{0,1:T(8,128)(2,1)S(1)}, u32[]{:S(2)}, u32[]{:S(2)}) %collective-permute-start.42) | collective-permute-done | bytes 262176 | tf_op jit(solution)/shard_map/ppermute | solution.py:35
  343.1 5.0 convolution_convert_fusion.2
  353.7 7.9 %fusion.191 = (bf16[2048]{0:T(1024)(128)(2,1)S(1)}, bf16[1024,2048]{1,0:T(8,128)(2,1)S(1)}) fusion(f32[1024,2048]{1,0:T(8,128)S(1)} %bitcast.517, f32[2048]{0:T(1024)S(1)} %convert.84, bf16[1024,1024]{0,1:T(8,128)(2,1)S(1)} %get-tuple-element.135, bf16[2048,1024]{1,0:T(8,128)(2,1)S(1)} %bitcast.404), kind=kOutput, calls=%fused_computation.606 | convolution fusion | flops 4324325376 | bytes 18886656 | tf_op jit(solution)/shard_map/dot_general | solution.py:27
  361.6 5.2 convolution_convert_fusion.1
  378.0 6.3 fusion.195
  384.3 5.3 copy.162
  404.2 18.8 %table_product.1.sum_ref = f32[8,1000,256]{2,1,0:T(8,128)} custom-call(bf16[8,1000,2048]{2,1,0:T(8,128)(2,1)} %get-tuple-element.133.raised_ref, bf16[2048,256]{1,0:T(8,128)(2,1)S(1)} %bitcast.400, f32[2048,8]{1,0:T(8,128)S(1)} %fusion.41.coef_ref), custom_call_target="tpu_custom_call" | custom-call | flops 8388608000 | bytes 32768000 | tf_op jit(solution)/shard_map/table_product/pallas_call | solution.py:445
  443.5 22.7 %attend_back.1 = (bf16[1024,512]{1,0:T(8,128)(2,1)S(1)}, bf16[1024,512]{1,0:T(8,128)(2,1)S(1)}, bf16[1024,512]{1,0:T(8,128)(2,1)S(1)}) custom-call(s32[4]{0:T(128)S(1)} %copy-done.27, s32[4]{0:T(128)S(1)} %copy-done.25, bf16[1024,512]{1,0:T(8,128)(2,1)S(1)} %copy-done.8, bf16[1024,512]{1,0:T(8,128)(2,1)S(1)} %copy-done.16, bf16[1024,512]{1,0:T(8,128)(2,1)S(1)} %copy-done.14, ...), custom_call_target="tpu_custom_call" | custom-call | flops 17179869184 | bytes 8388608 | tf_op jit(solution)/shard_map/attend_back/pallas_call | solution.py:313
  509.3 7.2 %collective-permute-done.55 = bf16[512,256]{1,0:T(8,128)(2,1)S(1)} collective-permute-done((bf16[512,256]{1,0:T(8,128)(2,1)S(1)}, bf16[512,256]{1,0:T(8,128)(2,1)S(1)}, u32[]{:S(2)}, u32[]{:S(2)}) %collective-permute-start.55) | collective-permute-done | bytes 262176 | tf_op jit(solution)/shard_map/token_pair/ppermute | solution.py:35
  527.6 7.1 %collective-permute-done.62 = bf16[4,32,768]{2,1,0:T(8,128)(2,1)S(1)} collective-permute-done((bf16[4,32,768]{2,1,0:T(8,128)(2,1)S(1)}, bf16[4,32,768]{2,1,0:T(8,128)(2,1)S(1)}, u32[]{:S(2)}, u32[]{:S(2)}) %collective-permute-start.62) | collective-permute-done | bytes 196640 | tf_op jit(solution)/shard_map/reduce_small/ppermute | solution.py:35
  535.2 11.6 %table_add.1 = bf16[8,1000,256]{2,1,0:T(8,128)(2,1)S(1)} custom-call(f32[8,1000,256]{2,1,0:T(8,128)} %table_product.1.sum_ref, s32[1,2048]{1,0:T(1,128)S(1)} %bitcast.420, bf16[2048,256]{1,0:T(8,128)(2,1)S(1)} %pad_maximum_fusion.16.grad_ref), custom_call_target="tpu_custom_call" | custom-call | flops 8388608000 | bytes 12288000 | tf_op jit(solution)/shard_map/table_add/pallas_call | solution.py:476
  553.5 8.1 %collective-permute-done.69 = bf16[64,2432]{1,0:T(8,128)(2,1)S(1)} collective-permute-done((bf16[64,2432]{1,0:T(8,128)(2,1)S(1)}, bf16[64,2432]{1,0:T(8,128)(2,1)S(1)}, u32[]{:S(2)}, u32[]{:S(2)}) %collective-permute-start.69) | collective-permute-done | bytes 311328 | tf_op jit(solution)/shard_map/reduce_rest/ppermute | solution.py:45
  561.6 8.0 %collective-permute-done.68 = bf16[2,440,256]{2,1,0:T(8,128)(2,1)S(1)} collective-permute-done((bf16[2,440,256]{2,1,0:T(8,128)(2,1)S(1)}, bf16[2,440,256]{2,1,0:T(8,128)(2,1)S(1)}, u32[]{:S(2)}, u32[]{:S(2)}) %collective-permute-start.68) | collective-permute-done | bytes 450592 | tf_op jit(solution)/shard_map/reduce_table/ppermute | solution.py:45
  576.6 6.2 collective-permute-done.72
  582.8 7.0 %collective-permute-done.71 = bf16[2,440,256]{2,1,0:T(8,128)(2,1)S(1)} collective-permute-done((bf16[2,440,256]{2,1,0:T(8,128)(2,1)}, bf16[2,440,256]{2,1,0:T(8,128)(2,1)S(1)}, u32[]{:S(2)}, u32[]{:S(2)}) %collective-permute-start.71) | collective-permute-done | bytes 450592 | tf_op jit(solution)/shard_map/reduce_table/ppermute | solution.py:45
  595.1 16.5 %collective-permute-done.75 = bf16[560,256]{1,0:T(8,128)(2,1)S(1)} collective-permute-done((bf16[560,256]{1,0:T(8,128)(2,1)S(1)}, bf16[560,256]{1,0:T(8,128)(2,1)S(1)}, u32[]{:S(2)}, u32[]{:S(2)}) %collective-permute-start.75) | collective-permute-done | bytes 286752 | tf_op jit(solution)/shard_map/reduce_table/ppermute | solution.py:45
  (682 shorter events, 317.8 us)
Async XLA Ops:
  24.0 30.7 %collective-permute-start.12 = (bf16[2,504,256]{2,1,0:T(8,128)(2,1)S(1)}, bf16[2,504,256]{2,1,0:T(8,128)(2,1)}, u32[]{:S(2)}, u32[]{:S(2)}) collective-permute-start(bf16[2,504,256]{2,1,0:T(8,128)(2,1)S(1)} %get-tuple-element.267), channel_id=1, source_target_pairs={{0,24},{8,0},{16,8},{24,16},{1,25},{9,1},{17,9},{25,17},{2,26},{10... | collective-permute-start | bytes 1548296 | tf_op jit(solution)/shard_map/gather_table/ppermute | solution.py:40
  30.8 23.9 %collective-permute-start.3 = (bf16[1,496,256]{2,1,0:T(8,128)(2,1)S(1)}, bf16[1,496,256]{2,1,0:T(8,128)(2,1)S(1)}, u32[]{:S(2)}, u32[]{:S(2)}) collective-permute-start(bf16[1,496,256]{2,1,0:T(8,128)(2,1)S(1)} %collective-permute-done.2), channel_id=1, source_target_pairs={{0,24},{8,0},{16,8},{24,16},{1,25},{9,1},{17,9},{25,17},{2,26},{10... | collective-permute-start | bytes 761864 | tf_op jit(solution)/shard_map/gather_table/ppermute | solution.py:40
  38.3 23.9 %collective-permute-start.7 = (bf16[1,64,2688]{2,1,0:T(8,128)(2,1)}, bf16[1,64,2688]{2,1,0:T(8,128)(2,1)}, u32[]{:S(2)}, u32[]{:S(2)}) collective-permute-start(bf16[1,64,2688]{2,1,0:T(8,128)(2,1)} %collective-permute-done.6), channel_id=1, source_target_pairs={{0,24},{8,0},{16,8},{24,16},{1,25},{9,1},{17,9},{25,17},{2,26},{10... | collective-permute-start | bytes 1032200 | tf_op jit(solution)/shard_map/gather_first/ppermute | solution.py:40
  65.9 25.5 %collective-permute-start.4 = (bf16[4,496,256]{2,1,0:T(8,128)(2,1)S(1)}, bf16[4,496,256]{2,1,0:T(8,128)(2,1)S(1)}, u32[]{:S(2)}, u32[]{:S(2)}) collective-permute-start(bf16[4,496,256]{2,1,0:T(8,128)(2,1)S(1)} %pad_maximum_fusion.18), channel_id=1, source_target_pairs={{0,4},{4,0},{1,5},{5,1},{2,6},{6,2},{3,7},{7,3},{8,12},{12,8},{9,1... | collective-permute-start | bytes 3047432 | tf_op jit(solution)/shard_map/gather_table/ppermute | solution.py:35
  81.9 22.2 %collective-permute-start.9 = (bf16[4,32,2688]{2,1,0:T(8,128)(2,1)S(1)}, bf16[4,32,2688]{2,1,0:T(8,128)(2,1)S(1)}, u32[]{:S(2)}, u32[]{:S(2)}) collective-permute-start(bf16[4,32,2688]{2,1,0:T(8,128)(2,1)S(1)} %get-tuple-element.249), channel_id=1, source_target_pairs={{0,4},{4,0},{1,5},{5,1},{2,6},{6,2},{3,7},{7,3},{8,12},{12,8},{9,1... | collective-permute-start | bytes 2064392 | tf_op jit(solution)/shard_map/gather_first/ppermute | solution.py:35
  82.5 23.2 %collective-permute-start.10 = (bf16[4,32,2688]{2,1,0:T(8,128)(2,1)S(1)}, bf16[4,32,2688]{2,1,0:T(8,128)(2,1)S(1)}, u32[]{:S(2)}, u32[]{:S(2)}) collective-permute-start(bf16[4,32,2688]{2,1,0:T(8,128)(2,1)S(1)} %get-tuple-element.248), channel_id=1, source_target_pairs={{0,1},{1,0},{2,3},{3,2},{4,5},{5,4},{6,7},{7,6},{8,9},{9,8},{10,11... | collective-permute-start | bytes 2064392 | tf_op jit(solution)/shard_map/gather_first/ppermute | solution.py:35
  104.2 30.3 %collective-permute-start.17 = (bf16[8,32,2688]{2,1,0:T(8,128)(2,1)S(1)}, bf16[8,32,2688]{2,1,0:T(8,128)(2,1)}, u32[]{:S(2)}, u32[]{:S(2)}) collective-permute-start(bf16[8,32,2688]{2,1,0:T(8,128)(2,1)S(1)} %pad_maximum_fusion.5.refs_0_), channel_id=1, source_target_pairs={{0,1},{1,0},{2,3},{3,2},{4,5},{5,4},{6,7},{7,6},{8,9},{9,8},{10,11... | collective-permute-start | bytes 4128776 | tf_op jit(solution)/shard_map/gather_first/ppermute | solution.py:35
  105.9 30.0 %collective-permute-start.18 = (bf16[8,32,2688]{2,1,0:T(8,128)(2,1)S(1)}, bf16[8,32,2688]{2,1,0:T(8,128)(2,1)}, u32[]{:S(2)}, u32[]{:S(2)}) collective-permute-start(bf16[8,32,2688]{2,1,0:T(8,128)(2,1)S(1)} %pad_maximum_fusion.6.refs_2_), channel_id=1, source_target_pairs={{0,4},{4,0},{1,5},{5,1},{2,6},{6,2},{3,7},{7,3},{8,12},{12,8},{9,1... | collective-permute-start | bytes 4128776 | tf_op jit(solution)/shard_map/gather_first/ppermute | solution.py:35
  108.0 23.0 %collective-permute-start.19 = (bf16[2,64,2048]{2,1,0:T(8,128)(2,1)}, bf16[2,64,2048]{2,1,0:T(8,128)(2,1)}, u32[]{:S(2)}, u32[]{:S(2)}) collective-permute-start(bf16[2,64,2048]{2,1,0:T(8,128)(2,1)} %pad_maximum_fusion.19), channel_id=1, source_target_pairs={{0,16},{8,24},{16,0},{24,8},{1,17},{9,25},{17,1},{25,9},{2,18},{10... | collective-permute-start | bytes 1572872 | tf_op jit(solution)/shard_map/gather_up/ppermute | solution.py:75
  151.5 26.2 %collective-permute-start.25 = (bf16[2,128,1024]{2,1,0:T(8,128)(2,1)}, bf16[2,128,1024]{2,1,0:T(8,128)(2,1)S(1)}, u32[]{:S(2)}, u32[]{:S(2)}) collective-permute-start(bf16[2,128,1024]{2,1,0:T(8,128)(2,1)} %pad_maximum_fusion.20), channel_id=1, source_target_pairs={{0,16},{8,24},{16,0},{24,8},{1,17},{9,25},{17,1},{25,9},{2,18},{10... | collective-permute-start | bytes 1572872 | tf_op jit(solution)/shard_map/gather_down/ppermute | solution.py:75
  166.3 42.4 %collective-permute-start.26 = (bf16[8,32,2048]{2,1,0:T(8,128)(2,1)S(1)}, bf16[8,32,2048]{2,1,0:T(8,128)(2,1)S(1)}, u32[]{:S(2)}, u32[]{:S(2)}) collective-permute-start(bf16[8,32,2048]{2,1,0:T(8,128)(2,1)S(1)} %pad_maximum_fusion.10.refs_0_), channel_id=1, source_target_pairs={{0,1},{1,0},{2,3},{3,2},{4,5},{5,4},{6,7},{7,6},{8,9},{9,8},{10,11... | collective-permute-start | bytes 3145736 | tf_op jit(solution)/shard_map/gather_up/ppermute | solution.py:35
  167.8 40.8 %collective-permute-start.27 = (bf16[8,32,2048]{2,1,0:T(8,128)(2,1)S(1)}, bf16[8,32,2048]{2,1,0:T(8,128)(2,1)S(1)}, u32[]{:S(2)}, u32[]{:S(2)}) collective-permute-start(bf16[8,32,2048]{2,1,0:T(8,128)(2,1)S(1)} %pad_maximum_fusion.11.refs_2_), channel_id=1, source_target_pairs={{0,4},{4,0},{1,5},{5,1},{2,6},{6,2},{3,7},{7,3},{8,12},{12,8},{9,1... | collective-permute-start | bytes 3145736 | tf_op jit(solution)/shard_map/gather_up/ppermute | solution.py:35
  179.9 28.7 %collective-permute-start.29 = (bf16[4,64,1024]{2,1,0:T(8,128)(2,1)S(1)}, bf16[4,64,1024]{2,1,0:T(8,128)(2,1)S(1)}, u32[]{:S(2)}, u32[]{:S(2)}) collective-permute-start(bf16[4,64,1024]{2,1,0:T(8,128)(2,1)S(1)} %get-tuple-element.254), channel_id=1, source_target_pairs={{0,1},{1,0},{2,3},{3,2},{4,5},{5,4},{6,7},{7,6},{8,9},{9,8},{10,11... | collective-permute-start | bytes 1572872 | tf_op jit(solution)/shard_map/gather_down/ppermute | solution.py:35
  181.4 27.2 %collective-permute-start.28 = (bf16[4,64,1024]{2,1,0:T(8,128)(2,1)S(1)}, bf16[4,64,1024]{2,1,0:T(8,128)(2,1)S(1)}, u32[]{:S(2)}, u32[]{:S(2)}) collective-permute-start(bf16[4,64,1024]{2,1,0:T(8,128)(2,1)S(1)} %get-tuple-element.255), channel_id=1, source_target_pairs={{0,4},{4,0},{1,5},{5,1},{2,6},{6,2},{3,7},{7,3},{8,12},{12,8},{9,1... | collective-permute-start | bytes 1572872 | tf_op jit(solution)/shard_map/gather_down/ppermute | solution.py:35
  214.6 27.0 %collective-permute-start.31 = (bf16[8,64,1024]{2,1,0:T(8,128)(2,1)S(1)}, bf16[8,64,1024]{2,1,0:T(8,128)(2,1)S(1)}, u32[]{:S(2)}, u32[]{:S(2)}) collective-permute-start(bf16[8,64,1024]{2,1,0:T(8,128)(2,1)S(1)} %pad_maximum_fusion.12.refs_0_), channel_id=1, source_target_pairs={{0,1},{1,0},{2,3},{3,2},{4,5},{5,4},{6,7},{7,6},{8,9},{9,8},{10,11... | collective-permute-start | bytes 3145736 | tf_op jit(solution)/shard_map/gather_down/ppermute | solution.py:35
  216.0 25.6 %collective-permute-start.32 = (bf16[8,64,1024]{2,1,0:T(8,128)(2,1)S(1)}, bf16[8,64,1024]{2,1,0:T(8,128)(2,1)S(1)}, u32[]{:S(2)}, u32[]{:S(2)}) collective-permute-start(bf16[8,64,1024]{2,1,0:T(8,128)(2,1)S(1)} %pad_maximum_fusion.13.refs_2_), channel_id=1, source_target_pairs={{0,4},{4,0},{1,5},{5,1},{2,6},{6,2},{3,7},{7,3},{8,12},{12,8},{9,1... | collective-permute-start | bytes 3145736 | tf_op jit(solution)/shard_map/gather_down/ppermute | solution.py:35
  350.1 25.4 %collective-permute-start.45 = (bf16[4,2,64,1024]{3,2,0,1:T(8,128)(2,1)S(1)}, bf16[4,2,64,1024]{3,2,0,1:T(8,128)(2,1)}, u32[]{:S(2)}, u32[]{:S(2)}) collective-permute-start(bf16[4,2,64,1024]{3,2,0,1:T(8,128)(2,1)S(1)} %bitcast.444), channel_id=1, source_target_pairs={{0,4},{4,0},{1,5},{5,1},{2,6},{6,2},{3,7},{7,3},{8,12},{12,8},{9,1... | collective-permute-start | bytes 3145736 | tf_op jit(solution)/shard_map/reduce_down/ppermute | solution.py:35
  351.7 26.2 %collective-permute-start.44 = (bf16[4,2,64,1024]{3,2,0,1:T(8,128)(2,1)S(1)}, bf16[4,2,64,1024]{3,2,0,1:T(8,128)(2,1)}, u32[]{:S(2)}, u32[]{:S(2)}) collective-permute-start(bf16[4,2,64,1024]{3,2,0,1:T(8,128)(2,1)S(1)} %bitcast.445), channel_id=1, source_target_pairs={{0,1},{1,0},{2,3},{3,2},{4,5},{5,4},{6,7},{7,6},{8,9},{9,8},{10,11... | collective-permute-start | bytes 3145736 | tf_op jit(solution)/shard_map/reduce_down/ppermute | solution.py:35
  370.9 60.1 %collective-permute-start.48 = (bf16[4,2,32,2048]{3,2,0,1:T(8,128)(2,1)}, bf16[4,2,32,2048]{3,2,0,1:T(8,128)(2,1)}, u32[]{:S(2)}, u32[]{:S(2)}) collective-permute-start(bf16[4,2,32,2048]{3,2,0,1:T(8,128)(2,1)} %bitcast.389), channel_id=1, source_target_pairs={{0,1},{1,0},{2,3},{3,2},{4,5},{5,4},{6,7},{7,6},{8,9},{9,8},{10,11... | collective-permute-start | bytes 3145736 | tf_op jit(solution)/shard_map/reduce_up/ppermute | solution.py:35
  392.3 30.7 %collective-permute-start.46 = (bf16[1024,1024]{0,1:T(8,128)(2,1)S(1)}, bf16[1024,1024]{0,1:T(8,128)(2,1)S(1)}, u32[]{:S(2)}, u32[]{:S(2)}) collective-permute-start(bf16[1024,1024]{0,1:T(8,128)(2,1)S(1)} %convert_element_type.616), channel_id=1, source_target_pairs={{0,2},{2,0},{1,3},{3,1},{4,6},{6,4},{5,7},{7,5},{8,10},{10,8},{9,1... | collective-permute-start | bytes 6291464 | tf_op jit(solution)/shard_map/ppermute | solution.py:35
  394.7 36.3 %collective-permute-start.47 = (bf16[4,2,32,2048]{3,2,0,1:T(8,128)(2,1)}, bf16[4,2,32,2048]{3,2,0,1:T(8,128)(2,1)}, u32[]{:S(2)}, u32[]{:S(2)}) collective-permute-start(bf16[4,2,32,2048]{3,2,0,1:T(8,128)(2,1)} %bitcast.390), channel_id=1, source_target_pairs={{0,4},{4,0},{1,5},{5,1},{2,6},{6,2},{3,7},{7,3},{8,12},{12,8},{9,1... | collective-permute-start | bytes 3145736 | tf_op jit(solution)/shard_map/reduce_up/ppermute | solution.py:35
  400.1 67.3 %collective-permute-start.52 = (bf16[4,64,1024]{2,1,0:T(8,128)(2,1)}, bf16[4,64,1024]{2,1,0:T(8,128)(2,1)}, u32[]{:S(2)}, u32[]{:S(2)}) collective-permute-start(bf16[4,64,1024]{2,1,0:T(8,128)(2,1)} %dynamic-slice_bitcast_fusion.1), channel_id=1, source_target_pairs={{0,1},{1,0},{2,3},{3,2},{4,5},{5,4},{6,7},{7,6},{8,9},{9,8},{10,11... | collective-permute-start | bytes 1572872 | tf_op jit(solution)/shard_map/reduce_down/ppermute | solution.py:35
  403.0 64.4 %collective-permute-start.51 = (bf16[4,64,1024]{2,1,0:T(8,128)(2,1)}, bf16[4,64,1024]{2,1,0:T(8,128)(2,1)}, u32[]{:S(2)}, u32[]{:S(2)}) collective-permute-start(bf16[4,64,1024]{2,1,0:T(8,128)(2,1)} %dynamic-slice_bitcast_fusion.2), channel_id=1, source_target_pairs={{0,4},{4,0},{1,5},{5,1},{2,6},{6,2},{3,7},{7,3},{8,12},{12,8},{9,1... | collective-permute-start | bytes 1572872 | tf_op jit(solution)/shard_map/reduce_down/ppermute | solution.py:35
  440.7 26.7 %collective-permute-start.50 = (bf16[4,32,2048]{2,1,0:T(8,128)(2,1)}, bf16[4,32,2048]{2,1,0:T(8,128)(2,1)}, u32[]{:S(2)}, u32[]{:S(2)}) collective-permute-start(bf16[4,32,2048]{2,1,0:T(8,128)(2,1)} %dynamic-slice_bitcast_fusion.3), channel_id=1, source_target_pairs={{0,4},{4,0},{1,5},{5,1},{2,6},{6,2},{3,7},{7,3},{8,12},{12,8},{9,1... | collective-permute-start | bytes 1572872 | tf_op jit(solution)/shard_map/reduce_up/ppermute | solution.py:35
  441.6 25.9 %collective-permute-start.49 = (bf16[4,32,2048]{2,1,0:T(8,128)(2,1)}, bf16[4,32,2048]{2,1,0:T(8,128)(2,1)}, u32[]{:S(2)}, u32[]{:S(2)}) collective-permute-start(bf16[4,32,2048]{2,1,0:T(8,128)(2,1)} %dynamic-slice_bitcast_fusion.4), channel_id=1, source_target_pairs={{0,1},{1,0},{2,3},{3,2},{4,5},{5,4},{6,7},{7,6},{8,9},{9,8},{10,11... | collective-permute-start | bytes 1572872 | tf_op jit(solution)/shard_map/reduce_up/ppermute | solution.py:35
  443.2 24.2 %collective-permute-start.53 = (bf16[4,2,32,1024]{3,2,0,1:T(8,128)(2,1)}, bf16[4,2,32,1024]{3,2,0,1:T(8,128)(2,1)}, u32[]{:S(2)}, u32[]{:S(2)}) collective-permute-start(bf16[4,2,32,1024]{3,2,0,1:T(8,128)(2,1)} %bitcast.395), channel_id=1, source_target_pairs={{0,4},{4,0},{1,5},{5,1},{2,6},{6,2},{3,7},{7,3},{8,12},{12,8},{9,1... | collective-permute-start | bytes 1572872 | tf_op jit(solution)/shard_map/reduce_attn/ppermute | solution.py:35
  484.1 24.4 %collective-permute-start.63 = (bf16[4,32,1024]{2,1,0:T(8,128)(2,1)}, bf16[4,32,1024]{2,1,0:T(8,128)(2,1)}, u32[]{:S(2)}, u32[]{:S(2)}) collective-permute-start(bf16[4,32,1024]{2,1,0:T(8,128)(2,1)} %dynamic-slice_bitcast_fusion.11), channel_id=1, source_target_pairs={{0,1},{1,0},{2,3},{3,2},{4,5},{5,4},{6,7},{7,6},{8,9},{9,8},{10,11... | collective-permute-start | bytes 786440 | tf_op jit(solution)/shard_map/reduce_attn/ppermute | solution.py:35
  487.2 31.3 %collective-permute-start.57 = (bf16[4,2,32,1536]{3,2,0,1:T(8,128)(2,1)}, bf16[4,2,32,1536]{3,2,0,1:T(8,128)(2,1)}, u32[]{:S(2)}, u32[]{:S(2)}) collective-permute-start(bf16[4,2,32,1536]{3,2,0,1:T(8,128)(2,1)} %bitcast.394), channel_id=1, source_target_pairs={{0,4},{4,0},{1,5},{5,1},{2,6},{6,2},{3,7},{7,3},{8,12},{12,8},{9,1... | collective-permute-start | bytes 2359304 | tf_op jit(solution)/shard_map/reduce_qkv/ppermute | solution.py:35
  491.3 29.2 %collective-permute-start.59 = (bf16[4,2,32,1536]{3,2,0,1:T(8,128)(2,1)}, bf16[4,2,32,1536]{3,2,0,1:T(8,128)(2,1)}, u32[]{:S(2)}, u32[]{:S(2)}) collective-permute-start(bf16[4,2,32,1536]{3,2,0,1:T(8,128)(2,1)} %bitcast.393), channel_id=1, source_target_pairs={{0,1},{1,0},{2,3},{3,2},{4,5},{5,4},{6,7},{7,6},{8,9},{9,8},{10,11... | collective-permute-start | bytes 2359304 | tf_op jit(solution)/shard_map/reduce_qkv/ppermute | solution.py:35
  526.5 22.8 %collective-permute-start.66 = (bf16[64,4096]{1,0:T(8,128)(2,1)S(1)}, bf16[64,4096]{1,0:T(8,128)(2,1)S(1)}, u32[]{:S(2)}, u32[]{:S(2)}) collective-permute-start(bf16[64,4096]{1,0:T(8,128)(2,1)S(1)} %fusion.34), channel_id=1, source_target_pairs={{0,8},{8,16},{16,24},{24,0},{1,9},{9,17},{17,25},{25,1},{2,10},{10... | collective-permute-start | bytes 1572872 | tf_op jit(solution)/shard_map/reduce_mlp/ppermute | solution.py:45
  551.8 21.0 %collective-permute-start.80 = (f32[32,2048]{1,0:T(8,128)S(1)}, f32[32,2048]{1,0:T(8,128)}, u32[]{:S(2)}, u32[]{:S(2)}) collective-permute-start(f32[32,2048]{1,0:T(8,128)S(1)} %get-tuple-element.263), channel_id=1, source_target_pairs={{0,2},{2,0},{1,3},{3,1},{4,6},{6,4},{5,7},{7,5},{8,10},{10,8},{9,1... | collective-permute-start | bytes 786440 | tf_op jit(solution)/shard_map/ppermute | solution.py:35
  552.0 24.6 %collective-permute-start.73 = (bf16[4,288,256]{2,1,0:T(8,128)(2,1)S(1)}, bf16[4,288,256]{2,1,0:T(8,128)(2,1)S(1)}, u32[]{:S(2)}, u32[]{:S(2)}) collective-permute-start(bf16[4,288,256]{2,1,0:T(8,128)(2,1)S(1)} %slice_bitcast_fusion.1), channel_id=1, source_target_pairs={{0,4},{4,0},{1,5},{5,1},{2,6},{6,2},{3,7},{7,3},{8,12},{12,8},{9,1... | collective-permute-start | bytes 1769480 | tf_op jit(solution)/shard_map/reduce_table/ppermute | solution.py:35
  (166 other events, 1877.7 us)

commit v4 on v3

--- a/solution.py
+++ b/solution.py
@@ -847,7 +847,7 @@
     ).T
 
     zy = (zn, lax.axis_size("y"))
-    table_cut = block_len * 9 // 256 * 16
+    table_cut = block_len // 32 * 16
 
     def rows_of(grad):
         rows = grad.shape[0] // (2 * groups)

time: 646 us -> 652 us (level)
  transfers between devices with their start and end apart: 81 -> 81, of which waited for: 38 -> 37; matrix products, arithmetic and copies ran while one was open for 30% -> 30% of each run, Pallas kernels for 13% -> 13%
where the time goes in v4:
time: 652 us; the launch traced here: 643 us
  waiting for transfers between devices  189 us (29%)
  Pallas kernels  115 us (18%)
  local copies, waits for them, and re-layouts  101 us (15%)
  other arithmetic  93.5 us (14%)
  matrix products  73.9 us (11%)
  starting transfers between devices  64.8 us (10%)
    ppermute x56, waiting for transfers between devices, swap(): return lax.ppermute(value, axis, SWAP)  78.9 us
    ppermute x12, waiting for transfers between devices, ring_up(): return lax.ppermute(value, axis, [(i, (i + 1) % n) for i in range(n)])  59.9 us
    ppermute x56, starting transfers between devices, swap(): return lax.ppermute(value, axis, SWAP)  42 us
    ppermute x9, waiting for transfers between devices, ring_down(): return lax.ppermute(value, axis, [(i, (i - 1) % n) for i in range(n)])  40.7 us
    pallas_call x1, Pallas kernels, score(): pl.pallas_call(score_body, out_shape=(jax.ShapeDtypeStruct((blocks, rows,...  32.4 us
    dot_general x6, matrix products, dot_nn(): lax.dot_general(left, right, (((1,), (0,)), ((), ())), preferred_element_...  28.8 us
    unnamed x258, local copies, waits for them, and re-layouts  27.3 us
    dot_general x7, matrix products, dot_nt(): lax.dot_general(left, right, (((1,), (1,)), ((), ())), preferred_element_...  26.2 us
  transfers between devices with their start and end apart: 81, of which 37 were waited for; matrix products, arithmetic and copies ran while one was open for 30% of the time, Pallas kernels for 13%

profile of v4, /device:TPU:0, one launch (start us, length us, event | category | flops | bytes accessed | tf_op | source)
XLA Modules:
  0.0 643.4 jit_solution(4456175554027644851)
XLA Ops:
  33.0 5.2 collective-permute-done.6
  40.9 13.7 %collective-permute-done.3 = bf16[1,496,256]{2,1,0:T(8,128)(2,1)S(1)} collective-permute-done((bf16[1,496,256]{2,1,0:T(8,128)(2,1)S(1)}, bf16[1,496,256]{2,1,0:T(8,128)(2,1)S(1)}, u32[]{:S(2)}, u32[]{:S(2)}) %collective-permute-start.3) | collective-permute-done | bytes 253984 | tf_op jit(solution)/shard_map/gather_table/ppermute | solution.py:40
  66.4 6.6 %collective-permute-done.13 = bf16[2,504,256]{2,1,0:T(8,128)(2,1)S(1)} collective-permute-done((bf16[2,504,256]{2,1,0:T(8,128)(2,1)}, bf16[2,504,256]{2,1,0:T(8,128)(2,1)S(1)}, u32[]{:S(2)}, u32[]{:S(2)}) %collective-permute-start.13) | collective-permute-done | bytes 516128 | tf_op jit(solution)/shard_map/gather_table/ppermute | solution.py:40
  75.3 5.1 collective-permute-done.8
  84.1 7.3 %collective-permute-done.4 = bf16[4,496,256]{2,1,0:T(8,128)(2,1)S(1)} collective-permute-done((bf16[4,496,256]{2,1,0:T(8,128)(2,1)S(1)}, bf16[4,496,256]{2,1,0:T(8,128)(2,1)S(1)}, u32[]{:S(2)}, u32[]{:S(2)}) %collective-permute-start.4) | collective-permute-done | bytes 1015840 | tf_op jit(solution)/shard_map/gather_table/ppermute | solution.py:35
  92.9 11.1 %collective-permute-done.9 = bf16[4,32,2688]{2,1,0:T(8,128)(2,1)S(1)} collective-permute-done((bf16[4,32,2688]{2,1,0:T(8,128)(2,1)S(1)}, bf16[4,32,2688]{2,1,0:T(8,128)(2,1)S(1)}, u32[]{:S(2)}, u32[]{:S(2)}) %collective-permute-start.9) | collective-permute-done | bytes 688160 | tf_op jit(solution)/shard_map/gather_first/ppermute | solution.py:35
  110.2 11.4 %gather_fusion = bf16[2048,256]{1,0:T(8,128)(2,1)} fusion(bf16[8000,256]{1,0:T(8,128)(2,1)} %bitcast.423, s32[2048]{0:T(1024)S(1)} %broadcast_clamp_fusion), kind=kCustom, calls=%fused_computation | custom fusion | bytes 2105344 | tf_op jit(solution)/shard_map/jit(_take)/gather | solution.py:662
  157.2 6.2 collective-permute-done.24
  182.4 26.1 %attend.1 = (bf16[1024,512]{1,0:T(8,128)(2,1)S(1)}, f32[4,2,1024]{2,1,0:T(2,128)S(1)}) custom-call(s32[4]{0:T(128)S(1)} %get-tuple-element.354.lo_ref, s32[4]{0:T(128)S(1)} %get-tuple-element.353.hi_ref, bf16[1024,512]{1,0:T(8,128)(2,1)S(1)} %fusion.6.q_ref, bf16[1024,512]{1,0:T(8,128)(2,1)S(1)} %get-tuple-element.231.k_ref, ...), custom_call_target="tpu_custom_call" | custom-call | flops 8589934592 | bytes 4194304 | tf_op jit(solution)/shard_map/attend/pallas_call | solution.py:220
  224.6 9.2 %multiply_convert_fusion.1 = (bf16[1024,2048]{1,0:T(8,128)(2,1)S(1)}, f32[1024,2048]{1,0:T(8,128)}) fusion(f32[2048]{0:T(1024)S(1)} %convert.84, bf16[1024,2048]{1,0:T(8,128)(2,1)S(1)} %bitcast.401, f32[1024,1024]{0,1:T(8,128)S(1)} %get-tuple-element.219, f32[1024]{0:T(1024)S(1)} %reshape.1504, f32[1024]{0:T(1024)S(1)} %reshape.1503, ...), kind=kOutput, calls=%fused_computation.8 | convolution fusion | flops 4312793088 | bytes 20996096 | tf_op jit(solution)/shard_map/dot_general | solution.py:23
  233.8 7.8 %collective-permute-done.32.refs_3_ = bf16[8,64,1024]{2,1,0:T(8,128)(2,1)S(1)} collective-permute-done((bf16[8,64,1024]{2,1,0:T(8,128)(2,1)S(1)}, bf16[8,64,1024]{2,1,0:T(8,128)(2,1)S(1)}, u32[]{:S(2)}, u32[]{:S(2)}) %collective-permute-start.32) | collective-permute-done | bytes 1048608 | tf_op jit(solution)/shard_map/gather_down/ppermute | solution.py:35
  242.4 6.9 %fusion.189 = (bf16[1024,1024]{0,1:T(8,128)(2,1)}, f32[1024,1024]{0,1:T(8,128)}) fusion(bf16[1024,2048]{1,0:T(8,128)(2,1)S(1)} %get-tuple-element.337, bf16[2048,1024]{1,0:T(8,128)(2,1)S(1)} %bitcast.403), kind=kOutput, calls=%fused_computation.604 | convolution fusion | flops 4296015872 | bytes 14680064 | tf_op jit(solution)/shard_map/dot_general | solution.py:23
  258.2 5.4 add_convert_fusion.1
  268.1 5.5 collective-permute-done.34
  276.9 32.4 %score.1 = (bf16[8,1000,2048]{2,1,0:T(8,128)(2,1)}, f32[8,1,2048]{2,1,0:T(1,128)S(1)}, f32[256,2048]{1,0:T(8,128)S(1)}, f32[1,2048]{1,0:T(1,128)S(1)}) custom-call(f32[1,2048]{1,0:T(1,128)S(1)} %fusion.5.norm_ref, bf16[2048,256]{1,0:T(8,128)(2,1)S(1)} %bitcast.399, bf16[8,1000,256]{2,1,0:T(8,128)(2,1)} %pad_maximum_fusion.table_ref, ...), custom_call_target="tpu_custom_call" | custom-call | flops 16777216000 | bytes 32768000 | tf_op jit(solution)/shard_map/score/pallas_call | solution.py:402
  329.1 6.6 %collective-permute-done.42 = bf16[256,512]{0,1:T(8,128)(2,1)S(1)} collective-permute-done((bf16[256,512]{0,1:T(8,128)(2,1)S(1)}, bf16[256,512]{0,1:T(8,128)(2,1)S(1)}, u32[]{:S(2)}, u32[]{:S(2)}) %collective-permute-start.42) | collective-permute-done | bytes 262176 | tf_op jit(solution)/shard_map/ppermute | solution.py:35
  343.0 5.0 convolution_convert_fusion.2
  353.7 7.9 %fusion.191 = (bf16[2048]{0:T(1024)(128)(2,1)S(1)}, bf16[1024,2048]{1,0:T(8,128)(2,1)S(1)}) fusion(f32[1024,2048]{1,0:T(8,128)S(1)} %bitcast.517, f32[2048]{0:T(1024)S(1)} %convert.84, bf16[1024,1024]{0,1:T(8,128)(2,1)S(1)} %get-tuple-element.135, bf16[2048,1024]{1,0:T(8,128)(2,1)S(1)} %bitcast.404), kind=kOutput, calls=%fused_computation.606 | convolution fusion | flops 4324325376 | bytes 18886656 | tf_op jit(solution)/shard_map/dot_general | solution.py:27
  361.6 5.2 convolution_convert_fusion.1
  378.0 6.3 fusion.195
  384.3 5.3 copy.162
  403.3 18.8 %table_product.1.sum_ref = f32[8,1000,256]{2,1,0:T(8,128)} custom-call(bf16[8,1000,2048]{2,1,0:T(8,128)(2,1)} %get-tuple-element.133.raised_ref, bf16[2048,256]{1,0:T(8,128)(2,1)S(1)} %bitcast.400, f32[2048,8]{1,0:T(8,128)S(1)} %fusion.41.coef_ref), custom_call_target="tpu_custom_call" | custom-call | flops 8388608000 | bytes 32768000 | tf_op jit(solution)/shard_map/table_product/pallas_call | solution.py:445
  444.1 22.7 %attend_back.1 = (bf16[1024,512]{1,0:T(8,128)(2,1)S(1)}, bf16[1024,512]{1,0:T(8,128)(2,1)S(1)}, bf16[1024,512]{1,0:T(8,128)(2,1)S(1)}) custom-call(s32[4]{0:T(128)S(1)} %copy-done.27, s32[4]{0:T(128)S(1)} %copy-done.25, bf16[1024,512]{1,0:T(8,128)(2,1)S(1)} %copy-done.8, bf16[1024,512]{1,0:T(8,128)(2,1)S(1)} %copy-done.16, bf16[1024,512]{1,0:T(8,128)(2,1)S(1)} %copy-done.14, ...), custom_call_target="tpu_custom_call" | custom-call | flops 17179869184 | bytes 8388608 | tf_op jit(solution)/shard_map/attend_back/pallas_call | solution.py:313
  510.0 5.9 collective-permute-done.55
  528.0 6.4 collective-permute-done.62
  535.4 11.2 %table_add.1 = bf16[8,1000,256]{2,1,0:T(8,128)(2,1)S(1)} custom-call(f32[8,1000,256]{2,1,0:T(8,128)} %table_product.1.sum_ref, s32[1,2048]{1,0:T(1,128)S(1)} %bitcast.420, bf16[2048,256]{1,0:T(8,128)(2,1)S(1)} %pad_maximum_fusion.15.grad_ref), custom_call_target="tpu_custom_call" | custom-call | flops 8388608000 | bytes 12288000 | tf_op jit(solution)/shard_map/table_add/pallas_call | solution.py:476
  554.0 7.8 %collective-permute-done.69 = bf16[64,2432]{1,0:T(8,128)(2,1)S(1)} collective-permute-done((bf16[64,2432]{1,0:T(8,128)(2,1)S(1)}, bf16[64,2432]{1,0:T(8,128)(2,1)S(1)}, u32[]{:S(2)}, u32[]{:S(2)}) %collective-permute-start.69) | collective-permute-done | bytes 311328 | tf_op jit(solution)/shard_map/reduce_rest/ppermute | solution.py:45
  564.0 7.3 %collective-permute-done.68 = bf16[2,504,256]{2,1,0:T(8,128)(2,1)S(1)} collective-permute-done((bf16[2,504,256]{2,1,0:T(8,128)(2,1)S(1)}, bf16[2,504,256]{2,1,0:T(8,128)(2,1)S(1)}, u32[]{:S(2)}, u32[]{:S(2)}) %collective-permute-start.68) | collective-permute-done | bytes 516128 | tf_op jit(solution)/shard_map/reduce_table/ppermute | solution.py:45
  576.7 15.4 %collective-permute-done.72 = bf16[64,2432]{1,0:T(8,128)(2,1)S(1)} collective-permute-done((bf16[64,2432]{1,0:T(8,128)(2,1)}, bf16[64,2432]{1,0:T(8,128)(2,1)S(1)}, u32[]{:S(2)}, u32[]{:S(2)}) %collective-permute-start.72) | collective-permute-done | bytes 311328 | tf_op jit(solution)/shard_map/reduce_rest/ppermute | solution.py:45
  602.2 6.2 collective-permute-done.75
  608.5 10.7 %collective-permute-done.74 = bf16[2,504,256]{2,1,0:T(8,128)(2,1)S(1)} collective-permute-done((bf16[2,504,256]{2,1,0:T(8,128)(2,1)}, bf16[2,504,256]{2,1,0:T(8,128)(2,1)S(1)}, u32[]{:S(2)}, u32[]{:S(2)}) %collective-permute-start.74) | collective-permute-done | bytes 516128 | tf_op jit(solution)/shard_map/reduce_table/ppermute | solution.py:45
  633.8 7.7 %collective-permute-done.78 = bf16[496,256]{1,0:T(8,128)(2,1)S(1)} collective-permute-done((bf16[496,256]{1,0:T(8,128)(2,1)S(1)}, bf16[496,256]{1,0:T(8,128)(2,1)S(1)}, u32[]{:S(2)}, u32[]{:S(2)}) %collective-permute-start.78) | collective-permute-done | bytes 253984 | tf_op jit(solution)/shard_map/reduce_table/ppermute | solution.py:45
  (682 shorter events, 321.4 us)
Async XLA Ops:
  24.0 30.7 %collective-permute-start.12 = (bf16[2,504,256]{2,1,0:T(8,128)(2,1)S(1)}, bf16[2,504,256]{2,1,0:T(8,128)(2,1)}, u32[]{:S(2)}, u32[]{:S(2)}) collective-permute-start(bf16[2,504,256]{2,1,0:T(8,128)(2,1)S(1)} %get-tuple-element.267), channel_id=1, source_target_pairs={{0,24},{8,0},{16,8},{24,16},{1,25},{9,1},{17,9},{25,17},{2,26},{10... | collective-permute-start | bytes 1548296 | tf_op jit(solution)/shard_map/gather_table/ppermute | solution.py:40
  30.8 23.9 %collective-permute-start.3 = (bf16[1,496,256]{2,1,0:T(8,128)(2,1)S(1)}, bf16[1,496,256]{2,1,0:T(8,128)(2,1)S(1)}, u32[]{:S(2)}, u32[]{:S(2)}) collective-permute-start(bf16[1,496,256]{2,1,0:T(8,128)(2,1)S(1)} %collective-permute-done.2), channel_id=1, source_target_pairs={{0,24},{8,0},{16,8},{24,16},{1,25},{9,1},{17,9},{25,17},{2,26},{10... | collective-permute-start | bytes 761864 | tf_op jit(solution)/shard_map/gather_table/ppermute | solution.py:40
  38.2 23.9 %collective-permute-start.7 = (bf16[1,64,2688]{2,1,0:T(8,128)(2,1)}, bf16[1,64,2688]{2,1,0:T(8,128)(2,1)}, u32[]{:S(2)}, u32[]{:S(2)}) collective-permute-start(bf16[1,64,2688]{2,1,0:T(8,128)(2,1)} %collective-permute-done.6), channel_id=1, source_target_pairs={{0,24},{8,0},{16,8},{24,16},{1,25},{9,1},{17,9},{25,17},{2,26},{10... | collective-permute-start | bytes 1032200 | tf_op jit(solution)/shard_map/gather_first/ppermute | solution.py:40
  65.9 25.5 %collective-permute-start.4 = (bf16[4,496,256]{2,1,0:T(8,128)(2,1)S(1)}, bf16[4,496,256]{2,1,0:T(8,128)(2,1)S(1)}, u32[]{:S(2)}, u32[]{:S(2)}) collective-permute-start(bf16[4,496,256]{2,1,0:T(8,128)(2,1)S(1)} %pad_maximum_fusion.17), channel_id=1, source_target_pairs={{0,4},{4,0},{1,5},{5,1},{2,6},{6,2},{3,7},{7,3},{8,12},{12,8},{9,1... | collective-permute-start | bytes 3047432 | tf_op jit(solution)/shard_map/gather_table/ppermute | solution.py:35
  81.8 22.2 %collective-permute-start.9 = (bf16[4,32,2688]{2,1,0:T(8,128)(2,1)S(1)}, bf16[4,32,2688]{2,1,0:T(8,128)(2,1)S(1)}, u32[]{:S(2)}, u32[]{:S(2)}) collective-permute-start(bf16[4,32,2688]{2,1,0:T(8,128)(2,1)S(1)} %get-tuple-element.249), channel_id=1, source_target_pairs={{0,4},{4,0},{1,5},{5,1},{2,6},{6,2},{3,7},{7,3},{8,12},{12,8},{9,1... | collective-permute-start | bytes 2064392 | tf_op jit(solution)/shard_map/gather_first/ppermute | solution.py:35
  82.5 23.2 %collective-permute-start.10 = (bf16[4,32,2688]{2,1,0:T(8,128)(2,1)S(1)}, bf16[4,32,2688]{2,1,0:T(8,128)(2,1)S(1)}, u32[]{:S(2)}, u32[]{:S(2)}) collective-permute-start(bf16[4,32,2688]{2,1,0:T(8,128)(2,1)S(1)} %get-tuple-element.248), channel_id=1, source_target_pairs={{0,1},{1,0},{2,3},{3,2},{4,5},{5,4},{6,7},{7,6},{8,9},{9,8},{10,11... | collective-permute-start | bytes 2064392 | tf_op jit(solution)/shard_map/gather_first/ppermute | solution.py:35
  104.2 30.3 %collective-permute-start.17 = (bf16[8,32,2688]{2,1,0:T(8,128)(2,1)S(1)}, bf16[8,32,2688]{2,1,0:T(8,128)(2,1)}, u32[]{:S(2)}, u32[]{:S(2)}) collective-permute-start(bf16[8,32,2688]{2,1,0:T(8,128)(2,1)S(1)} %pad_maximum_fusion.5.refs_0_), channel_id=1, source_target_pairs={{0,1},{1,0},{2,3},{3,2},{4,5},{5,4},{6,7},{7,6},{8,9},{9,8},{10,11... | collective-permute-start | bytes 4128776 | tf_op jit(solution)/shard_map/gather_first/ppermute | solution.py:35
  105.9 30.0 %collective-permute-start.18 = (bf16[8,32,2688]{2,1,0:T(8,128)(2,1)S(1)}, bf16[8,32,2688]{2,1,0:T(8,128)(2,1)}, u32[]{:S(2)}, u32[]{:S(2)}) collective-permute-start(bf16[8,32,2688]{2,1,0:T(8,128)(2,1)S(1)} %pad_maximum_fusion.6.refs_2_), channel_id=1, source_target_pairs={{0,4},{4,0},{1,5},{5,1},{2,6},{6,2},{3,7},{7,3},{8,12},{12,8},{9,1... | collective-permute-start | bytes 4128776 | tf_op jit(solution)/shard_map/gather_first/ppermute | solution.py:35
  108.0 23.0 %collective-permute-start.19 = (bf16[2,64,2048]{2,1,0:T(8,128)(2,1)}, bf16[2,64,2048]{2,1,0:T(8,128)(2,1)}, u32[]{:S(2)}, u32[]{:S(2)}) collective-permute-start(bf16[2,64,2048]{2,1,0:T(8,128)(2,1)} %pad_maximum_fusion.19), channel_id=1, source_target_pairs={{0,16},{8,24},{16,0},{24,8},{1,17},{9,25},{17,1},{25,9},{2,18},{10... | collective-permute-start | bytes 1572872 | tf_op jit(solution)/shard_map/gather_up/ppermute | solution.py:75
  151.5 26.2 %collective-permute-start.25 = (bf16[2,128,1024]{2,1,0:T(8,128)(2,1)}, bf16[2,128,1024]{2,1,0:T(8,128)(2,1)S(1)}, u32[]{:S(2)}, u32[]{:S(2)}) collective-permute-start(bf16[2,128,1024]{2,1,0:T(8,128)(2,1)} %pad_maximum_fusion.20), channel_id=1, source_target_pairs={{0,16},{8,24},{16,0},{24,8},{1,17},{9,25},{17,1},{25,9},{2,18},{10... | collective-permute-start | bytes 1572872 | tf_op jit(solution)/shard_map/gather_down/ppermute | solution.py:75
  166.3 42.4 %collective-permute-start.26 = (bf16[8,32,2048]{2,1,0:T(8,128)(2,1)S(1)}, bf16[8,32,2048]{2,1,0:T(8,128)(2,1)S(1)}, u32[]{:S(2)}, u32[]{:S(2)}) collective-permute-start(bf16[8,32,2048]{2,1,0:T(8,128)(2,1)S(1)} %pad_maximum_fusion.9.refs_0_), channel_id=1, source_target_pairs={{0,1},{1,0},{2,3},{3,2},{4,5},{5,4},{6,7},{7,6},{8,9},{9,8},{10,11... | collective-permute-start | bytes 3145736 | tf_op jit(solution)/shard_map/gather_up/ppermute | solution.py:35
  167.8 40.8 %collective-permute-start.27 = (bf16[8,32,2048]{2,1,0:T(8,128)(2,1)S(1)}, bf16[8,32,2048]{2,1,0:T(8,128)(2,1)S(1)}, u32[]{:S(2)}, u32[]{:S(2)}) collective-permute-start(bf16[8,32,2048]{2,1,0:T(8,128)(2,1)S(1)} %pad_maximum_fusion.10.refs_2_), channel_id=1, source_target_pairs={{0,4},{4,0},{1,5},{5,1},{2,6},{6,2},{3,7},{7,3},{8,12},{12,8},{9,1... | collective-permute-start | bytes 3145736 | tf_op jit(solution)/shard_map/gather_up/ppermute | solution.py:35
  179.8 28.7 %collective-permute-start.29 = (bf16[4,64,1024]{2,1,0:T(8,128)(2,1)S(1)}, bf16[4,64,1024]{2,1,0:T(8,128)(2,1)S(1)}, u32[]{:S(2)}, u32[]{:S(2)}) collective-permute-start(bf16[4,64,1024]{2,1,0:T(8,128)(2,1)S(1)} %get-tuple-element.254), channel_id=1, source_target_pairs={{0,1},{1,0},{2,3},{3,2},{4,5},{5,4},{6,7},{7,6},{8,9},{9,8},{10,11... | collective-permute-start | bytes 1572872 | tf_op jit(solution)/shard_map/gather_down/ppermute | solution.py:35
  181.4 27.2 %collective-permute-start.28 = (bf16[4,64,1024]{2,1,0:T(8,128)(2,1)S(1)}, bf16[4,64,1024]{2,1,0:T(8,128)(2,1)S(1)}, u32[]{:S(2)}, u32[]{:S(2)}) collective-permute-start(bf16[4,64,1024]{2,1,0:T(8,128)(2,1)S(1)} %get-tuple-element.255), channel_id=1, source_target_pairs={{0,4},{4,0},{1,5},{5,1},{2,6},{6,2},{3,7},{7,3},{8,12},{12,8},{9,1... | collective-permute-start | bytes 1572872 | tf_op jit(solution)/shard_map/gather_down/ppermute | solution.py:35
  214.5 27.0 %collective-permute-start.31 = (bf16[8,64,1024]{2,1,0:T(8,128)(2,1)S(1)}, bf16[8,64,1024]{2,1,0:T(8,128)(2,1)S(1)}, u32[]{:S(2)}, u32[]{:S(2)}) collective-permute-start(bf16[8,64,1024]{2,1,0:T(8,128)(2,1)S(1)} %pad_maximum_fusion.11.refs_0_), channel_id=1, source_target_pairs={{0,1},{1,0},{2,3},{3,2},{4,5},{5,4},{6,7},{7,6},{8,9},{9,8},{10,11... | collective-permute-start | bytes 3145736 | tf_op jit(solution)/shard_map/gather_down/ppermute | solution.py:35
  215.9 25.6 %collective-permute-start.32 = (bf16[8,64,1024]{2,1,0:T(8,128)(2,1)S(1)}, bf16[8,64,1024]{2,1,0:T(8,128)(2,1)S(1)}, u32[]{:S(2)}, u32[]{:S(2)}) collective-permute-start(bf16[8,64,1024]{2,1,0:T(8,128)(2,1)S(1)} %pad_maximum_fusion.12.refs_2_), channel_id=1, source_target_pairs={{0,4},{4,0},{1,5},{5,1},{2,6},{6,2},{3,7},{7,3},{8,12},{12,8},{9,1... | collective-permute-start | bytes 3145736 | tf_op jit(solution)/shard_map/gather_down/ppermute | solution.py:35
  350.1 25.4 %collective-permute-start.45 = (bf16[4,2,64,1024]{3,2,0,1:T(8,128)(2,1)S(1)}, bf16[4,2,64,1024]{3,2,0,1:T(8,128)(2,1)}, u32[]{:S(2)}, u32[]{:S(2)}) collective-permute-start(bf16[4,2,64,1024]{3,2,0,1:T(8,128)(2,1)S(1)} %bitcast.444), channel_id=1, source_target_pairs={{0,4},{4,0},{1,5},{5,1},{2,6},{6,2},{3,7},{7,3},{8,12},{12,8},{9,1... | collective-permute-start | bytes 3145736 | tf_op jit(solution)/shard_map/reduce_down/ppermute | solution.py:35
  351.7 26.2 %collective-permute-start.44 = (bf16[4,2,64,1024]{3,2,0,1:T(8,128)(2,1)S(1)}, bf16[4,2,64,1024]{3,2,0,1:T(8,128)(2,1)}, u32[]{:S(2)}, u32[]{:S(2)}) collective-permute-start(bf16[4,2,64,1024]{3,2,0,1:T(8,128)(2,1)S(1)} %bitcast.445), channel_id=1, source_target_pairs={{0,1},{1,0},{2,3},{3,2},{4,5},{5,4},{6,7},{7,6},{8,9},{9,8},{10,11... | collective-permute-start | bytes 3145736 | tf_op jit(solution)/shard_map/reduce_down/ppermute | solution.py:35
  370.9 59.1 %collective-permute-start.48 = (bf16[4,2,32,2048]{3,2,0,1:T(8,128)(2,1)}, bf16[4,2,32,2048]{3,2,0,1:T(8,128)(2,1)}, u32[]{:S(2)}, u32[]{:S(2)}) collective-permute-start(bf16[4,2,32,2048]{3,2,0,1:T(8,128)(2,1)} %bitcast.389), channel_id=1, source_target_pairs={{0,1},{1,0},{2,3},{3,2},{4,5},{5,4},{6,7},{7,6},{8,9},{9,8},{10,11... | collective-permute-start | bytes 3145736 | tf_op jit(solution)/shard_map/reduce_up/ppermute | solution.py:35
  392.3 29.7 %collective-permute-start.46 = (bf16[1024,1024]{0,1:T(8,128)(2,1)S(1)}, bf16[1024,1024]{0,1:T(8,128)(2,1)S(1)}, u32[]{:S(2)}, u32[]{:S(2)}) collective-permute-start(bf16[1024,1024]{0,1:T(8,128)(2,1)S(1)} %convert_element_type.616), channel_id=1, source_target_pairs={{0,2},{2,0},{1,3},{3,1},{4,6},{6,4},{5,7},{7,5},{8,10},{10,8},{9,1... | collective-permute-start | bytes 6291464 | tf_op jit(solution)/shard_map/ppermute | solution.py:35
  394.7 35.3 %collective-permute-start.47 = (bf16[4,2,32,2048]{3,2,0,1:T(8,128)(2,1)}, bf16[4,2,32,2048]{3,2,0,1:T(8,128)(2,1)}, u32[]{:S(2)}, u32[]{:S(2)}) collective-permute-start(bf16[4,2,32,2048]{3,2,0,1:T(8,128)(2,1)} %bitcast.390), channel_id=1, source_target_pairs={{0,4},{4,0},{1,5},{5,1},{2,6},{6,2},{3,7},{7,3},{8,12},{12,8},{9,1... | collective-permute-start | bytes 3145736 | tf_op jit(solution)/shard_map/reduce_up/ppermute | solution.py:35
  400.1 67.9 %collective-permute-start.52 = (bf16[4,64,1024]{2,1,0:T(8,128)(2,1)}, bf16[4,64,1024]{2,1,0:T(8,128)(2,1)}, u32[]{:S(2)}, u32[]{:S(2)}) collective-permute-start(bf16[4,64,1024]{2,1,0:T(8,128)(2,1)} %dynamic-slice_bitcast_fusion.1), channel_id=1, source_target_pairs={{0,1},{1,0},{2,3},{3,2},{4,5},{5,4},{6,7},{7,6},{8,9},{9,8},{10,11... | collective-permute-start | bytes 1572872 | tf_op jit(solution)/shard_map/reduce_down/ppermute | solution.py:35
  403.0 65.0 %collective-permute-start.51 = (bf16[4,64,1024]{2,1,0:T(8,128)(2,1)}, bf16[4,64,1024]{2,1,0:T(8,128)(2,1)}, u32[]{:S(2)}, u32[]{:S(2)}) collective-permute-start(bf16[4,64,1024]{2,1,0:T(8,128)(2,1)} %dynamic-slice_bitcast_fusion.2), channel_id=1, source_target_pairs={{0,4},{4,0},{1,5},{5,1},{2,6},{6,2},{3,7},{7,3},{8,12},{12,8},{9,1... | collective-permute-start | bytes 1572872 | tf_op jit(solution)/shard_map/reduce_down/ppermute | solution.py:35
  440.3 27.6 %collective-permute-start.50 = (bf16[4,32,2048]{2,1,0:T(8,128)(2,1)}, bf16[4,32,2048]{2,1,0:T(8,128)(2,1)}, u32[]{:S(2)}, u32[]{:S(2)}) collective-permute-start(bf16[4,32,2048]{2,1,0:T(8,128)(2,1)} %dynamic-slice_bitcast_fusion.3), channel_id=1, source_target_pairs={{0,4},{4,0},{1,5},{5,1},{2,6},{6,2},{3,7},{7,3},{8,12},{12,8},{9,1... | collective-permute-start | bytes 1572872 | tf_op jit(solution)/shard_map/reduce_up/ppermute | solution.py:35
  442.1 25.9 %collective-permute-start.49 = (bf16[4,32,2048]{2,1,0:T(8,128)(2,1)}, bf16[4,32,2048]{2,1,0:T(8,128)(2,1)}, u32[]{:S(2)}, u32[]{:S(2)}) collective-permute-start(bf16[4,32,2048]{2,1,0:T(8,128)(2,1)} %dynamic-slice_bitcast_fusion.4), channel_id=1, source_target_pairs={{0,1},{1,0},{2,3},{3,2},{4,5},{5,4},{6,7},{7,6},{8,9},{9,8},{10,11... | collective-permute-start | bytes 1572872 | tf_op jit(solution)/shard_map/reduce_up/ppermute | solution.py:35
  443.8 24.2 %collective-permute-start.53 = (bf16[4,2,32,1024]{3,2,0,1:T(8,128)(2,1)}, bf16[4,2,32,1024]{3,2,0,1:T(8,128)(2,1)}, u32[]{:S(2)}, u32[]{:S(2)}) collective-permute-start(bf16[4,2,32,1024]{3,2,0,1:T(8,128)(2,1)} %bitcast.395), channel_id=1, source_target_pairs={{0,4},{4,0},{1,5},{5,1},{2,6},{6,2},{3,7},{7,3},{8,12},{12,8},{9,1... | collective-permute-start | bytes 1572872 | tf_op jit(solution)/shard_map/reduce_attn/ppermute | solution.py:35
  484.5 24.4 %collective-permute-start.63 = (bf16[4,32,1024]{2,1,0:T(8,128)(2,1)}, bf16[4,32,1024]{2,1,0:T(8,128)(2,1)}, u32[]{:S(2)}, u32[]{:S(2)}) collective-permute-start(bf16[4,32,1024]{2,1,0:T(8,128)(2,1)} %dynamic-slice_bitcast_fusion.11), channel_id=1, source_target_pairs={{0,1},{1,0},{2,3},{3,2},{4,5},{5,4},{6,7},{7,6},{8,9},{9,8},{10,11... | collective-permute-start | bytes 786440 | tf_op jit(solution)/shard_map/reduce_attn/ppermute | solution.py:35
  487.7 30.2 %collective-permute-start.57 = (bf16[4,2,32,1536]{3,2,0,1:T(8,128)(2,1)}, bf16[4,2,32,1536]{3,2,0,1:T(8,128)(2,1)}, u32[]{:S(2)}, u32[]{:S(2)}) collective-permute-start(bf16[4,2,32,1536]{3,2,0,1:T(8,128)(2,1)} %bitcast.394), channel_id=1, source_target_pairs={{0,4},{4,0},{1,5},{5,1},{2,6},{6,2},{3,7},{7,3},{8,12},{12,8},{9,1... | collective-permute-start | bytes 2359304 | tf_op jit(solution)/shard_map/reduce_qkv/ppermute | solution.py:35
  490.2 30.6 %collective-permute-start.59 = (bf16[4,2,32,1536]{3,2,0,1:T(8,128)(2,1)}, bf16[4,2,32,1536]{3,2,0,1:T(8,128)(2,1)}, u32[]{:S(2)}, u32[]{:S(2)}) collective-permute-start(bf16[4,2,32,1536]{3,2,0,1:T(8,128)(2,1)} %bitcast.393), channel_id=1, source_target_pairs={{0,1},{1,0},{2,3},{3,2},{4,5},{5,4},{6,7},{7,6},{8,9},{9,8},{10,11... | collective-permute-start | bytes 2359304 | tf_op jit(solution)/shard_map/reduce_qkv/ppermute | solution.py:35
  526.7 22.8 %collective-permute-start.66 = (bf16[64,4096]{1,0:T(8,128)(2,1)S(1)}, bf16[64,4096]{1,0:T(8,128)(2,1)S(1)}, u32[]{:S(2)}, u32[]{:S(2)}) collective-permute-start(bf16[64,4096]{1,0:T(8,128)(2,1)S(1)} %fusion.34), channel_id=1, source_target_pairs={{0,8},{8,16},{16,24},{24,0},{1,9},{9,17},{17,25},{25,1},{2,10},{10... | collective-permute-start | bytes 1572872 | tf_op jit(solution)/shard_map/reduce_mlp/ppermute | solution.py:45
  552.9 23.8 %collective-permute-start.73 = (bf16[4,256,256]{2,1,0:T(8,128)(2,1)S(1)}, bf16[4,256,256]{2,1,0:T(8,128)(2,1)S(1)}, u32[]{:S(2)}, u32[]{:S(2)}) collective-permute-start(bf16[4,256,256]{2,1,0:T(8,128)(2,1)S(1)} %slice_bitcast_fusion.1), channel_id=1, source_target_pairs={{0,4},{4,0},{1,5},{5,1},{2,6},{6,2},{3,7},{7,3},{8,12},{12,8},{9,1... | collective-permute-start | bytes 1572872 | tf_op jit(solution)/shard_map/reduce_table/ppermute | solution.py:35
  597.7 25.5 %collective-permute-start.79 = (f32[32,1536]{1,0:T(8,128)}, f32[32,1536]{1,0:T(8,128)}, u32[]{:S(2)}, u32[]{:S(2)}) collective-permute-start(f32[32,1536]{1,0:T(8,128)} %get-tuple-element.269), channel_id=1, source_target_pairs={{0,2},{2,0},{1,3},{3,1},{4,6},{6,4},{5,7},{7,5},{8,10},{10,8},{9,1... | collective-permute-start | bytes 589832 | tf_op jit(solution)/shard_map/ppermute | solution.py:35
  (166 other events, 2014.7 us)
